TPU v7x, 128 devices: a whole 4x4x4 slice. The times are simulated.
128 devices in a mesh: face: 4 (over z), tile: 32 (over x, y, core).
Axes of the slice: x: 4, y: 4, z: 4, core: 2. Of those that a mesh axis runs over, the one named last changes fastest.
Arguments:
- fields: bfloat16 [3072, 384, 128], P('tile', 'face'), may hold values from -6 to 6
- first_kernel_taps: bfloat16 [9, 128, 128], replicated, may hold values from -0.1875 to 0.1875
- first_conv_bias: float32 [128], replicated, may hold values from -0.5 to 0.5
- second_kernel_taps: bfloat16 [9, 128, 128], replicated, may hold values from -0.1875 to 0.1875
- second_conv_bias: float32 [128], replicated, may hold values from -0.5 to 0.5
- obs_weight: bfloat16 [128, 128], replicated, may hold values from -0.5 to 0.5
- obs_values: bfloat16 [131072, 128], P(('face', 'tile')), may hold values from -6 to 6
- obs_owner: int32 [131072, 1], P(('face', 'tile')), may hold values from 0 to 127; in each aligned block of 1024 rows (0 to 1023, 1024 to 2047, ...) at most 16 rows name the same one
- obs_cells: int32 [131072], P(('face', 'tile')), may hold values from 0 to 9215
- polar_neighbor_sector: int32 [4, 2], replicated, may hold values from 0 to 3, as said below
- polar_link_reversal: int32 [4, 2], replicated, may hold values from 0 to 1
Outputs:
- level_out: bfloat16 [3072, 384, 128], P('tile', 'face')
Inputs may be any that keep to these rules, and one draw needn't show every extreme that they name: `obs_owner`: among the rows of one device at most 16 name the same tile, and in every draw some device sends exactly 16 rows to one tile. `polar_neighbor_sector`: each column links the sectors in one cycle through all 4 of them; no sector names itself.
All inputs are finite; a program needn't handle non-finite values.
Results may differ from a plain program's by a relative error of at most 0.0034.
Values may be sent and summed in bfloat16 or wider, within the bound.
No kernel may reach another device: no remote copies, remote signals or barrier semaphores. Data moves between devices by JAX's collectives and lax.ppermute only.
A program may use at most 64 MiB of HBM per device.

v0:
```python
import functools

import jax
import jax.numpy as jnp
from jax import lax
from jax.experimental import pallas as pl
from jax.experimental.pallas import tpu as pltpu
from jax.sharding import PartitionSpec as P

FIRST_DILATION = 2
SECOND_DILATION = 4
CAP = 16
META = 8

BF16 = jnp.bfloat16
F32 = jnp.float32
I32 = jnp.int32
VMEM = pltpu.VMEM


def full_spec(memory_space=None):
    return pl.BlockSpec(memory_space=VMEM if memory_space is None else memory_space)


def iota(shape, axis):
    return lax.broadcasted_iota(I32, shape, axis)


def pack_kernel(dests, side, owner_ref, cell_ref, vals_ref, send_ref):
    rows = vals_ref.shape[0]
    owner = owner_ref[...]
    cell = cell_ref[...]
    block = 256
    earlier = (iota((block, block), 0) < iota((block, block), 1)).astype(F32).astype(BF16)
    onehot_parts = []
    rank_parts = []
    carry = jnp.zeros((dests, 1), F32)
    for b in range(rows // block):
        hit = owner[:, b * block : (b + 1) * block] == iota((dests, block), 0)
        hit_f = jnp.where(hit, 1.0, 0.0)
        hit_b = hit_f.astype(BF16)
        before = jnp.dot(hit_b, earlier, preferred_element_type=F32) + carry
        rank_parts.append(jnp.sum(before * hit_f, axis=0, keepdims=True))
        carry = carry + jnp.sum(hit_f, axis=1, keepdims=True)
        onehot_parts.append(hit_b)
    rank = jnp.concatenate(rank_parts, axis=1).astype(I32)
    onehot = jnp.concatenate(onehot_parts, axis=1)
    target = owner * CAP + rank

    cell_row = ((cell.astype(F32) + 0.5) * (1.0 / side)).astype(I32)
    cell_col = cell - cell_row * side
    me = lax.axis_index("face") * lax.axis_size("tile") + lax.axis_index("tile")
    base_lane = lax.rem(me, 8) * CAP
    slot_hit = iota((128, rows), 0) == rank + base_lane
    row_map = jnp.where(slot_hit, cell_row.astype(F32), 0.0).astype(BF16)
    col_map = jnp.where(slot_hit, cell_col.astype(F32), 0.0).astype(BF16)
    contract = (((1,), (1,)), ((), ()))
    meta_row = lax.dot_general(onehot, row_map, contract, preferred_element_type=F32)
    meta_col = lax.dot_general(onehot, col_map, contract, preferred_element_type=F32)
    meta = jnp.where(
        iota((dests, META, 128), 1) == 0,
        jnp.broadcast_to(meta_row[:, None, :], (dests, META, 128)),
        jnp.broadcast_to(meta_col[:, None, :], (dests, META, 128)),
    )
    send_ref[:, CAP:, :] = meta.astype(BF16)

    chunk_dests = 16
    chunk = chunk_dests * CAP
    for c in range(dests // chunk_dests):
        match = target == iota((chunk, rows), 0) + c * chunk
        match = jnp.where(match, 1.0, 0.0).astype(BF16)
        placed = jnp.dot(match, vals_ref[...], preferred_element_type=F32).astype(BF16)
        send_ref[c * chunk_dests : (c + 1) * chunk_dests, :CAP, :] = placed.reshape(
            chunk_dests, CAP, placed.shape[-1]
        )


def pack(owner, cells, vals, dests, side):
    rows, features = vals.shape
    return pl.pallas_call(
        functools.partial(pack_kernel, dests, side),
        out_shape=jax.ShapeDtypeStruct((dests, CAP + META, features), BF16),
        in_specs=[full_spec()] * 3,
        out_specs=full_spec(),
        cost_estimate=pl.CostEstimate(
            flops=2 * dests * CAP * rows * features, bytes_accessed=2_000_000, transcendentals=0
        ),
        name="pack",
    )(owner.reshape(1, rows), cells.reshape(1, rows), vals)


def gelu(x):
    inner = 0.7978845608028654 * (x + 0.044715 * (x * x * x))
    return 0.5 * x * (1.0 + jnp.tanh(inner))


def conv_kernel(
    d,
    groups,
    has_residual,
    neighbor_ref,
    reversal_ref,
    grid_ref,
    left_ref,
    right_ref,
    above_ref,
    below_ref,
    p0_ref,
    p1_ref,
    p2_ref,
    p3_ref,
    taps_ref,
    bias_ref,
    *rest,
):
    if has_residual:
        fields_ref, out_ref, strip, weights = rest
    else:
        out_ref, strip, weights = rest
    rows, cols, ch = grid_ref.shape
    face = lax.axis_index("face")
    tile = lax.axis_index("tile")
    nface = lax.axis_size("face")
    last_tile = lax.axis_size("tile") - 1

    for a in range(4):
        for e in range(3):
            at = (a * 3 + e) * ch
            if a < 3:
                weights[at : at + ch, :ch] = taps_ref[a * 3 + e]
            else:
                weights[at : at + ch, :ch] = jnp.zeros((ch, ch), BF16)
            if a > 0:
                weights[at : at + ch, ch:] = taps_ref[(a - 1) * 3 + e]
            else:
                weights[at : at + ch, ch:] = jnp.zeros((ch, ch), BF16)

    def build(r, carry):
        v = grid_ref[r]
        p = r + d
        strip[p, :, ch : 2 * ch] = v
        strip[p, d:, :ch] = v[: cols - d]
        strip[p, :d, :ch] = left_ref[r]
        strip[p, : cols - d, 2 * ch :] = v[d:]
        strip[p, cols - d :, 2 * ch :] = right_ref[r]
        return carry

    lax.fori_loop(0, rows, build, 0, unroll=4)

    def plain_rows(source_ref, at):
        for r in range(d):
            for e in range(3):
                strip[at + r, :, e * ch : (e + 1) * ch] = source_ref[r, e * d : e * d + cols, :]

    def polar_rows(which, at):
        sector = neighbor_ref[face, which]
        flip = reversal_ref[face, which]
        for e in range(3):
            place = iota((cols, 1), 0) + e * d
            place = jnp.where(flip == 1, cols + 2 * d - 1 - place, place)
            column = place - d + cols
            step = jnp.where(column >= 2 * cols, 2, jnp.where(column >= cols, 1, 0))
            inside = column - step * cols
            shift = lax.rem(face - sector - (step - 1) + 2 * nface, nface)
            wanted = shift * cols + inside
            pick = jnp.where(iota((cols, nface * cols), 1) == wanted, 1.0, 0.0).astype(BF16)
            for r in range(d):
                source = jnp.concatenate(
                    [ref[d - 1 - r] for ref in (p0_ref, p1_ref, p2_ref, p3_ref)], axis=0
                )
                strip[at + r, :, e * ch : (e + 1) * ch] = jnp.dot(
                    pick, source, preferred_element_type=F32
                ).astype(BF16)

    @pl.when(tile > 0)
    def _():
        plain_rows(above_ref, 0)

    @pl.when(tile == 0)
    def _():
        polar_rows(0, 0)

    @pl.when(tile < last_tile)
    def _():
        plain_rows(below_ref, rows + d)

    @pl.when(tile == last_tile)
    def _():
        polar_rows(1, rows + d)

    bias = bias_ref[...]
    bias2 = jnp.concatenate([bias, bias], axis=1)
    m = d * cols

    def block(i, carry):
        base = i * (groups * 2 * d)
        parts = []
        for a in range(4):
            for_a = [
                strip[pl.ds(base + g * 2 * d + a * d, d)].reshape(m, 3 * ch) for g in range(groups)
            ]
            parts.append(jnp.concatenate(for_a, axis=0))
        lhs = jnp.concatenate(parts, axis=1)
        acc = jnp.dot(lhs, weights[...], preferred_element_type=F32) + bias2
        y = gelu(acc)
        for g in range(groups):
            for half in range(2):
                at = base + g * 2 * d + half * d
                piece = y[g * m : (g + 1) * m, half * ch : (half + 1) * ch].reshape(d, cols, ch)
                if has_residual:
                    piece = piece + fields_ref[pl.ds(at, d)].astype(F32)
                out_ref[pl.ds(at, d)] = piece.astype(out_ref.dtype)
        return carry

    lax.fori_loop(0, rows // (groups * 2 * d), block, 0)


def conv(grid, halo, polar, neighbor, reversal, taps, bias, d, groups, fields, out_dtype, name):
    rows, cols, ch = grid.shape
    left, right, above, below = halo
    operands = [neighbor, reversal, grid, left, right, above, below, *polar, taps]
    operands.append(bias.reshape(1, ch))
    smem = full_spec(pltpu.SMEM)
    in_specs = [smem, smem] + [full_spec()] * (len(operands) - 2)
    if fields is not None:
        operands.append(fields)
        in_specs.append(full_spec())
    return pl.pallas_call(
        functools.partial(conv_kernel, d, groups, fields is not None),
        out_shape=jax.ShapeDtypeStruct((rows, cols, ch), out_dtype),
        in_specs=in_specs,
        out_specs=full_spec(),
        scratch_shapes=[
            VMEM((rows + 2 * d, cols, 3 * ch), BF16),
            VMEM((12 * ch, 2 * ch), BF16),
        ],
        cost_estimate=pl.CostEstimate(
            flops=2 * 12 * rows * cols * ch * ch, bytes_accessed=9_000_000, transcendentals=0
        ),
        name=name,
    )(*operands)


def scatter_kernel(
    side, recv_ref, weight_ref, first_ref, mixed_ref, acc_ref, enc, cells_v, cells_s, sem, first_sem
):
    load = pltpu.make_async_copy(first_ref, acc_ref, first_sem)
    load.start()
    sources = recv_ref.shape[0]
    ch = weight_ref.shape[1]
    for g in range(sources // 8):
        meta = jnp.sum(recv_ref[g * 8 : (g + 1) * 8, CAP:, :].astype(F32), axis=0)
        cells_v[g : g + 1, :] = (meta[0:1, :] * side + meta[1:2, :]).astype(I32)
    copy = pltpu.make_async_copy(cells_v, cells_s, sem)
    copy.start()
    for g in range(sources // 8):
        rows = recv_ref[g * 8 : (g + 1) * 8, :CAP, :].reshape(8 * CAP, recv_ref.shape[2])
        enc[g * 128 : (g + 1) * 128, :] = jnp.dot(
            rows, weight_ref[...], preferred_element_type=F32
        )
    copy.wait()
    load.wait()

    def add_rows(g, carry):
        for j in range(128):
            c = cells_s[g, j]
            acc_ref[pl.ds(c, 1), :] += enc[pl.ds(g * 128 + j, 1), :]
        return carry

    lax.fori_loop(0, sources // 8, add_rows, 0)

    def rounding(r, carry):
        mixed_ref[r] = acc_ref[pl.ds(r * side, side), :].astype(BF16)
        return carry

    lax.fori_loop(0, side, rounding, 0, unroll=4)


def scatter(recv, weight, first):
    side, cols, ch = first.shape
    sources, height, features = recv.shape
    flat = first.reshape(side * cols, ch)
    return pl.pallas_call(
        functools.partial(scatter_kernel, side),
        out_shape=jax.ShapeDtypeStruct((side, cols, ch), BF16),
        in_specs=[full_spec(), full_spec(), full_spec(pl.ANY)],
        out_specs=full_spec(),
        scratch_shapes=[
            VMEM(flat.shape, F32),
            VMEM((sources * CAP, ch), F32),
            VMEM((sources // 8, 128), I32),
            pltpu.SMEM((sources // 8, 128), I32),
            pltpu.SemaphoreType.DMA,
            pltpu.SemaphoreType.DMA,
        ],
        cost_estimate=pl.CostEstimate(
            flops=200_000_000, bytes_accessed=12_000_000, transcendentals=0
        ),
        name="scatter",
    )(recv, weight, flat)


def exchange(grid, d):
    nface = lax.axis_size("face")
    ntile = lax.axis_size("tile")
    rows = grid.shape[0]
    left = lax.ppermute(grid[:, grid.shape[1] - d :], "face", [(f, (f + 1) % nface) for f in range(nface)])
    right = lax.ppermute(grid[:, :d], "face", [(f, (f - 1) % nface) for f in range(nface)])
    tile = lax.axis_index("tile")
    edge = jnp.where(tile == 0, grid[:d], grid[rows - d :])
    ends = (0, ntile - 1)
    polar = [edge]
    for k in range(1, nface):
        pairs = [(f * ntile + t, ((f + k) % nface) * ntile + t) for f in range(nface) for t in ends]
        polar.append(lax.ppermute(edge, ("face", "tile"), pairs))
    wide_top = jnp.concatenate([left[:d], grid[:d], right[:d]], axis=1)
    wide_bottom = jnp.concatenate([left[rows - d :], grid[rows - d :], right[rows - d :]], axis=1)
    above = lax.ppermute(wide_bottom, "tile", [(t, t + 1) for t in range(ntile - 1)])
    below = lax.ppermute(wide_top, "tile", [(t + 1, t) for t in range(ntile - 1)])
    return (left, right, above, below), polar


def local(
    fields,
    first_kernel_taps,
    first_conv_bias,
    second_kernel_taps,
    second_conv_bias,
    obs_weight,
    obs_values,
    obs_owner,
    obs_cells,
    polar_neighbor_sector,
    polar_link_reversal,
):
    side = fields.shape[0]
    dests = lax.axis_size("face") * lax.axis_size("tile")
    send = pack(obs_owner, obs_cells, obs_values, dests, side)
    recv = lax.all_to_all(send, ("face", "tile"), split_axis=0, concat_axis=0, tiled=True)
    halo, polar = exchange(fields, FIRST_DILATION)
    first = conv(
        fields, halo, polar, polar_neighbor_sector, polar_link_reversal,
        first_kernel_taps, first_conv_bias, FIRST_DILATION, 2, None, F32, "conv_first",
    )
    mixed = scatter(recv, obs_weight, first)
    halo, polar = exchange(mixed, SECOND_DILATION)
    return conv(
        mixed, halo, polar, polar_neighbor_sector, polar_link_reversal,
        second_kernel_taps, second_conv_bias, SECOND_DILATION, 1, fields, BF16, "conv_second",
    )


def solution(mesh):
    in_specs = (
        P("tile", "face", None),
        P(),
        P(),
        P(),
        P(),
        P(),
        P(("face", "tile"), None),
        P(("face", "tile"), None),
        P(("face", "tile")),
        P(),
        P(),
    )
    out_specs = P("tile", "face", None)
    return jax.shard_map(local, mesh=mesh, in_specs=in_specs, out_specs=out_specs, check_vma=False)
```

profile of v0, /device:TPU:0, one launch (start us, length us, event | category | flops | bytes accessed | tf_op | source)
XLA Modules:
  0.0 105.3 jit_solution(9211390500258601805)
XLA Ops:
  0.0 1.1 %fusion.1 = (bf16[96,2,128]{2,1,0:T(2,128)(2,1)S(1)}, bf16[96,2,128]{2,1,0:T(2,128)(2,1)S(1)}) fusion(bf16[96,96,128]{2,1,0:T(8,128)(2,1)} %rest_0_.1), kind=kLoop, calls=%fused_computation.7 | loop fusion | bytes 196608 | tf_op jit(solution)/shard_map/slice | solution.py:308
  1.1 4.2 %collective-permute-start.1 = (bf16[96,2,128]{2,1,0:T(2,128)(2,1)S(1)}, bf16[96,2,128]{2,1,0:T(2,128)(2,1)S(1)}, u32[]{:S(2)}, u32[]{:S(2)}) collective-permute-start(bf16[96,2,128]{2,1,0:T(2,128)(2,1)S(1)} %get-tuple-element.13), channel_id=1, source_target_pairs={{0,96},{32,0},{64,32},{96,64},{1,97},{33,1},{65,33},{97,65},{2,98}... | collective-permute-start | bytes 147464 | tf_op jit(solution)/shard_map/ppermute | solution.py:308
  5.4 3.7 %pack.1 = bf16[128,24,128]{2,1,0:T(8,128)(2,1)} custom-call(s32[1,1024]{1,0:T(1,128)} %bitcast.6, s32[1,1024]{1,0:T(1,128)} %bitcast.7, bf16[1024,128]{1,0:T(8,128)(2,1)} %vals_ref.1), custom_call_target="tpu_custom_call" | custom-call | flops 536870912 | bytes 2000000 | tf_op jit(solution)/shard_map/pack/pallas_call | solution.py:80
  9.1 10.3 %all-to-all-start = ((bf16[128,24,128]{2,1,0:T(8,128)(2,1)}), bf16[128,24,128]{2,1,0:T(8,128)(2,1)S(1)}, u32[]{:S(2)}, u32[]{:S(2)}) async-start(bf16[128,24,128]{2,1,0:T(8,128)(2,1)} %pack.1), calls=%async_computation | async-start | bytes 1572864 | tf_op jit(solution)/shard_map/all_to_all | solution.py:339
  20.3 1.3 %collective-permute-start.2 = (bf16[2,100,128]{2,1,0:T(8,128)(2,1)S(1)}, bf16[2,100,128]{2,1,0:T(8,128)(2,1)S(1)}, u32[]{:S(2)}, u32[]{:S(2)}) collective-permute-start(bf16[2,100,128]{2,1,0:T(8,128)(2,1)S(1)} %pad_maximum_fusion.2), channel_id=1, source_target_pairs={{0,1},{1,2},{2,3},{3,4},{4,5},{5,6},{6,7},{7,8},{8,9},{9,10},{10,1... | collective-permute-start | bytes 153608 | tf_op jit(solution)/shard_map/ppermute | solution.py:318
  21.7 1.3 %collective-permute-start.3 = (bf16[2,100,128]{2,1,0:T(8,128)(2,1)S(1)}, bf16[2,100,128]{2,1,0:T(8,128)(2,1)S(1)}, u32[]{:S(2)}, u32[]{:S(2)}) collective-permute-start(bf16[2,100,128]{2,1,0:T(8,128)(2,1)S(1)} %pad_maximum_fusion.3), channel_id=1, source_target_pairs={{1,0},{2,1},{3,2},{4,3},{5,4},{6,5},{7,6},{8,7},{9,8},{10,9},{11,1... | collective-permute-start | bytes 153608 | tf_op jit(solution)/shard_map/ppermute | solution.py:319
  23.0 5.4 %collective-permute-start.6 = (bf16[2,96,128]{2,1,0:T(8,128)(2,1)S(1)}, bf16[2,96,128]{2,1,0:T(8,128)(2,1)S(1)}, u32[]{:S(2)}, u32[]{:S(2)}) collective-permute-start(bf16[2,96,128]{2,1,0:T(8,128)(2,1)S(1)} %get-tuple-element.10.p0_ref), channel_id=1, source_target_pairs={{0,96},{31,127},{32,0},{63,31},{64,32},{95,63},{96,64},{127,95}} | collective-permute-start | bytes 147464 | tf_op jit(solution)/shard_map/ppermute | solution.py:315
  28.4 2.2 %collective-permute-start.5 = (bf16[2,96,128]{2,1,0:T(8,128)(2,1)S(1)}, bf16[2,96,128]{2,1,0:T(8,128)(2,1)S(1)}, u32[]{:S(2)}, u32[]{:S(2)}) collective-permute-start(bf16[2,96,128]{2,1,0:T(8,128)(2,1)S(1)} %get-tuple-element.10.p0_ref), channel_id=1, source_target_pairs={{0,64},{31,95},{32,96},{63,127},{64,0},{95,31},{96,32},{127,63}} | collective-permute-start | bytes 147464 | tf_op jit(solution)/shard_map/ppermute | solution.py:315
  30.6 3.0 %collective-permute-start.4 = (bf16[2,96,128]{2,1,0:T(8,128)(2,1)S(1)}, bf16[2,96,128]{2,1,0:T(8,128)(2,1)S(1)}, u32[]{:S(2)}, u32[]{:S(2)}) collective-permute-start(bf16[2,96,128]{2,1,0:T(8,128)(2,1)S(1)} %get-tuple-element.10.p0_ref), channel_id=1, source_target_pairs={{0,32},{31,63},{32,64},{63,95},{64,96},{95,127},{96,0},{127,31}} | collective-permute-start | bytes 147464 | tf_op jit(solution)/shard_map/ppermute | solution.py:315
  36.0 1.9 %collective-permute-done.4.p1_ref = bf16[2,96,128]{2,1,0:T(8,128)(2,1)S(1)} collective-permute-done((bf16[2,96,128]{2,1,0:T(8,128)(2,1)S(1)}, bf16[2,96,128]{2,1,0:T(8,128)(2,1)S(1)}, u32[]{:S(2)}, u32[]{:S(2)}) %collective-permute-start.4) | collective-permute-done | bytes 49184 | tf_op jit(solution)/shard_map/ppermute | solution.py:315
  38.5 12.4 %conv_first.1 = f32[96,96,128]{2,1,0:T(8,128)} custom-call(s32[4,2]{1,0:T(4,128)} %copy.14.neighbor_ref, s32[4,2]{1,0:T(4,128)} %copy.15.reversal_ref, bf16[96,96,128]{2,1,0:T(8,128)(2,1)} %rest_0_.1, bf16[96,2,128]{2,1,0:T(2,128)(2,1)} %copy-done.8, bf16[96,2,128]{2,1,0:T(2,128)(2,1)} %copy-done.7, bf16[2,100,128]{2,1,0:T(8,128)(2,1)} %copy-done.14, ...), custom_call_target="tpu_custom_call" | custom-call | flops 3623878656 | bytes 9000000 | tf_op jit(solution)/shard_map/conv_first/pallas_call | solution.py:228
  51.8 14.9 %scatter.1.grid_ref = bf16[96,96,128]{2,1,0:T(8,128)(2,1)} custom-call(bf16[128,24,128]{2,1,0:T(8,128)(2,1)} %copy-done, bf16[128,128]{1,0:T(8,128)(2,1)} %weight_ref.1, f32[9216,128]{1,0:T(8,128)} %bitcast.5), custom_call_target="tpu_custom_call" | custom-call | flops 200000000 | bytes 12000000 | tf_op jit(solution)/shard_map/scatter/pallas_call | solution.py:283
  66.7 1.1 %fusion = (bf16[96,4,128]{2,1,0:T(4,128)(2,1)S(1)}, bf16[96,4,128]{2,1,0:T(4,128)(2,1)S(1)}) fusion(bf16[96,96,128]{2,1,0:T(8,128)(2,1)} %scatter.1.grid_ref), kind=kLoop, calls=%fused_computation.6 | loop fusion | bytes 393216 | tf_op jit(solution)/shard_map/slice | solution.py:308
  69.6 1.4 %collective-permute-start.7 = (bf16[96,4,128]{2,1,0:T(4,128)(2,1)S(1)}, bf16[96,4,128]{2,1,0:T(4,128)(2,1)S(1)}, u32[]{:S(2)}, u32[]{:S(2)}) collective-permute-start(bf16[96,4,128]{2,1,0:T(4,128)(2,1)S(1)} %get-tuple-element.9), channel_id=1, source_target_pairs={{0,32},{32,64},{64,96},{96,0},{1,33},{33,65},{65,97},{97,1},{2,34}... | collective-permute-start | bytes 294920 | tf_op jit(solution)/shard_map/ppermute | solution.py:307
  71.0 1.5 %collective-permute-done.8.right_ref = bf16[96,4,128]{2,1,0:T(4,128)(2,1)S(1)} collective-permute-done((bf16[96,4,128]{2,1,0:T(4,128)(2,1)S(1)}, bf16[96,4,128]{2,1,0:T(4,128)(2,1)S(1)}, u32[]{:S(2)}, u32[]{:S(2)}) %collective-permute-start.8) | collective-permute-done | bytes 98336 | tf_op jit(solution)/shard_map/ppermute | solution.py:308
  72.5 3.0 %collective-permute-done.7.left_ref = bf16[96,4,128]{2,1,0:T(4,128)(2,1)S(1)} collective-permute-done((bf16[96,4,128]{2,1,0:T(4,128)(2,1)S(1)}, bf16[96,4,128]{2,1,0:T(4,128)(2,1)S(1)}, u32[]{:S(2)}, u32[]{:S(2)}) %collective-permute-start.7) | collective-permute-done | bytes 98336 | tf_op jit(solution)/shard_map/ppermute | solution.py:307
  75.5 1.3 %collective-permute-start.9 = (bf16[4,104,128]{2,1,0:T(8,128)(2,1)S(1)}, bf16[4,104,128]{2,1,0:T(8,128)(2,1)S(1)}, u32[]{:S(2)}, u32[]{:S(2)}) collective-permute-start(bf16[4,104,128]{2,1,0:T(8,128)(2,1)S(1)} %pad_maximum_fusion), channel_id=1, source_target_pairs={{0,1},{1,2},{2,3},{3,4},{4,5},{5,6},{6,7},{7,8},{8,9},{9,10},{10,1... | collective-permute-start | bytes 319496 | tf_op jit(solution)/shard_map/ppermute | solution.py:318
  76.9 1.3 %collective-permute-start.10 = (bf16[4,104,128]{2,1,0:T(8,128)(2,1)S(1)}, bf16[4,104,128]{2,1,0:T(8,128)(2,1)S(1)}, u32[]{:S(2)}, u32[]{:S(2)}) collective-permute-start(bf16[4,104,128]{2,1,0:T(8,128)(2,1)S(1)} %pad_maximum_fusion.1), channel_id=1, source_target_pairs={{1,0},{2,1},{3,2},{4,3},{5,4},{6,5},{7,6},{8,7},{9,8},{10,9},{11,1... | collective-permute-start | bytes 319496 | tf_op jit(solution)/shard_map/ppermute | solution.py:319
  78.2 2.2 %collective-permute-start.13 = (bf16[4,96,128]{2,1,0:T(8,128)(2,1)S(1)}, bf16[4,96,128]{2,1,0:T(8,128)(2,1)S(1)}, u32[]{:S(2)}, u32[]{:S(2)}) collective-permute-start(bf16[4,96,128]{2,1,0:T(8,128)(2,1)S(1)} %get-tuple-element.5.p0_ref), channel_id=1, source_target_pairs={{0,96},{31,127},{32,0},{63,31},{64,32},{95,63},{96,64},{127,95}} | collective-permute-start | bytes 294920 | tf_op jit(solution)/shard_map/ppermute | solution.py:315
  80.4 3.8 %collective-permute-start.12 = (bf16[4,96,128]{2,1,0:T(8,128)(2,1)S(1)}, bf16[4,96,128]{2,1,0:T(8,128)(2,1)S(1)}, u32[]{:S(2)}, u32[]{:S(2)}) collective-permute-start(bf16[4,96,128]{2,1,0:T(8,128)(2,1)S(1)} %get-tuple-element.5.p0_ref), channel_id=1, source_target_pairs={{0,64},{31,95},{32,96},{63,127},{64,0},{95,31},{96,32},{127,63}} | collective-permute-start | bytes 294920 | tf_op jit(solution)/shard_map/ppermute | solution.py:315
  84.2 1.9 %collective-permute-start.11 = (bf16[4,96,128]{2,1,0:T(8,128)(2,1)S(1)}, bf16[4,96,128]{2,1,0:T(8,128)(2,1)S(1)}, u32[]{:S(2)}, u32[]{:S(2)}) collective-permute-start(bf16[4,96,128]{2,1,0:T(8,128)(2,1)S(1)} %get-tuple-element.5.p0_ref), channel_id=1, source_target_pairs={{0,32},{31,63},{32,64},{63,95},{64,96},{95,127},{96,0},{127,31}} | collective-permute-start | bytes 294920 | tf_op jit(solution)/shard_map/ppermute | solution.py:315
  86.1 2.2 %collective-permute-done.12.p2_ref = bf16[4,96,128]{2,1,0:T(8,128)(2,1)S(1)} collective-permute-done((bf16[4,96,128]{2,1,0:T(8,128)(2,1)S(1)}, bf16[4,96,128]{2,1,0:T(8,128)(2,1)S(1)}, u32[]{:S(2)}, u32[]{:S(2)}) %collective-permute-start.12) | collective-permute-done | bytes 98336 | tf_op jit(solution)/shard_map/ppermute | solution.py:315
  88.4 3.5 %collective-permute-done.11.p1_ref = bf16[4,96,128]{2,1,0:T(8,128)(2,1)S(1)} collective-permute-done((bf16[4,96,128]{2,1,0:T(8,128)(2,1)S(1)}, bf16[4,96,128]{2,1,0:T(8,128)(2,1)S(1)}, u32[]{:S(2)}, u32[]{:S(2)}) %collective-permute-start.11) | collective-permute-done | bytes 98336 | tf_op jit(solution)/shard_map/ppermute | solution.py:315
  92.6 12.7 %conv_second.1 = bf16[96,96,128]{2,1,0:T(8,128)(2,1)} custom-call(s32[4,2]{1,0:T(4,128)} %copy.14.neighbor_ref, s32[4,2]{1,0:T(4,128)} %copy.15.reversal_ref, bf16[96,96,128]{2,1,0:T(8,128)(2,1)} %scatter.1.grid_ref, bf16[96,4,128]{2,1,0:T(4,128)(2,1)} %copy-done.6, bf16[96,4,128]{2,1,0:T(4,128)(2,1)} %copy-done.5, bf16[4,104,128]{2,1,0:T(8,128)(2,1)} %copy-done.9, ...), custom_call_target="tpu_custom_call" | custom-call | flops 3623878656 | bytes 9000000 | tf_op jit(solution)/shard_map/conv_second/pallas_call | solution.py:228
  (62 shorter events, 7.2 us)
Async XLA Ops:
  0.0 33.7 %copy-start.3 = (s32[4,2]{0,1:T(2,128)S(1)}, s32[4,2]{0,1:T(2,128)}, u32[]{:S(2)}) copy-start(s32[4,2]{0,1:T(2,128)} %param.20) | copy-start | bytes 100
  0.0 34.4 %copy-start.4 = (s32[4,2]{0,1:T(2,128)S(1)}, s32[4,2]{0,1:T(2,128)}, u32[]{:S(2)}) copy-start(s32[4,2]{0,1:T(2,128)} %param.21) | copy-start | bytes 100
  1.1 19.1 %collective-permute-start.1 = (bf16[96,2,128]{2,1,0:T(2,128)(2,1)S(1)}, bf16[96,2,128]{2,1,0:T(2,128)(2,1)S(1)}, u32[]{:S(2)}, u32[]{:S(2)}) collective-permute-start(bf16[96,2,128]{2,1,0:T(2,128)(2,1)S(1)} %get-tuple-element.13), channel_id=1, source_target_pairs={{0,96},{32,0},{64,32},{96,64},{1,97},{33,1},{65,33},{97,65},{2,98}... | collective-permute-start | bytes 147464 | tf_op jit(solution)/shard_map/ppermute | solution.py:308
  5.4 14.9 %collective-permute-start = (bf16[96,2,128]{2,1,0:T(2,128)(2,1)S(1)}, bf16[96,2,128]{2,1,0:T(2,128)(2,1)S(1)}, u32[]{:S(2)}, u32[]{:S(2)}) collective-permute-start(bf16[96,2,128]{2,1,0:T(2,128)(2,1)S(1)} %get-tuple-element.14), channel_id=1, source_target_pairs={{0,32},{32,64},{64,96},{96,0},{1,33},{33,65},{65,97},{97,1},{2,34}... | collective-permute-start | bytes 147464 | tf_op jit(solution)/shard_map/ppermute | solution.py:307
  9.1 41.8 %all-to-all-start = ((bf16[128,24,128]{2,1,0:T(8,128)(2,1)}), bf16[128,24,128]{2,1,0:T(8,128)(2,1)S(1)}, u32[]{:S(2)}, u32[]{:S(2)}) async-start(bf16[128,24,128]{2,1,0:T(8,128)(2,1)} %pack.1), calls=%async_computation | async-start | bytes 1572864 | tf_op jit(solution)/shard_map/all_to_all | solution.py:339
  20.2 17.7 %copy-start.2 = (bf16[2,96,128]{2,1,0:T(8,128)(2,1)}, bf16[2,96,128]{2,1,0:T(8,128)(2,1)S(1)}, u32[]{:S(2)}) copy-start(bf16[2,96,128]{2,1,0:T(8,128)(2,1)S(1)} %get-tuple-element.10.p0_ref) | copy-start | bytes 147460
  20.2 17.7 %copy-start.7 = (bf16[96,2,128]{2,1,0:T(2,128)(2,1)}, bf16[96,2,128]{2,1,0:T(2,128)(2,1)S(1)}, u32[]{:S(2)}) copy-start(bf16[96,2,128]{2,1,0:T(2,128)(2,1)S(1)} %collective-permute-done.1.right_ref) | copy-start | bytes 147460
  20.2 17.6 %copy-start.8 = (bf16[96,2,128]{2,1,0:T(2,128)(2,1)}, bf16[96,2,128]{2,1,0:T(2,128)(2,1)S(1)}, u32[]{:S(2)}) copy-start(bf16[96,2,128]{2,1,0:T(2,128)(2,1)S(1)} %collective-permute-done.left_ref) | copy-start | bytes 147460
  20.3 17.5 %collective-permute-start.2 = (bf16[2,100,128]{2,1,0:T(8,128)(2,1)S(1)}, bf16[2,100,128]{2,1,0:T(8,128)(2,1)S(1)}, u32[]{:S(2)}, u32[]{:S(2)}) collective-permute-start(bf16[2,100,128]{2,1,0:T(8,128)(2,1)S(1)} %pad_maximum_fusion.2), channel_id=1, source_target_pairs={{0,1},{1,2},{2,3},{3,4},{4,5},{5,6},{6,7},{7,8},{8,9},{9,10},{10,1... | collective-permute-start | bytes 153608 | tf_op jit(solution)/shard_map/ppermute | solution.py:318
  21.7 16.2 %collective-permute-start.3 = (bf16[2,100,128]{2,1,0:T(8,128)(2,1)S(1)}, bf16[2,100,128]{2,1,0:T(8,128)(2,1)S(1)}, u32[]{:S(2)}, u32[]{:S(2)}) collective-permute-start(bf16[2,100,128]{2,1,0:T(8,128)(2,1)S(1)} %pad_maximum_fusion.3), channel_id=1, source_target_pairs={{1,0},{2,1},{3,2},{4,3},{5,4},{6,5},{7,6},{8,7},{9,8},{10,9},{11,1... | collective-permute-start | bytes 153608 | tf_op jit(solution)/shard_map/ppermute | solution.py:319
  23.0 12.0 %collective-permute-start.6 = (bf16[2,96,128]{2,1,0:T(8,128)(2,1)S(1)}, bf16[2,96,128]{2,1,0:T(8,128)(2,1)S(1)}, u32[]{:S(2)}, u32[]{:S(2)}) collective-permute-start(bf16[2,96,128]{2,1,0:T(8,128)(2,1)S(1)} %get-tuple-element.10.p0_ref), channel_id=1, source_target_pairs={{0,96},{31,127},{32,0},{63,31},{64,32},{95,63},{96,64},{127,95}} | collective-permute-start | bytes 147464 | tf_op jit(solution)/shard_map/ppermute | solution.py:315
  28.4 7.5 %collective-permute-start.5 = (bf16[2,96,128]{2,1,0:T(8,128)(2,1)S(1)}, bf16[2,96,128]{2,1,0:T(8,128)(2,1)S(1)}, u32[]{:S(2)}, u32[]{:S(2)}) collective-permute-start(bf16[2,96,128]{2,1,0:T(8,128)(2,1)S(1)} %get-tuple-element.10.p0_ref), channel_id=1, source_target_pairs={{0,64},{31,95},{32,96},{63,127},{64,0},{95,31},{96,32},{127,63}} | collective-permute-start | bytes 147464 | tf_op jit(solution)/shard_map/ppermute | solution.py:315
  30.6 7.2 %collective-permute-start.4 = (bf16[2,96,128]{2,1,0:T(8,128)(2,1)S(1)}, bf16[2,96,128]{2,1,0:T(8,128)(2,1)S(1)}, u32[]{:S(2)}, u32[]{:S(2)}) collective-permute-start(bf16[2,96,128]{2,1,0:T(8,128)(2,1)S(1)} %get-tuple-element.10.p0_ref), channel_id=1, source_target_pairs={{0,32},{31,63},{32,64},{63,95},{64,96},{95,127},{96,0},{127,31}} | collective-permute-start | bytes 147464 | tf_op jit(solution)/shard_map/ppermute | solution.py:315
  67.8 4.7 %collective-permute-start.8 = (bf16[96,4,128]{2,1,0:T(4,128)(2,1)S(1)}, bf16[96,4,128]{2,1,0:T(4,128)(2,1)S(1)}, u32[]{:S(2)}, u32[]{:S(2)}) collective-permute-start(bf16[96,4,128]{2,1,0:T(4,128)(2,1)S(1)} %get-tuple-element.8), channel_id=1, source_target_pairs={{0,96},{32,0},{64,32},{96,64},{1,97},{33,1},{65,33},{97,65},{2,98}... | collective-permute-start | bytes 294920 | tf_op jit(solution)/shard_map/ppermute | solution.py:308
  69.6 22.4 %copy-start.1 = (bf16[4,96,128]{2,1,0:T(8,128)(2,1)}, bf16[4,96,128]{2,1,0:T(8,128)(2,1)S(1)}, u32[]{:S(2)}) copy-start(bf16[4,96,128]{2,1,0:T(8,128)(2,1)S(1)} %get-tuple-element.5.p0_ref) | copy-start | bytes 294916
  69.6 5.9 %collective-permute-start.7 = (bf16[96,4,128]{2,1,0:T(4,128)(2,1)S(1)}, bf16[96,4,128]{2,1,0:T(4,128)(2,1)S(1)}, u32[]{:S(2)}, u32[]{:S(2)}) collective-permute-start(bf16[96,4,128]{2,1,0:T(4,128)(2,1)S(1)} %get-tuple-element.9), channel_id=1, source_target_pairs={{0,32},{32,64},{64,96},{96,0},{1,33},{33,65},{65,97},{97,1},{2,34}... | collective-permute-start | bytes 294920 | tf_op jit(solution)/shard_map/ppermute | solution.py:307
  72.5 19.4 %copy-start.5 = (bf16[96,4,128]{2,1,0:T(4,128)(2,1)}, bf16[96,4,128]{2,1,0:T(4,128)(2,1)S(1)}, u32[]{:S(2)}) copy-start(bf16[96,4,128]{2,1,0:T(4,128)(2,1)S(1)} %collective-permute-done.8.right_ref) | copy-start | bytes 294916
  75.5 16.5 %copy-start.6 = (bf16[96,4,128]{2,1,0:T(4,128)(2,1)}, bf16[96,4,128]{2,1,0:T(4,128)(2,1)S(1)}, u32[]{:S(2)}) copy-start(bf16[96,4,128]{2,1,0:T(4,128)(2,1)S(1)} %collective-permute-done.7.left_ref) | copy-start | bytes 294916
  75.5 16.4 %collective-permute-start.9 = (bf16[4,104,128]{2,1,0:T(8,128)(2,1)S(1)}, bf16[4,104,128]{2,1,0:T(8,128)(2,1)S(1)}, u32[]{:S(2)}, u32[]{:S(2)}) collective-permute-start(bf16[4,104,128]{2,1,0:T(8,128)(2,1)S(1)} %pad_maximum_fusion), channel_id=1, source_target_pairs={{0,1},{1,2},{2,3},{3,4},{4,5},{5,6},{6,7},{7,8},{8,9},{9,10},{10,1... | collective-permute-start | bytes 319496 | tf_op jit(solution)/shard_map/ppermute | solution.py:318
  76.9 15.0 %collective-permute-start.10 = (bf16[4,104,128]{2,1,0:T(8,128)(2,1)S(1)}, bf16[4,104,128]{2,1,0:T(8,128)(2,1)S(1)}, u32[]{:S(2)}, u32[]{:S(2)}) collective-permute-start(bf16[4,104,128]{2,1,0:T(8,128)(2,1)S(1)} %pad_maximum_fusion.1), channel_id=1, source_target_pairs={{1,0},{2,1},{3,2},{4,3},{5,4},{6,5},{7,6},{8,7},{9,8},{10,9},{11,1... | collective-permute-start | bytes 319496 | tf_op jit(solution)/shard_map/ppermute | solution.py:319
  78.2 7.9 %collective-permute-start.13 = (bf16[4,96,128]{2,1,0:T(8,128)(2,1)S(1)}, bf16[4,96,128]{2,1,0:T(8,128)(2,1)S(1)}, u32[]{:S(2)}, u32[]{:S(2)}) collective-permute-start(bf16[4,96,128]{2,1,0:T(8,128)(2,1)S(1)} %get-tuple-element.5.p0_ref), channel_id=1, source_target_pairs={{0,96},{31,127},{32,0},{63,31},{64,32},{95,63},{96,64},{127,95}} | collective-permute-start | bytes 294920 | tf_op jit(solution)/shard_map/ppermute | solution.py:315
  80.4 8.0 %collective-permute-start.12 = (bf16[4,96,128]{2,1,0:T(8,128)(2,1)S(1)}, bf16[4,96,128]{2,1,0:T(8,128)(2,1)S(1)}, u32[]{:S(2)}, u32[]{:S(2)}) collective-permute-start(bf16[4,96,128]{2,1,0:T(8,128)(2,1)S(1)} %get-tuple-element.5.p0_ref), channel_id=1, source_target_pairs={{0,64},{31,95},{32,96},{63,127},{64,0},{95,31},{96,32},{127,63}} | collective-permute-start | bytes 294920 | tf_op jit(solution)/shard_map/ppermute | solution.py:315
  84.2 7.7 %collective-permute-start.11 = (bf16[4,96,128]{2,1,0:T(8,128)(2,1)S(1)}, bf16[4,96,128]{2,1,0:T(8,128)(2,1)S(1)}, u32[]{:S(2)}, u32[]{:S(2)}) collective-permute-start(bf16[4,96,128]{2,1,0:T(8,128)(2,1)S(1)} %get-tuple-element.5.p0_ref), channel_id=1, source_target_pairs={{0,32},{31,63},{32,64},{63,95},{64,96},{95,127},{96,0},{127,31}} | collective-permute-start | bytes 294920 | tf_op jit(solution)/shard_map/ppermute | solution.py:315
  86.1 5.8 %copy-start.11 = (bf16[4,96,128]{2,1,0:T(8,128)(2,1)}, bf16[4,96,128]{2,1,0:T(8,128)(2,1)S(1)}, u32[]{:S(2)}) copy-start(bf16[4,96,128]{2,1,0:T(8,128)(2,1)S(1)} %collective-permute-done.13.p3_ref) | copy-start | bytes 294916
  (10 other events, 13.2 us)
where the time goes:
time: 106 us; the launch traced here: 105 us
  Pallas kernels  43.7 us (41%)
  starting transfers between devices  40.4 us (38%)
  waiting for transfers between devices  13.1 us (12%)
  local copies, waits for them, and re-layouts  5.75 us (5%)
  other arithmetic  1.92 us (2%)
    pallas_call x2, Pallas kernels, conv(): pl.pallas_call(functools.partial(conv_kernel, d, groups, fields is not No...  25.1 us
    ppermute x6, starting transfers between devices, exchange(): polar.append(lax.ppermute(edge, ('face', 'tile'), pairs))  18.6 us
    pallas_call x1, Pallas kernels, scatter(): pl.pallas_call(functools.partial(scatter_kernel, side), out_shape=jax.Sha...  14.9 us
    all_to_all x1, starting transfers between devices, local(): lax.all_to_all(send, ('face', 'tile'), split_axis=0, concat_axis=0, tiled...  10.3 us
    ppermute x6, waiting for transfers between devices, exchange(): polar.append(lax.ppermute(edge, ('face', 'tile'), pairs))  8.58 us
    ppermute x2, starting transfers between devices, exchange(): lax.ppermute(grid[:, :d], 'face', [(f, (f - 1) % nface) for f in range(nf...  5.01 us
    pallas_call x1, Pallas kernels, pack(): pl.pallas_call(functools.partial(pack_kernel, dests, side), out_shape=jax...  3.72 us
    unnamed x40, local copies, waits for them, and re-layouts  3.49 us
  transfers between devices with their start and end apart: 15, of which 6 were waited for; matrix products, arithmetic and copies ran while one was open for 3% of the time, Pallas kernels for 15%

commit v1 on v0

v1 whole, which is shorter than its diff:
```python
import functools

import jax
import jax.numpy as jnp
from jax import lax
from jax.experimental import pallas as pl
from jax.experimental.pallas import tpu as pltpu
from jax.sharding import PartitionSpec as P

FIRST_DILATION = 2
SECOND_DILATION = 4
CAP = 16
META = 8

BF16 = jnp.bfloat16
F32 = jnp.float32
I32 = jnp.int32
VMEM = pltpu.VMEM


def full_spec(memory_space=None):
    return pl.BlockSpec(memory_space=VMEM if memory_space is None else memory_space)


def iota(shape, axis):
    return lax.broadcasted_iota(I32, shape, axis)


def pack_kernel(dests, side, owner_ref, cell_ref, vals_ref, send_ref):
    rows = vals_ref.shape[0]
    owner = owner_ref[...]
    cell = cell_ref[...]
    block = 256
    earlier = (iota((block, block), 0) < iota((block, block), 1)).astype(F32).astype(BF16)
    onehot_parts = []
    rank_parts = []
    carry = jnp.zeros((dests, 1), F32)
    for b in range(rows // block):
        hit = owner[:, b * block : (b + 1) * block] == iota((dests, block), 0)
        hit_f = jnp.where(hit, 1.0, 0.0)
        hit_b = hit_f.astype(BF16)
        before = jnp.dot(hit_b, earlier, preferred_element_type=F32) + carry
        rank_parts.append(jnp.sum(before * hit_f, axis=0, keepdims=True))
        carry = carry + jnp.sum(hit_f, axis=1, keepdims=True)
        onehot_parts.append(hit_b)
    rank = jnp.concatenate(rank_parts, axis=1).astype(I32)
    onehot = jnp.concatenate(onehot_parts, axis=1)
    target = owner * CAP + rank

    cell_row = ((cell.astype(F32) + 0.5) * (1.0 / side)).astype(I32)
    cell_col = cell - cell_row * side
    me = lax.axis_index("face") * lax.axis_size("tile") + lax.axis_index("tile")
    base_lane = lax.rem(me, 8) * CAP
    slot_hit = iota((128, rows), 0) == rank + base_lane
    row_map = jnp.where(slot_hit, cell_row.astype(F32), 0.0).astype(BF16)
    col_map = jnp.where(slot_hit, cell_col.astype(F32), 0.0).astype(BF16)
    contract = (((1,), (1,)), ((), ()))
    meta_row = lax.dot_general(onehot, row_map, contract, preferred_element_type=F32)
    meta_col = lax.dot_general(onehot, col_map, contract, preferred_element_type=F32)
    meta = jnp.where(
        iota((dests, META, 128), 1) == 0,
        jnp.broadcast_to(meta_row[:, None, :], (dests, META, 128)),
        jnp.broadcast_to(meta_col[:, None, :], (dests, META, 128)),
    )
    send_ref[:, CAP:, :] = meta.astype(BF16)

    chunk_dests = 16
    chunk = chunk_dests * CAP
    for c in range(dests // chunk_dests):
        match = target == iota((chunk, rows), 0) + c * chunk
        match = jnp.where(match, 1.0, 0.0).astype(BF16)
        placed = jnp.dot(match, vals_ref[...], preferred_element_type=F32).astype(BF16)
        send_ref[c * chunk_dests : (c + 1) * chunk_dests, :CAP, :] = placed.reshape(
            chunk_dests, CAP, placed.shape[-1]
        )


def pack(owner, cells, vals, dests, side):
    rows, features = vals.shape
    return pl.pallas_call(
        functools.partial(pack_kernel, dests, side),
        out_shape=jax.ShapeDtypeStruct((dests, CAP + META, features), BF16),
        in_specs=[full_spec()] * 3,
        out_specs=full_spec(),
        cost_estimate=pl.CostEstimate(
            flops=2 * dests * CAP * rows * features, bytes_accessed=2_000_000, transcendentals=0
        ),
        name="pack",
    )(owner.reshape(1, rows), cells.reshape(1, rows), vals)


def parities():
    face = lax.axis_index("face")
    tile = lax.axis_index("tile")
    return face, tile, lax.rem(face, 2) == 0, lax.rem(tile, 2) == 0


def edges_kernel(d, grid_ref, a_ref, b_ref, low, high, sems):
    rows, cols, ch = grid_ref.shape
    _, _, face_even, tile_even = parities()
    start = jnp.where(tile_even, 0, rows - d)
    copies = [
        pltpu.make_async_copy(grid_ref.at[:, pl.ds(0, 8), :], low, sems.at[0]),
        pltpu.make_async_copy(grid_ref.at[:, pl.ds(cols - 8, 8), :], high, sems.at[1]),
        pltpu.make_async_copy(grid_ref.at[pl.ds(start, d)], a_ref.at[pl.ds(d, d)], sems.at[2]),
        pltpu.make_async_copy(grid_ref.at[pl.ds(start, d)], b_ref.at[pl.ds(d, d)], sems.at[3]),
    ]
    for copy in copies:
        copy.start()
    for copy in copies:
        copy.wait()
    per = cols // d
    group = 8 // d

    def plane(p, carry):
        for r in range(0, per, group):
            at = [p * per + r + k for k in range(group)]
            west = jnp.concatenate([low[i].astype(F32)[:d] for i in at], axis=0)
            east = jnp.concatenate([high[i].astype(F32)[8 - d :] for i in at], axis=0)
            a_ref[p, r * d : r * d + 8, :] = jnp.where(face_even, east, west).astype(BF16)
            b_ref[p, r * d : r * d + 8, :] = jnp.where(face_even, west, east).astype(BF16)
        return carry

    lax.fori_loop(0, d, plane, 0)


def edges(grid, d):
    rows, cols, ch = grid.shape
    side = jax.ShapeDtypeStruct((2 * d, cols, ch), BF16)
    return pl.pallas_call(
        functools.partial(edges_kernel, d),
        out_shape=(side, side),
        in_specs=[full_spec(pl.ANY)],
        out_specs=(full_spec(), full_spec()),
        scratch_shapes=[
            VMEM((rows, 8, ch), BF16),
            VMEM((rows, 8, ch), BF16),
            pltpu.SemaphoreType.DMA((4,)),
        ],
        cost_estimate=pl.CostEstimate(flops=1_000_000, bytes_accessed=800_000, transcendentals=0),
        name="edges",
    )(grid)


def widen_kernel(d, grid_ref, ra_ref, rb_ref, wa_ref, wb_ref, ends, sems):
    rows, cols, ch = grid_ref.shape
    _, _, face_even, tile_even = parities()
    copies = [
        pltpu.make_async_copy(grid_ref.at[pl.ds(at, d)], ends.at[i], sems.at[i])
        for i, at in enumerate((0, rows - d))
    ]
    for copy in copies:
        copy.start()
    for copy in copies:
        copy.wait()
    per = cols // d
    for r in range(d):
        wide = []
        for i, row in enumerate((r, rows - d + r)):
            at = (row % per) * d
            tile_at = at // 8 * 8
            a = ra_ref[row // per, tile_at : tile_at + 8, :].astype(F32)[at - tile_at : at - tile_at + d]
            b = rb_ref[row // per, tile_at : tile_at + 8, :].astype(F32)[at - tile_at : at - tile_at + d]
            wide.append(
                jnp.concatenate(
                    [jnp.where(face_even, b, a), ends[i, r].astype(F32), jnp.where(face_even, a, b)],
                    axis=0,
                )
            )
        wa_ref[r] = jnp.where(tile_even, wide[1], wide[0]).astype(BF16)
        wb_ref[r] = jnp.where(tile_even, wide[0], wide[1]).astype(BF16)


def widen(grid, received, d):
    rows, cols, ch = grid.shape
    wide = jax.ShapeDtypeStruct((d, cols + 2 * d, ch), BF16)
    return pl.pallas_call(
        functools.partial(widen_kernel, d),
        out_shape=(wide, wide),
        in_specs=[full_spec(pl.ANY), full_spec(), full_spec()],
        out_specs=(full_spec(), full_spec()),
        scratch_shapes=[VMEM((2, d, cols, ch), BF16), pltpu.SemaphoreType.DMA((2,))],
        cost_estimate=pl.CostEstimate(flops=1_000_000, bytes_accessed=800_000, transcendentals=0),
        name="widen",
    )(grid, *received)


def face_partner(f, nface, odd_up):
    return (f + 1) % nface if (f % 2 == 1) == odd_up else (f - 1) % nface


def swap_faces(sides):
    nface = lax.axis_size("face")
    inner = [(f, face_partner(f, nface, False)) for f in range(nface)]
    outer = [(f, face_partner(f, nface, True)) for f in range(nface)]
    return lax.ppermute(sides[0], "face", inner), lax.ppermute(sides[1], "face", outer)


def swap_tiles(wide):
    nface = lax.axis_size("face")
    ntile = lax.axis_size("tile")
    inner = [(t, t ^ 1) for t in range(ntile)]
    outer = []
    for f in range(nface):
        for t in range(ntile):
            if t in (0, ntile - 1):
                to = ((f + 2) % nface) * ntile + t
            else:
                to = f * ntile + (t + 1 if t % 2 == 1 else t - 1)
            outer.append((f * ntile + t, to))
    return lax.ppermute(wide[0], "tile", inner), lax.ppermute(wide[1], ("face", "tile"), outer)


def gelu(x):
    half = 0.5 * x
    inner = x * (0.7978845608028654 + (0.7978845608028654 * 0.044715) * (x * x))
    return half + half * jnp.tanh(inner)


def conv_kernel(
    d,
    groups,
    has_residual,
    neighbor_ref,
    reversal_ref,
    grid_ref,
    ra_ref,
    rb_ref,
    wa_ref,
    wb_ref,
    taps_ref,
    bias_ref,
    *rest,
):
    if has_residual:
        fields_ref, out_ref, strip, weights, wide, acc, result, sems, out_sems, fields = rest
    else:
        out_ref, strip, weights, wide, acc, result, sems, out_sems = rest
    rows, cols, ch = grid_ref.shape
    face, tile, face_even, tile_even = parities()
    nface = lax.axis_size("face")
    last_tile = lax.axis_size("tile") - 1
    load = pltpu.make_async_copy(
        grid_ref, strip.at[pl.ds(d, rows), :, pl.ds(ch, ch)], sems.at[0]
    )
    load.start()
    if has_residual:
        load_fields = pltpu.make_async_copy(fields_ref, fields, sems.at[1])
        load_fields.start()

    for a in range(4):
        for e in range(3):
            at = (a * 3 + e) * ch
            if a < 3:
                weights[at : at + ch, :ch] = taps_ref[a * 3 + e]
            else:
                weights[at : at + ch, :ch] = jnp.zeros((ch, ch), BF16)
            if a > 0:
                weights[at : at + ch, ch:] = taps_ref[(a - 1) * 3 + e]
            else:
                weights[at : at + ch, ch:] = jnp.zeros((ch, ch), BF16)

    for r in range(d):
        wide[0, r] = jnp.where(tile_even, wb_ref[r].astype(F32), wa_ref[r].astype(F32)).astype(BF16)
        wide[1, r] = jnp.where(tile_even, wa_ref[r].astype(F32), wb_ref[r].astype(F32)).astype(BF16)
    load.wait()

    @pl.when((tile == 0) | (tile == last_tile))
    def _():
        which = jnp.where(tile == 0, 0, 1)
        sector = neighbor_ref[face, which]
        flip = reversal_ref[face, which]
        own = jnp.where(tile == 0, d, rows)
        width = cols + 2 * d

        def source_index(s):
            s = lax.rem(s + nface, nface)
            inner = jnp.where(face_even, face + 1, face - 1)
            outer = lax.rem(jnp.where(face_even, face - 1, face + 1) + nface, nface)
            return jnp.where(s == face, 0, jnp.where(s == inner, 1, jnp.where(s == outer, 2, 3)))

        place = iota((width, 1), 0)
        place = jnp.where(flip == 1, width - 1 - place, place)
        column = place - d + cols
        step = jnp.where(column >= 2 * cols, 2, jnp.where(column >= cols, 1, 0))
        inside = column - step * cols
        index = jnp.where(
            step == 0,
            source_index(sector - 1),
            jnp.where(step == 1, source_index(sector), source_index(sector + 1)),
        )
        wanted = index * cols + inside
        pick = jnp.where(iota((width, nface * cols), 1) == wanted, 1.0, 0.0).astype(BF16)
        for r in range(d):
            source = jnp.concatenate(
                [
                    strip[own + r, :, ch : 2 * ch],
                    ra_ref[d + r],
                    rb_ref[d + r],
                    wb_ref[r, d : d + cols, :],
                ],
                axis=0,
            )
            wide[which, d - 1 - r] = jnp.dot(pick, source, preferred_element_type=F32).astype(BF16)

    for side, at in ((0, 0), (1, rows + d)):
        for r in range(d):
            for e in range(3):
                strip[at + r, :, e * ch : (e + 1) * ch] = wide[side, r, e * d : e * d + cols, :]

    per = cols // d
    group = 8 // d

    def build(i, p):
        at = pl.multiple_of(i * 8, 8)
        a = ra_ref[p, pl.ds(at, 8), :].astype(F32)
        b = rb_ref[p, pl.ds(at, 8), :].astype(F32)
        west = jnp.where(face_even, b, a).astype(BF16)
        east = jnp.where(face_even, a, b).astype(BF16)
        for k in range(group):
            row = p * per + i * group + k + d
            v = strip[row, :, ch : 2 * ch]
            strip[row, d:, :ch] = v[: cols - d]
            strip[row, :d, :ch] = west[k * d : (k + 1) * d]
            strip[row, : cols - d, 2 * ch :] = v[d:]
            strip[row, cols - d :, 2 * ch :] = east[k * d : (k + 1) * d]
        return p

    def build_plane(p, carry):
        lax.fori_loop(0, per // group, build, p, unroll=2)
        return carry

    lax.fori_loop(0, d, build_plane, 0)
    if has_residual:
        load_fields.wait()

    bias = bias_ref[...]
    bias2 = jnp.concatenate([bias, bias], axis=1)
    m = d * cols
    step_rows = groups * 2 * d
    blocks = rows // step_rows

    def product(i):
        base = i * step_rows
        parts = []
        for a in range(4):
            of_a = [
                strip[pl.ds(base + g * 2 * d + a * d, d)].reshape(m, 3 * ch) for g in range(groups)
            ]
            parts.append(jnp.concatenate(of_a, axis=0))
        return jnp.dot(
            jnp.concatenate(parts, axis=1), weights[...], preferred_element_type=F32
        )

    def send(i):
        at = pl.ds(i * step_rows, step_rows)
        return pltpu.make_async_copy(result.at[at], out_ref.at[at], out_sems.at[i])

    def finish(i):
        y = gelu(acc[...] + bias2)
        for g in range(groups):
            for half in range(2):
                at = i * step_rows + g * 2 * d + half * d
                piece = y[g * m : (g + 1) * m, half * ch : (half + 1) * ch].reshape(d, cols, ch)
                if has_residual:
                    piece = piece + fields[pl.ds(at, d)].astype(F32)
                result[pl.ds(at, d)] = piece.astype(result.dtype)

    acc[...] = product(0)

    def block(i, carry):
        finish(i - 1)
        acc[...] = product(i)
        send(i - 1).start()
        return carry

    lax.fori_loop(1, blocks, block, 0)
    finish(blocks - 1)
    send(blocks - 1).start()
    for i in range(blocks):
        send(i).wait()


def conv(grid, sides, wide, neighbor, reversal, taps, bias, d, groups, fields, out_dtype, name):
    rows, cols, ch = grid.shape
    operands = [neighbor, reversal, grid, *sides, *wide, taps, bias.reshape(1, ch)]
    smem = full_spec(pltpu.SMEM)
    in_specs = [smem, smem, full_spec(pl.ANY)] + [full_spec()] * 6
    scratch = [
        VMEM((rows + 2 * d, cols, 3 * ch), BF16),
        VMEM((12 * ch, 2 * ch), BF16),
        VMEM((2, d, cols + 2 * d, ch), BF16),
        VMEM((groups * d * cols, 2 * ch), F32),
        VMEM((rows, cols, ch), out_dtype),
        pltpu.SemaphoreType.DMA((2,)),
        pltpu.SemaphoreType.DMA((rows // (groups * 2 * d),)),
    ]
    if fields is not None:
        operands.append(fields)
        in_specs.append(full_spec(pl.ANY))
        scratch.append(VMEM(fields.shape, BF16))
    return pl.pallas_call(
        functools.partial(conv_kernel, d, groups, fields is not None),
        out_shape=jax.ShapeDtypeStruct((rows, cols, ch), out_dtype),
        in_specs=in_specs,
        out_specs=full_spec(pl.ANY),
        scratch_shapes=scratch,
        cost_estimate=pl.CostEstimate(
            flops=2 * 12 * rows * cols * ch * ch, bytes_accessed=9_000_000, transcendentals=0
        ),
        name=name,
    )(*operands)


def scatter_kernel(
    d,
    recv_hbm,
    weight_ref,
    first_ref,
    mixed_ref,
    a_ref,
    b_ref,
    recv,
    acc,
    extra,
    enc,
    mixed,
    cells_v,
    cells_s,
    sems,
    out_sems,
):
    load = pltpu.make_async_copy(first_ref, acc, sems.at[0])
    load_recv = pltpu.make_async_copy(recv_hbm, recv, sems.at[1])
    load_recv.start()
    load.start()
    side, _, ch = mixed.shape
    sources = recv.shape[0]
    _, _, face_even, tile_even = parities()
    load_recv.wait()
    for g in range(sources // 8):
        meta = jnp.sum(recv[g * 8 : (g + 1) * 8, CAP:, :].astype(F32), axis=0)
        cells_v[g : g + 1, :] = (meta[0:1, :] * side + meta[1:2, :]).astype(I32)
    copy = pltpu.make_async_copy(cells_v, cells_s, sems.at[2])
    copy.start()
    for g in range(sources // 8):
        rows = recv[g * 8 : (g + 1) * 8, :CAP, :].reshape(8 * CAP, recv.shape[2])
        enc[g * 128 : (g + 1) * 128, :] = jnp.dot(
            rows, weight_ref[...], preferred_element_type=F32
        )

    def clear(r, carry):
        extra[pl.ds(r * side, side), :] = jnp.zeros((side, ch), F32)
        return carry

    lax.fori_loop(0, side, clear, 0, unroll=4)
    copy.wait()
    load.wait()

    def add_rows(g, carry):
        for j in range(0, 128, 2):
            for k, target in ((0, acc), (1, extra)):
                c = cells_s[g, j + k]
                target[pl.ds(c, 1), :] += enc[pl.ds(g * 128 + j + k, 1), :]
        return carry

    lax.fori_loop(0, sources // 8, add_rows, 0)

    per = side // d
    group = 8 // d

    def send(p):
        at = pl.ds(p * per, per)
        return pltpu.make_async_copy(mixed.at[at], mixed_ref.at[at], out_sems.at[p])

    def plane(p, carry):
        def rows_of(i, inner):
            west = []
            east = []
            for k in range(group):
                row = p * per + i * group + k
                at = pl.ds(pl.multiple_of(row * side, side), side)
                v = acc[at, :] + extra[at, :]
                mixed[row] = v.astype(BF16)
                west.append(v[:d])
                east.append(v[side - d :])
            west = jnp.concatenate(west, axis=0)
            east = jnp.concatenate(east, axis=0)
            at = pl.ds(pl.multiple_of(i * 8, 8), 8)
            a_ref[p, at, :] = jnp.where(face_even, east, west).astype(BF16)
            b_ref[p, at, :] = jnp.where(face_even, west, east).astype(BF16)
            return inner

        lax.fori_loop(0, per // group, rows_of, 0, unroll=2)
        send(p).start()
        return carry

    lax.fori_loop(0, d, plane, 0)
    start = jnp.where(tile_even, 0, side - d)
    for r in range(d):
        row = mixed[start + r]
        a_ref[d + r] = row
        b_ref[d + r] = row
    for p in range(d):
        send(p).wait()


def scatter(recv, weight, first, d):
    side, cols, ch = first.shape
    sources, height, features = recv.shape
    flat = first.reshape(side * cols, ch)
    out = jax.ShapeDtypeStruct((2 * d, cols, ch), BF16)
    return pl.pallas_call(
        functools.partial(scatter_kernel, d),
        out_shape=(jax.ShapeDtypeStruct((side, cols, ch), BF16), out, out),
        in_specs=[full_spec(pl.ANY), full_spec(), full_spec(pl.ANY)],
        out_specs=(full_spec(pl.ANY), full_spec(), full_spec()),
        scratch_shapes=[
            VMEM(recv.shape, BF16),
            VMEM(flat.shape, F32),
            VMEM(flat.shape, F32),
            VMEM((sources * CAP, ch), F32),
            VMEM((side, cols, ch), BF16),
            VMEM((sources // 8, 128), I32),
            pltpu.SMEM((sources // 8, 128), I32),
            pltpu.SemaphoreType.DMA((3,)),
            pltpu.SemaphoreType.DMA((d,)),
        ],
        cost_estimate=pl.CostEstimate(
            flops=200_000_000, bytes_accessed=12_000_000, transcendentals=0
        ),
        name="scatter",
    )(recv, weight, flat)


def local(
    fields,
    first_kernel_taps,
    first_conv_bias,
    second_kernel_taps,
    second_conv_bias,
    obs_weight,
    obs_values,
    obs_owner,
    obs_cells,
    polar_neighbor_sector,
    polar_link_reversal,
):
    side = fields.shape[0]
    dests = lax.axis_size("face") * lax.axis_size("tile")
    d = FIRST_DILATION
    sides = swap_faces(edges(fields, d))
    send = pack(obs_owner, obs_cells, obs_values, dests, side)
    recv = lax.all_to_all(send, ("face", "tile"), split_axis=0, concat_axis=0, tiled=True)
    wide = swap_tiles(widen(fields, sides, d))
    first = conv(
        fields, sides, wide, polar_neighbor_sector, polar_link_reversal,
        first_kernel_taps, first_conv_bias, d, 4, None, F32, "conv_first",
    )
    d = SECOND_DILATION
    mixed, side_a, side_b = scatter(recv, obs_weight, first, d)
    sides = swap_faces((side_a, side_b))
    wide = swap_tiles(widen(mixed, sides, d))
    return conv(
        mixed, sides, wide, polar_neighbor_sector, polar_link_reversal,
        second_kernel_taps, second_conv_bias, d, 2, fields, BF16, "conv_second",
    )


def solution(mesh):
    in_specs = (
        P("tile", "face", None),
        P(),
        P(),
        P(),
        P(),
        P(),
        P(("face", "tile"), None),
        P(("face", "tile"), None),
        P(("face", "tile")),
        P(),
        P(),
    )
    out_specs = P("tile", "face", None)
    return jax.shard_map(local, mesh=mesh, in_specs=in_specs, out_specs=out_specs, check_vma=False)
```

time: 106 us -> 91.6 us (0.86)
  starting transfers between devices: 40.4 us -> 20.9 us
  waiting for transfers between devices: 13.1 us -> 22.9 us
  other arithmetic: 1.92 us -> 0 us
  Pallas kernels: 43.7 us -> 42.4 us
    ppermute x14 -> x8, starting transfers between devices: 30.2 us -> 9.7 us  [the longest x2 3.94 us: swap_faces(): lax.ppermute(sides[1], 'face', outer)]
    ppermute x14 -> x8, waiting for transfers between devices: 13.1 us -> 22.9 us  [the longest x2 10.2 us: swap_faces(): lax.ppermute(sides[0], 'face', inner)]
    pallas_call x2, Pallas kernels: 25.1 us -> 20.7 us  [conv(): pl.pallas_call(functools.partial(conv_kernel, d, groups, fields is not No...]
    pallas_call x1 -> x4, Pallas kernels: 14.9 us -> 18 us  [the longest x1 11 us: scatter(): pl.pallas_call(functools.partial(scatter_kernel, d), out_shape=(jax.Shape...]
    slice x6 -> x0, local copies, waits for them, and re-layouts: 2.27 us -> none  [the longest x2 2.24 us: exchange(): grid[:, :d]]
    select_n x2 -> x0, other arithmetic: 1.8 us -> none  [exchange(): edge = jnp.where(tile == 0, grid[:d], grid[rows - d:])]
    unnamed x40 -> x24, local copies, waits for them, and re-layouts: 3.49 us -> 4.82 us
  transfers between devices with their start and end apart: 15 -> 9, of which waited for: 6 -> 7; matrix products, arithmetic and copies ran while one was open for 3% -> 1% of each run, Pallas kernels for 15% -> 16%
where the time goes in v1:
time: 91.6 us; the launch traced here: 91.1 us
  Pallas kernels  42.4 us (46%)
  waiting for transfers between devices  22.9 us (25%)
  starting transfers between devices  20.9 us (23%)
  local copies, waits for them, and re-layouts  4.82 us (5%)
    pallas_call x2, Pallas kernels, conv(): pl.pallas_call(functools.partial(conv_kernel, d, groups, fields is not No...  20.7 us
    all_to_all x1, starting transfers between devices, local(): lax.all_to_all(send, ('face', 'tile'), split_axis=0, concat_axis=0, tiled...  11.2 us
    pallas_call x1, Pallas kernels, scatter(): pl.pallas_call(functools.partial(scatter_kernel, d), out_shape=(jax.Shape...  11 us
    ppermute x2, waiting for transfers between devices, swap_faces(): lax.ppermute(sides[0], 'face', inner)  10.2 us
    ppermute x2, waiting for transfers between devices, swap_tiles(): lax.ppermute(wide[1], ('face', 'tile'), outer)  7.09 us
    pallas_call x2, Pallas kernels, widen(): pl.pallas_call(functools.partial(widen_kernel, d), out_shape=(wide, wide)...  5.16 us
    unnamed x24, local copies, waits for them, and re-layouts  4.82 us
    ppermute x2, waiting for transfers between devices, swap_faces(): lax.ppermute(sides[1], 'face', outer)  4.49 us
  transfers between devices with their start and end apart: 9, of which 7 were waited for; matrix products, arithmetic and copies ran while one was open for 1% of the time, Pallas kernels for 16%

profile of v1, /device:TPU:0, one launch (start us, length us, event | category | flops | bytes accessed | tf_op | source)
XLA Modules:
  0.0 91.1 jit_solution(1596338440180682366)
XLA Ops:
  0.0 3.7 %pack.1 = bf16[128,24,128]{2,1,0:T(8,128)(2,1)} custom-call(s32[1,1024]{1,0:T(1,128)} %bitcast.6, s32[1,1024]{1,0:T(1,128)} %bitcast.7, bf16[1024,128]{1,0:T(8,128)(2,1)} %vals_ref.1), custom_call_target="tpu_custom_call" | custom-call | flops 536870912 | bytes 2000000 | tf_op jit(solution)/shard_map/pack/pallas_call | solution.py:80
  3.7 11.2 %all-to-all-start = ((bf16[128,24,128]{2,1,0:T(8,128)(2,1)}), bf16[128,24,128]{2,1,0:T(8,128)(2,1)S(1)}, u32[]{:S(2)}, u32[]{:S(2)}) async-start(bf16[128,24,128]{2,1,0:T(8,128)(2,1)} %pack.1), calls=%async_computation | async-start | bytes 1572864 | tf_op jit(solution)/shard_map/all_to_all | solution.py:554
  14.9 1.8 %edges.1 = (bf16[4,96,128]{2,1,0:T(8,128)(2,1)}, bf16[4,96,128]{2,1,0:T(8,128)(2,1)}) custom-call(bf16[96,96,128]{2,1,0:T(8,128)(2,1)} %rest_0_.1), custom_call_target="tpu_custom_call" | custom-call | flops 1000000 | bytes 800000 | tf_op jit(solution)/shard_map/edges/pallas_call | solution.py:130
  16.8 1.2 %collective-permute-start = (bf16[4,96,128]{2,1,0:T(8,128)(2,1)}, bf16[4,96,128]{2,1,0:T(8,128)(2,1)S(1)}, u32[]{:S(2)}, u32[]{:S(2)}) collective-permute-start(bf16[4,96,128]{2,1,0:T(8,128)(2,1)} %get-tuple-element.14), channel_id=1, source_target_pairs={{0,32},{32,0},{64,96},{96,64},{1,33},{33,1},{65,97},{97,65},{2,34}... | collective-permute-start | bytes 294920 | tf_op jit(solution)/shard_map/ppermute | solution.py:196
  17.9 2.3 %collective-permute-start.1 = (bf16[4,96,128]{2,1,0:T(8,128)(2,1)}, bf16[4,96,128]{2,1,0:T(8,128)(2,1)S(1)}, u32[]{:S(2)}, u32[]{:S(2)}) collective-permute-start(bf16[4,96,128]{2,1,0:T(8,128)(2,1)} %get-tuple-element.15), channel_id=1, source_target_pairs={{0,96},{32,64},{64,32},{96,0},{1,97},{33,65},{65,33},{97,1},{2,98}... | collective-permute-start | bytes 294920 | tf_op jit(solution)/shard_map/ppermute | solution.py:196
  20.3 7.4 %collective-permute-done.ra_ref = bf16[4,96,128]{2,1,0:T(8,128)(2,1)S(1)} collective-permute-done((bf16[4,96,128]{2,1,0:T(8,128)(2,1)}, bf16[4,96,128]{2,1,0:T(8,128)(2,1)S(1)}, u32[]{:S(2)}, u32[]{:S(2)}) %collective-permute-start) | collective-permute-done | bytes 98336 | tf_op jit(solution)/shard_map/ppermute | solution.py:196
  27.7 1.8 %collective-permute-done.1.rb_ref = bf16[4,96,128]{2,1,0:T(8,128)(2,1)S(1)} collective-permute-done((bf16[4,96,128]{2,1,0:T(8,128)(2,1)}, bf16[4,96,128]{2,1,0:T(8,128)(2,1)S(1)}, u32[]{:S(2)}, u32[]{:S(2)}) %collective-permute-start.1) | collective-permute-done | bytes 98336 | tf_op jit(solution)/shard_map/ppermute | solution.py:196
  29.5 0.7 copy-done.4
  30.2 2.4 %widen.2 = (bf16[2,100,128]{2,1,0:T(8,128)(2,1)}, bf16[2,100,128]{2,1,0:T(8,128)(2,1)}) custom-call(bf16[96,96,128]{2,1,0:T(8,128)(2,1)} %rest_0_.1, bf16[4,96,128]{2,1,0:T(8,128)(2,1)} %copy-done.3, bf16[4,96,128]{2,1,0:T(8,128)(2,1)} %copy-done.4), custom_call_target="tpu_custom_call" | custom-call | flops 1000000 | bytes 800000 | tf_op jit(solution)/shard_map/widen/pallas_call | solution.py:177
  32.7 2.5 %collective-permute-start.3 = (bf16[2,100,128]{2,1,0:T(8,128)(2,1)}, bf16[2,100,128]{2,1,0:T(8,128)(2,1)S(1)}, u32[]{:S(2)}, u32[]{:S(2)}) collective-permute-start(bf16[2,100,128]{2,1,0:T(8,128)(2,1)} %get-tuple-element.17), channel_id=1, source_target_pairs={{0,64},{1,2},{2,1},{3,4},{4,3},{5,6},{6,5},{7,8},{8,7},{9,10},{10,... | collective-permute-start | bytes 153608 | tf_op jit(solution)/shard_map/ppermute | solution.py:211
  35.8 0.7 copy.15.reversal_ref
  36.5 2.1 %collective-permute-done.3.wb_ref = bf16[2,100,128]{2,1,0:T(8,128)(2,1)S(1)} collective-permute-done((bf16[2,100,128]{2,1,0:T(8,128)(2,1)}, bf16[2,100,128]{2,1,0:T(8,128)(2,1)S(1)}, u32[]{:S(2)}, u32[]{:S(2)}) %collective-permute-start.3) | collective-permute-done | bytes 51232 | tf_op jit(solution)/shard_map/ppermute | solution.py:211
  39.2 10.3 %conv_first.1 = f32[96,96,128]{2,1,0:T(8,128)} custom-call(s32[4,2]{1,0:T(4,128)} %copy.14.neighbor_ref, s32[4,2]{1,0:T(4,128)} %copy.15.reversal_ref, bf16[96,96,128]{2,1,0:T(8,128)(2,1)} %rest_0_.1, bf16[4,96,128]{2,1,0:T(8,128)(2,1)} %copy-done.3, bf16[4,96,128]{2,1,0:T(8,128)(2,1)} %copy-done.4, bf16[2,100,128]{2,1,0:T(8,128)(2,1)} %copy-done.9, ...), custom_call_target="tpu_custom_call" | custom-call | flops 3623878656 | bytes 9000000 | tf_op jit(solution)/shard_map/conv_first/pallas_call | solution.py:402
  49.6 0.9 copy-done
  50.4 11.0 %scatter.1 = (bf16[96,96,128]{2,1,0:T(8,128)(2,1)}, bf16[8,96,128]{2,1,0:T(8,128)(2,1)}, bf16[8,96,128]{2,1,0:T(8,128)(2,1)}) custom-call(bf16[128,24,128]{2,1,0:T(8,128)(2,1)} %copy-done, bf16[128,128]{1,0:T(8,128)(2,1)} %weight_ref.1, f32[9216,128]{1,0:T(8,128)} %bitcast.5), custom_call_target="tpu_custom_call" | custom-call | flops 200000000 | bytes 12000000 | tf_op jit(solution)/shard_map/scatter/pallas_call | solution.py:513
  61.4 1.6 %collective-permute-start.4 = (bf16[8,96,128]{2,1,0:T(8,128)(2,1)}, bf16[8,96,128]{2,1,0:T(8,128)(2,1)S(1)}, u32[]{:S(2)}, u32[]{:S(2)}) collective-permute-start(bf16[8,96,128]{2,1,0:T(8,128)(2,1)} %get-tuple-element.19), channel_id=1, source_target_pairs={{0,32},{32,0},{64,96},{96,64},{1,33},{33,1},{65,97},{97,65},{2,34}... | collective-permute-start | bytes 589832 | tf_op jit(solution)/shard_map/ppermute | solution.py:196
  63.0 1.6 %collective-permute-start.5 = (bf16[8,96,128]{2,1,0:T(8,128)(2,1)}, bf16[8,96,128]{2,1,0:T(8,128)(2,1)S(1)}, u32[]{:S(2)}, u32[]{:S(2)}) collective-permute-start(bf16[8,96,128]{2,1,0:T(8,128)(2,1)} %get-tuple-element.20), channel_id=1, source_target_pairs={{0,96},{32,64},{64,32},{96,0},{1,97},{33,65},{65,33},{97,1},{2,98}... | collective-permute-start | bytes 589832 | tf_op jit(solution)/shard_map/ppermute | solution.py:196
  64.6 2.8 %collective-permute-done.4.ra_ref = bf16[8,96,128]{2,1,0:T(8,128)(2,1)S(1)} collective-permute-done((bf16[8,96,128]{2,1,0:T(8,128)(2,1)}, bf16[8,96,128]{2,1,0:T(8,128)(2,1)S(1)}, u32[]{:S(2)}, u32[]{:S(2)}) %collective-permute-start.4) | collective-permute-done | bytes 196640 | tf_op jit(solution)/shard_map/ppermute | solution.py:196
  67.4 2.7 %collective-permute-done.5.rb_ref = bf16[8,96,128]{2,1,0:T(8,128)(2,1)S(1)} collective-permute-done((bf16[8,96,128]{2,1,0:T(8,128)(2,1)}, bf16[8,96,128]{2,1,0:T(8,128)(2,1)S(1)}, u32[]{:S(2)}, u32[]{:S(2)}) %collective-permute-start.5) | collective-permute-done | bytes 196640 | tf_op jit(solution)/shard_map/ppermute | solution.py:196
  70.1 0.7 copy-done.2
  70.8 2.7 %widen.3 = (bf16[4,104,128]{2,1,0:T(8,128)(2,1)}, bf16[4,104,128]{2,1,0:T(8,128)(2,1)}) custom-call(bf16[96,96,128]{2,1,0:T(8,128)(2,1)} %get-tuple-element.18.grid_ref, bf16[8,96,128]{2,1,0:T(8,128)(2,1)} %copy-done.1, bf16[8,96,128]{2,1,0:T(8,128)(2,1)} %copy-done.2), custom_call_target="tpu_custom_call" | custom-call | flops 1000000 | bytes 800000 | tf_op jit(solution)/shard_map/widen/pallas_call | solution.py:177
  74.0 1.1 %collective-permute-done.6.wa_ref = bf16[4,104,128]{2,1,0:T(8,128)(2,1)S(1)} collective-permute-done((bf16[4,104,128]{2,1,0:T(8,128)(2,1)}, bf16[4,104,128]{2,1,0:T(8,128)(2,1)S(1)}, u32[]{:S(2)}, u32[]{:S(2)}) %collective-permute-start.6) | collective-permute-done | bytes 106528 | tf_op jit(solution)/shard_map/ppermute | solution.py:211
  75.1 5.0 %collective-permute-done.7.wb_ref = bf16[4,104,128]{2,1,0:T(8,128)(2,1)S(1)} collective-permute-done((bf16[4,104,128]{2,1,0:T(8,128)(2,1)}, bf16[4,104,128]{2,1,0:T(8,128)(2,1)S(1)}, u32[]{:S(2)}, u32[]{:S(2)}) %collective-permute-start.7) | collective-permute-done | bytes 106528 | tf_op jit(solution)/shard_map/ppermute | solution.py:211
  80.7 10.4 %conv_second.1 = bf16[96,96,128]{2,1,0:T(8,128)(2,1)} custom-call(s32[4,2]{1,0:T(4,128)} %copy.14.neighbor_ref, s32[4,2]{1,0:T(4,128)} %copy.15.reversal_ref, bf16[96,96,128]{2,1,0:T(8,128)(2,1)} %get-tuple-element.18.grid_ref, bf16[8,96,128]{2,1,0:T(8,128)(2,1)} %copy-done.1, bf16[8,96,128]{2,1,0:T(8,128)(2,1)} %copy-done.2, ...), custom_call_target="tpu_custom_call" | custom-call | flops 3623878656 | bytes 9000000 | tf_op jit(solution)/shard_map/conv_second/pallas_call | solution.py:402
  (25 shorter events, 2.5 us)
Async XLA Ops:
  3.7 45.8 %all-to-all-start = ((bf16[128,24,128]{2,1,0:T(8,128)(2,1)}), bf16[128,24,128]{2,1,0:T(8,128)(2,1)S(1)}, u32[]{:S(2)}, u32[]{:S(2)}) async-start(bf16[128,24,128]{2,1,0:T(8,128)(2,1)} %pack.1), calls=%async_computation | async-start | bytes 1572864 | tf_op jit(solution)/shard_map/all_to_all | solution.py:554
  14.9 20.3 %copy-start.5 = (s32[4,2]{0,1:T(2,128)S(1)}, s32[4,2]{0,1:T(2,128)}, u32[]{:S(2)}) copy-start(s32[4,2]{0,1:T(2,128)} %param.20) | copy-start | bytes 100
  14.9 20.9 %copy-start.6 = (s32[4,2]{0,1:T(2,128)S(1)}, s32[4,2]{0,1:T(2,128)}, u32[]{:S(2)}) copy-start(s32[4,2]{0,1:T(2,128)} %param.21) | copy-start | bytes 100
  16.8 10.9 %collective-permute-start = (bf16[4,96,128]{2,1,0:T(8,128)(2,1)}, bf16[4,96,128]{2,1,0:T(8,128)(2,1)S(1)}, u32[]{:S(2)}, u32[]{:S(2)}) collective-permute-start(bf16[4,96,128]{2,1,0:T(8,128)(2,1)} %get-tuple-element.14), channel_id=1, source_target_pairs={{0,32},{32,0},{64,96},{96,64},{1,33},{33,1},{65,97},{97,65},{2,34}... | collective-permute-start | bytes 294920 | tf_op jit(solution)/shard_map/ppermute | solution.py:196
  17.9 11.6 %collective-permute-start.1 = (bf16[4,96,128]{2,1,0:T(8,128)(2,1)}, bf16[4,96,128]{2,1,0:T(8,128)(2,1)S(1)}, u32[]{:S(2)}, u32[]{:S(2)}) collective-permute-start(bf16[4,96,128]{2,1,0:T(8,128)(2,1)} %get-tuple-element.15), channel_id=1, source_target_pairs={{0,96},{32,64},{64,32},{96,0},{1,97},{33,65},{65,33},{97,1},{2,98}... | collective-permute-start | bytes 294920 | tf_op jit(solution)/shard_map/ppermute | solution.py:196
  27.7 1.8 %copy-start.3 = (bf16[4,96,128]{2,1,0:T(8,128)(2,1)}, bf16[4,96,128]{2,1,0:T(8,128)(2,1)S(1)}, u32[]{:S(2)}) copy-start(bf16[4,96,128]{2,1,0:T(8,128)(2,1)S(1)} %collective-permute-done.ra_ref) | copy-start | bytes 294916
  29.5 0.7 copy-start.4
  32.6 3.9 %collective-permute-start.2 = (bf16[2,100,128]{2,1,0:T(8,128)(2,1)}, bf16[2,100,128]{2,1,0:T(8,128)(2,1)S(1)}, u32[]{:S(2)}, u32[]{:S(2)}) collective-permute-start(bf16[2,100,128]{2,1,0:T(8,128)(2,1)} %get-tuple-element.16), channel_id=1, source_target_pairs={{0,1},{1,0},{2,3},{3,2},{4,5},{5,4},{6,7},{7,6},{8,9},{9,8},{10,11... | collective-permute-start | bytes 153608 | tf_op jit(solution)/shard_map/ppermute | solution.py:211
  32.7 5.9 %collective-permute-start.3 = (bf16[2,100,128]{2,1,0:T(8,128)(2,1)}, bf16[2,100,128]{2,1,0:T(8,128)(2,1)S(1)}, u32[]{:S(2)}, u32[]{:S(2)}) collective-permute-start(bf16[2,100,128]{2,1,0:T(8,128)(2,1)} %get-tuple-element.17), channel_id=1, source_target_pairs={{0,64},{1,2},{2,1},{3,4},{4,3},{5,6},{6,5},{7,8},{8,7},{9,10},{10,... | collective-permute-start | bytes 153608 | tf_op jit(solution)/shard_map/ppermute | solution.py:211
  36.5 2.1 %copy-start.9 = (bf16[2,100,128]{2,1,0:T(8,128)(2,1)}, bf16[2,100,128]{2,1,0:T(8,128)(2,1)S(1)}, u32[]{:S(2)}) copy-start(bf16[2,100,128]{2,1,0:T(8,128)(2,1)S(1)} %collective-permute-done.2.wa_ref) | copy-start | bytes 153604
  38.6 0.6 copy-start.10
  49.6 0.9 copy-start
  61.4 6.0 %collective-permute-start.4 = (bf16[8,96,128]{2,1,0:T(8,128)(2,1)}, bf16[8,96,128]{2,1,0:T(8,128)(2,1)S(1)}, u32[]{:S(2)}, u32[]{:S(2)}) collective-permute-start(bf16[8,96,128]{2,1,0:T(8,128)(2,1)} %get-tuple-element.19), channel_id=1, source_target_pairs={{0,32},{32,0},{64,96},{96,64},{1,33},{33,1},{65,97},{97,65},{2,34}... | collective-permute-start | bytes 589832 | tf_op jit(solution)/shard_map/ppermute | solution.py:196
  63.0 7.1 %collective-permute-start.5 = (bf16[8,96,128]{2,1,0:T(8,128)(2,1)}, bf16[8,96,128]{2,1,0:T(8,128)(2,1)S(1)}, u32[]{:S(2)}, u32[]{:S(2)}) collective-permute-start(bf16[8,96,128]{2,1,0:T(8,128)(2,1)} %get-tuple-element.20), channel_id=1, source_target_pairs={{0,96},{32,64},{64,32},{96,0},{1,97},{33,65},{65,33},{97,1},{2,98}... | collective-permute-start | bytes 589832 | tf_op jit(solution)/shard_map/ppermute | solution.py:196
  67.4 2.7 %copy-start.1 = (bf16[8,96,128]{2,1,0:T(8,128)(2,1)}, bf16[8,96,128]{2,1,0:T(8,128)(2,1)S(1)}, u32[]{:S(2)}) copy-start(bf16[8,96,128]{2,1,0:T(8,128)(2,1)S(1)} %collective-permute-done.4.ra_ref) | copy-start | bytes 589828
  70.1 0.7 copy-start.2
  73.5 1.6 %collective-permute-start.6 = (bf16[4,104,128]{2,1,0:T(8,128)(2,1)}, bf16[4,104,128]{2,1,0:T(8,128)(2,1)S(1)}, u32[]{:S(2)}, u32[]{:S(2)}) collective-permute-start(bf16[4,104,128]{2,1,0:T(8,128)(2,1)} %get-tuple-element.21), channel_id=1, source_target_pairs={{0,1},{1,0},{2,3},{3,2},{4,5},{5,4},{6,7},{7,6},{8,9},{9,8},{10,11... | collective-permute-start | bytes 319496 | tf_op jit(solution)/shard_map/ppermute | solution.py:211
  73.6 6.5 %collective-permute-start.7 = (bf16[4,104,128]{2,1,0:T(8,128)(2,1)}, bf16[4,104,128]{2,1,0:T(8,128)(2,1)S(1)}, u32[]{:S(2)}, u32[]{:S(2)}) collective-permute-start(bf16[4,104,128]{2,1,0:T(8,128)(2,1)} %get-tuple-element.22), channel_id=1, source_target_pairs={{0,64},{1,2},{2,1},{3,4},{4,3},{5,6},{6,5},{7,8},{8,7},{9,10},{10,... | collective-permute-start | bytes 319496 | tf_op jit(solution)/shard_map/ppermute | solution.py:211
  75.1 5.0 %copy-start.7 = (bf16[4,104,128]{2,1,0:T(8,128)(2,1)}, bf16[4,104,128]{2,1,0:T(8,128)(2,1)S(1)}, u32[]{:S(2)}) copy-start(bf16[4,104,128]{2,1,0:T(8,128)(2,1)S(1)} %collective-permute-done.6.wa_ref) | copy-start | bytes 319492
  80.1 0.6 copy-start.8

commit v2 on v1

--- a/solution.py
+++ b/solution.py
@@ -20,6 +20,18 @@
 
 def full_spec(memory_space=None):
     return pl.BlockSpec(memory_space=VMEM if memory_space is None else memory_space)
+
+
+def room(mebibytes):
+    return pltpu.CompilerParams(vmem_limit_bytes=mebibytes << 20)
+
+
+def far(x):
+    return pltpu.with_memory_space_constraint(x, pltpu.HBM)
+
+
+def keep(x):
+    return pltpu.with_memory_space_constraint(x, VMEM)
 
 
 def iota(shape, axis):
@@ -85,6 +97,7 @@
         cost_estimate=pl.CostEstimate(
             flops=2 * dests * CAP * rows * features, bytes_accessed=2_000_000, transcendentals=0
         ),
+        compiler_params=room(16),
         name="pack",
     )(owner.reshape(1, rows), cells.reshape(1, rows), vals)
 
@@ -95,8 +108,8 @@
     return face, tile, lax.rem(face, 2) == 0, lax.rem(tile, 2) == 0
 
 
-def edges_kernel(d, grid_ref, a_ref, b_ref, low, high, sems):
-    rows, cols, ch = grid_ref.shape
+def edges_kernel(d, grid_ref, a_ref, b_ref, ends_ref, low, high, sems):
+    rows, cols, _ = grid_ref.shape
     _, _, face_even, tile_even = parities()
     start = jnp.where(tile_even, 0, rows - d)
     copies = [
@@ -104,6 +117,8 @@
         pltpu.make_async_copy(grid_ref.at[:, pl.ds(cols - 8, 8), :], high, sems.at[1]),
         pltpu.make_async_copy(grid_ref.at[pl.ds(start, d)], a_ref.at[pl.ds(d, d)], sems.at[2]),
         pltpu.make_async_copy(grid_ref.at[pl.ds(start, d)], b_ref.at[pl.ds(d, d)], sems.at[3]),
+        pltpu.make_async_copy(grid_ref.at[pl.ds(0, d)], ends_ref.at[0], sems.at[4]),
+        pltpu.make_async_copy(grid_ref.at[pl.ds(rows - d, d)], ends_ref.at[1], sems.at[5]),
     ]
     for copy in copies:
         copy.start()
@@ -126,33 +141,27 @@
 
 def edges(grid, d):
     rows, cols, ch = grid.shape
-    side = jax.ShapeDtypeStruct((2 * d, cols, ch), BF16)
+    side = VMEM((2 * d, cols, ch), BF16)
     return pl.pallas_call(
         functools.partial(edges_kernel, d),
-        out_shape=(side, side),
+        out_shape=(side, side, VMEM((2, d, cols, ch), BF16)),
         in_specs=[full_spec(pl.ANY)],
-        out_specs=(full_spec(), full_spec()),
+        out_specs=(full_spec(),) * 3,
         scratch_shapes=[
             VMEM((rows, 8, ch), BF16),
             VMEM((rows, 8, ch), BF16),
-            pltpu.SemaphoreType.DMA((4,)),
+            pltpu.SemaphoreType.DMA((6,)),
         ],
         cost_estimate=pl.CostEstimate(flops=1_000_000, bytes_accessed=800_000, transcendentals=0),
+        compiler_params=room(8),
         name="edges",
-    )(grid)
-
-
-def widen_kernel(d, grid_ref, ra_ref, rb_ref, wa_ref, wb_ref, ends, sems):
-    rows, cols, ch = grid_ref.shape
+    )(far(grid))
+
+
+def widen_kernel(d, ends_ref, ra_ref, rb_ref, wa_ref, wb_ref):
+    cols = ends_ref.shape[2]
+    rows = cols
     _, _, face_even, tile_even = parities()
-    copies = [
-        pltpu.make_async_copy(grid_ref.at[pl.ds(at, d)], ends.at[i], sems.at[i])
-        for i, at in enumerate((0, rows - d))
-    ]
-    for copy in copies:
-        copy.start()
-    for copy in copies:
-        copy.wait()
     per = cols // d
     for r in range(d):
         wide = []
@@ -163,7 +172,11 @@
             b = rb_ref[row // per, tile_at : tile_at + 8, :].astype(F32)[at - tile_at : at - tile_at + d]
             wide.append(
                 jnp.concatenate(
-                    [jnp.where(face_even, b, a), ends[i, r].astype(F32), jnp.where(face_even, a, b)],
+                    [
+                        jnp.where(face_even, b, a),
+                        ends_ref[i, r].astype(F32),
+                        jnp.where(face_even, a, b),
+                    ],
                     axis=0,
                 )
             )
@@ -171,18 +184,18 @@
         wb_ref[r] = jnp.where(tile_even, wide[0], wide[1]).astype(BF16)
 
 
-def widen(grid, received, d):
-    rows, cols, ch = grid.shape
-    wide = jax.ShapeDtypeStruct((d, cols + 2 * d, ch), BF16)
+def widen(ends, received, d):
+    _, _, cols, ch = ends.shape
+    wide = VMEM((d, cols + 2 * d, ch), BF16)
     return pl.pallas_call(
         functools.partial(widen_kernel, d),
         out_shape=(wide, wide),
-        in_specs=[full_spec(pl.ANY), full_spec(), full_spec()],
+        in_specs=[full_spec()] * 3,
         out_specs=(full_spec(), full_spec()),
-        scratch_shapes=[VMEM((2, d, cols, ch), BF16), pltpu.SemaphoreType.DMA((2,))],
         cost_estimate=pl.CostEstimate(flops=1_000_000, bytes_accessed=800_000, transcendentals=0),
+        compiler_params=room(8),
         name="widen",
-    )(grid, *received)
+    )(keep(ends), *[keep(x) for x in received])
 
 
 def face_partner(f, nface, odd_up):
@@ -268,8 +281,8 @@
     @pl.when((tile == 0) | (tile == last_tile))
     def _():
         which = jnp.where(tile == 0, 0, 1)
-        sector = neighbor_ref[face, which]
-        flip = reversal_ref[face, which]
+        sector = neighbor_ref[which, face]
+        flip = reversal_ref[which, face]
         own = jnp.where(tile == 0, d, rows)
         width = cols + 2 * d
 
@@ -353,7 +366,8 @@
         )
 
     def send(i):
-        at = pl.ds(i * step_rows, step_rows)
+        unit = step_rows if has_residual else step_rows * cols
+        at = pl.ds(i * unit, unit)
         return pltpu.make_async_copy(result.at[at], out_ref.at[at], out_sems.at[i])
 
     def finish(i):
@@ -361,10 +375,12 @@
         for g in range(groups):
             for half in range(2):
                 at = i * step_rows + g * 2 * d + half * d
-                piece = y[g * m : (g + 1) * m, half * ch : (half + 1) * ch].reshape(d, cols, ch)
+                piece = y[g * m : (g + 1) * m, half * ch : (half + 1) * ch]
                 if has_residual:
-                    piece = piece + fields[pl.ds(at, d)].astype(F32)
-                result[pl.ds(at, d)] = piece.astype(result.dtype)
+                    piece = piece.reshape(d, cols, ch) + fields[pl.ds(at, d)].astype(F32)
+                    result[pl.ds(at, d)] = piece.astype(BF16)
+                else:
+                    result[pl.ds(pl.multiple_of(at * cols, m), m), :] = piece
 
     acc[...] = product(0)
 
@@ -381,9 +397,9 @@
         send(i).wait()
 
 
-def conv(grid, sides, wide, neighbor, reversal, taps, bias, d, groups, fields, out_dtype, name):
+def conv(grid, sides, wide, neighbor, reversal, taps, bias, d, groups, fields, out_dtype):
     rows, cols, ch = grid.shape
-    operands = [neighbor, reversal, grid, *sides, *wide, taps, bias.reshape(1, ch)]
+    operands = [neighbor.T, reversal.T, far(grid) if fields is None else keep(grid), *[keep(x) for x in (*sides, *wide)], taps, bias.reshape(1, ch)]
     smem = full_spec(pltpu.SMEM)
     in_specs = [smem, smem, full_spec(pl.ANY)] + [full_spec()] * 6
     scratch = [
@@ -396,52 +412,51 @@
         pltpu.SemaphoreType.DMA((rows // (groups * 2 * d),)),
     ]
     if fields is not None:
-        operands.append(fields)
+        operands.append(far(fields))
         in_specs.append(full_spec(pl.ANY))
         scratch.append(VMEM(fields.shape, BF16))
+    out = (rows, cols, ch) if fields is not None else (rows * cols, ch)
+    scratch[4] = VMEM(out, out_dtype)
+    out = pltpu.HBM(out, out_dtype)
     return pl.pallas_call(
         functools.partial(conv_kernel, d, groups, fields is not None),
-        out_shape=jax.ShapeDtypeStruct((rows, cols, ch), out_dtype),
+        out_shape=out,
         in_specs=in_specs,
         out_specs=full_spec(pl.ANY),
         scratch_shapes=scratch,
         cost_estimate=pl.CostEstimate(
             flops=2 * 12 * rows * cols * ch * ch, bytes_accessed=9_000_000, transcendentals=0
         ),
-        name=name,
+        compiler_params=room(28),
     )(*operands)
 
 
 def scatter_kernel(
     d,
-    recv_hbm,
+    recv,
     weight_ref,
     first_ref,
-    mixed_ref,
+    mixed,
     a_ref,
     b_ref,
-    recv,
-    acc,
+    ends_ref,
+    first,
+    even,
     extra,
     enc,
-    mixed,
     cells_v,
     cells_s,
     sems,
-    out_sems,
 ):
-    load = pltpu.make_async_copy(first_ref, acc, sems.at[0])
-    load_recv = pltpu.make_async_copy(recv_hbm, recv, sems.at[1])
-    load_recv.start()
+    load = pltpu.make_async_copy(first_ref, first, sems.at[0])
     load.start()
     side, _, ch = mixed.shape
     sources = recv.shape[0]
     _, _, face_even, tile_even = parities()
-    load_recv.wait()
     for g in range(sources // 8):
         meta = jnp.sum(recv[g * 8 : (g + 1) * 8, CAP:, :].astype(F32), axis=0)
         cells_v[g : g + 1, :] = (meta[0:1, :] * side + meta[1:2, :]).astype(I32)
-    copy = pltpu.make_async_copy(cells_v, cells_s, sems.at[2])
+    copy = pltpu.make_async_copy(cells_v, cells_s, sems.at[1])
     copy.start()
     for g in range(sources // 8):
         rows = recv[g * 8 : (g + 1) * 8, :CAP, :].reshape(8 * CAP, recv.shape[2])
@@ -450,28 +465,25 @@
         )
 
     def clear(r, carry):
+        even[pl.ds(r * side, side), :] = jnp.zeros((side, ch), F32)
         extra[pl.ds(r * side, side), :] = jnp.zeros((side, ch), F32)
         return carry
 
     lax.fori_loop(0, side, clear, 0, unroll=4)
     copy.wait()
-    load.wait()
 
     def add_rows(g, carry):
         for j in range(0, 128, 2):
-            for k, target in ((0, acc), (1, extra)):
+            for k, target in ((0, even), (1, extra)):
                 c = cells_s[g, j + k]
                 target[pl.ds(c, 1), :] += enc[pl.ds(g * 128 + j + k, 1), :]
         return carry
 
     lax.fori_loop(0, sources // 8, add_rows, 0)
+    load.wait()
 
     per = side // d
     group = 8 // d
-
-    def send(p):
-        at = pl.ds(p * per, per)
-        return pltpu.make_async_copy(mixed.at[at], mixed_ref.at[at], out_sems.at[p])
 
     def plane(p, carry):
         def rows_of(i, inner):
@@ -480,7 +492,7 @@
             for k in range(group):
                 row = p * per + i * group + k
                 at = pl.ds(pl.multiple_of(row * side, side), side)
-                v = acc[at, :] + extra[at, :]
+                v = first[at, :] + even[at, :] + extra[at, :]
                 mixed[row] = v.astype(BF16)
                 west.append(v[:d])
                 east.append(v[side - d :])
@@ -492,7 +504,6 @@
             return inner
 
         lax.fori_loop(0, per // group, rows_of, 0, unroll=2)
-        send(p).start()
         return carry
 
     lax.fori_loop(0, d, plane, 0)
@@ -501,36 +512,35 @@
         row = mixed[start + r]
         a_ref[d + r] = row
         b_ref[d + r] = row
-    for p in range(d):
-        send(p).wait()
+        ends_ref[0, r] = mixed[r]
+        ends_ref[1, r] = mixed[side - d + r]
 
 
 def scatter(recv, weight, first, d):
-    side, cols, ch = first.shape
-    sources, height, features = recv.shape
-    flat = first.reshape(side * cols, ch)
-    out = jax.ShapeDtypeStruct((2 * d, cols, ch), BF16)
+    cells, ch = first.shape
+    side = cols = round(cells**0.5)
+    sources = recv.shape[0]
+    out = VMEM((2 * d, cols, ch), BF16)
     return pl.pallas_call(
         functools.partial(scatter_kernel, d),
-        out_shape=(jax.ShapeDtypeStruct((side, cols, ch), BF16), out, out),
-        in_specs=[full_spec(pl.ANY), full_spec(), full_spec(pl.ANY)],
-        out_specs=(full_spec(pl.ANY), full_spec(), full_spec()),
+        out_shape=(VMEM((side, cols, ch), BF16), out, out, VMEM((2, d, cols, ch), BF16)),
+        in_specs=[full_spec(), full_spec(), full_spec(pl.ANY)],
+        out_specs=(full_spec(),) * 4,
         scratch_shapes=[
-            VMEM(recv.shape, BF16),
-            VMEM(flat.shape, F32),
-            VMEM(flat.shape, F32),
+            VMEM(first.shape, F32),
+            VMEM(first.shape, F32),
+            VMEM(first.shape, F32),
             VMEM((sources * CAP, ch), F32),
-            VMEM((side, cols, ch), BF16),
             VMEM((sources // 8, 128), I32),
             pltpu.SMEM((sources // 8, 128), I32),
-            pltpu.SemaphoreType.DMA((3,)),
-            pltpu.SemaphoreType.DMA((d,)),
+            pltpu.SemaphoreType.DMA((2,)),
         ],
         cost_estimate=pl.CostEstimate(
             flops=200_000_000, bytes_accessed=12_000_000, transcendentals=0
         ),
+        compiler_params=room(28),
         name="scatter",
-    )(recv, weight, flat)
+    )(keep(recv), weight, far(first))
 
 
 def local(
@@ -549,21 +559,24 @@
     side = fields.shape[0]
     dests = lax.axis_size("face") * lax.axis_size("tile")
     d = FIRST_DILATION
-    sides = swap_faces(edges(fields, d))
+    a, b, ends = edges(fields, d)
+    sides = swap_faces((a, b))
     send = pack(obs_owner, obs_cells, obs_values, dests, side)
+    wide = widen(ends, sides, d)
+    send, wide = lax.optimization_barrier((send, wide))
+    wide = swap_tiles(wide)
     recv = lax.all_to_all(send, ("face", "tile"), split_axis=0, concat_axis=0, tiled=True)
-    wide = swap_tiles(widen(fields, sides, d))
     first = conv(
         fields, sides, wide, polar_neighbor_sector, polar_link_reversal,
-        first_kernel_taps, first_conv_bias, d, 4, None, F32, "conv_first",
+        first_kernel_taps, first_conv_bias, d, 4, None, F32,
     )
     d = SECOND_DILATION
-    mixed, side_a, side_b = scatter(recv, obs_weight, first, d)
-    sides = swap_faces((side_a, side_b))
-    wide = swap_tiles(widen(mixed, sides, d))
+    mixed, a, b, ends = scatter(recv, obs_weight, first, d)
+    sides = swap_faces((a, b))
+    wide = swap_tiles(widen(ends, sides, d))
     return conv(
         mixed, sides, wide, polar_neighbor_sector, polar_link_reversal,
-        second_kernel_taps, second_conv_bias, d, 2, fields, BF16, "conv_second",
+        second_kernel_taps, second_conv_bias, d, 2, fields, BF16,
     )
 
 

time: 91.6 us -> 71.9 us (0.78)
  the two profiles are of different devices: /device:TPU:0 before, /device:TPU:4 now
where the time goes in v2:
time: 71.9 us; the launch traced here: 71.6 us
  Pallas kernels  29.6 us (41%)
  starting transfers between devices  21.8 us (30%)
  waiting for transfers between devices  20 us (28%)
    pallas_call x2, Pallas kernels, conv(): pl.pallas_call(functools.partial(conv_kernel, d, groups, fields is not No...  18.2 us
    ppermute x2, waiting for transfers between devices, swap_tiles(): lax.ppermute(wide[1], ('face', 'tile'), outer)  14.3 us
    all_to_all x1, starting transfers between devices, local(): lax.all_to_all(send, ('face', 'tile'), split_axis=0, concat_axis=0, tiled...  8.99 us
    pallas_call x1, Pallas kernels, scatter(): pl.pallas_call(functools.partial(scatter_kernel, d), out_shape=(VMEM((sid...  7.36 us
    ppermute x2, starting transfers between devices, swap_faces(): lax.ppermute(sides[1], 'face', outer)  4.25 us
    ppermute x2, starting transfers between devices, swap_faces(): lax.ppermute(sides[0], 'face', inner)  4.13 us
    ppermute x2, starting transfers between devices, swap_tiles(): lax.ppermute(wide[1], ('face', 'tile'), outer)  4.12 us
    ppermute x2, waiting for transfers between devices, swap_faces(): lax.ppermute(sides[1], 'face', outer)  3.78 us
  transfers between devices with their start and end apart: 9, of which 5 were waited for; matrix products, arithmetic and copies ran while one was open for 0% of the time, Pallas kernels for 17%

profile of v2, /device:TPU:4, one launch (start us, length us, event | category | flops | bytes accessed | tf_op | source)
XLA Modules:
  0.0 71.6 jit_solution(17431953783309957649)
XLA Ops:
  0.0 1.3 %edges.1 = (bf16[4,96,128]{2,1,0:T(8,128)(2,1)S(1)}, bf16[4,96,128]{2,1,0:T(8,128)(2,1)S(1)}, bf16[2,2,96,128]{3,2,1,0:T(8,128)(2,1)S(1)}) custom-call(bf16[96,96,128]{2,1,0:T(8,128)(2,1)} %rest_0_.1), custom_call_target="tpu_custom_call" | custom-call | flops 1000000 | bytes 800000 | tf_op jit(solution)/shard_map/edges/pallas_call | solution.py:145
  1.3 0.0 copy-start.1
  1.3 0.0 copy-start.8
  1.3 2.0 %collective-permute-start = (bf16[4,96,128]{2,1,0:T(8,128)(2,1)S(1)}, bf16[4,96,128]{2,1,0:T(8,128)(2,1)S(1)}, u32[]{:S(2)}, u32[]{:S(2)}) collective-permute-start(bf16[4,96,128]{2,1,0:T(8,128)(2,1)S(1)} %get-tuple-element.20), channel_id=1, source_target_pairs={{0,32},{32,0},{64,96},{96,64},{1,33},{33,1},{65,97},{97,65},{2,34}... | collective-permute-start | bytes 294920 | tf_op jit(solution)/shard_map/ppermute | solution.py:209
  3.3 2.5 %collective-permute-start.1 = (bf16[4,96,128]{2,1,0:T(8,128)(2,1)S(1)}, bf16[4,96,128]{2,1,0:T(8,128)(2,1)S(1)}, u32[]{:S(2)}, u32[]{:S(2)}) collective-permute-start(bf16[4,96,128]{2,1,0:T(8,128)(2,1)S(1)} %get-tuple-element.21), channel_id=1, source_target_pairs={{0,96},{32,64},{64,32},{96,0},{1,97},{33,65},{65,33},{97,1},{2,98}... | collective-permute-start | bytes 294920 | tf_op jit(solution)/shard_map/ppermute | solution.py:209
  5.8 2.7 %pack.1 = bf16[128,24,128]{2,1,0:T(8,128)(2,1)} custom-call(s32[1,1024]{1,0:T(1,128)S(1)} %bitcast.6, s32[1,1024]{1,0:T(1,128)S(1)} %bitcast.7, bf16[1024,128]{1,0:T(8,128)(2,1)S(1)} %copy-done.3), custom_call_target="tpu_custom_call" | custom-call | flops 536870912 | bytes 2000000 | tf_op jit(solution)/shard_map/pack/pallas_call | solution.py:92
  8.6 0.6 collective-permute-done.1.rb_ref
  9.2 9.0 %all-to-all-start = ((bf16[128,24,128]{2,1,0:T(8,128)(2,1)}), bf16[128,24,128]{2,1,0:T(8,128)(2,1)S(1)}, u32[]{:S(2)}, u32[]{:S(2)}) async-start(bf16[128,24,128]{2,1,0:T(8,128)(2,1)} %pack.1), calls=%async_computation | async-start | bytes 1572864 | tf_op jit(solution)/shard_map/all_to_all | solution.py:568
  18.2 0.2 collective-permute-start.2
  18.4 2.7 %collective-permute-start.3 = (bf16[2,100,128]{2,1,0:T(8,128)(2,1)S(1)}, bf16[2,100,128]{2,1,0:T(8,128)(2,1)S(1)}, u32[]{:S(2)}, u32[]{:S(2)}) collective-permute-start(bf16[2,100,128]{2,1,0:T(8,128)(2,1)S(1)} %get-tuple-element.26), channel_id=1, source_target_pairs={{0,64},{1,2},{2,1},{3,4},{4,3},{5,6},{6,5},{7,8},{8,7},{9,10},{10,... | collective-permute-start | bytes 153608 | tf_op jit(solution)/shard_map/ppermute | solution.py:224
  21.1 9.3 %collective-permute-done.3.wb_ref = bf16[2,100,128]{2,1,0:T(8,128)(2,1)S(1)} collective-permute-done((bf16[2,100,128]{2,1,0:T(8,128)(2,1)S(1)}, bf16[2,100,128]{2,1,0:T(8,128)(2,1)S(1)}, u32[]{:S(2)}, u32[]{:S(2)}) %collective-permute-start.3) | collective-permute-done | bytes 51232 | tf_op jit(solution)/shard_map/ppermute | solution.py:224
  30.5 0.0 copy-start
  30.5 9.5 %shard_map.109.first_ref = f32[9216,128]{1,0:T(8,128)} custom-call(s32[2,4]{1,0:T(2,128)S(1)} %bitcast.8, s32[2,4]{1,0:T(2,128)S(1)} %bitcast.10, bf16[96,96,128]{2,1,0:T(8,128)(2,1)} %rest_0_.1, bf16[4,96,128]{2,1,0:T(8,128)(2,1)S(1)} %collective-permute-done.ra_ref, bf16[4,96,128]{2,1,0:T(8,128)(2,1)S(1)} %collective-permute-done.1.rb_ref, ...), custom_call_target="tpu_custom_call" | custom-call | flops 3623878656 | bytes 9000000 | tf_op jit(solution)/shard_map/pallas_call | solution.py:421
  40.0 0.0 copy-start.2
  40.1 7.4 %scatter.1 = (bf16[96,96,128]{2,1,0:T(8,128)(2,1)S(1)}, bf16[8,96,128]{2,1,0:T(8,128)(2,1)S(1)}, bf16[8,96,128]{2,1,0:T(8,128)(2,1)S(1)}, bf16[2,4,96,128]{3,2,1,0:T(8,128)(2,1)S(1)}) custom-call(bf16[128,24,128]{2,1,0:T(8,128)(2,1)S(1)} %all-to-all-done.recv, bf16[128,128]{1,0:T(8,128)(2,1)S(1)} %copy-done, f32[9216,128]{1,0:T(8,128)} %shard_map.109.first_ref), custom_call_target="tpu_custom_call" | custom-call | flops 200000000 | bytes 12000000 | tf_op jit(solution)/shard_map/scatter/pallas_call | solution.py:524
  47.4 2.1 %collective-permute-start.4 = (bf16[8,96,128]{2,1,0:T(8,128)(2,1)S(1)}, bf16[8,96,128]{2,1,0:T(8,128)(2,1)S(1)}, u32[]{:S(2)}, u32[]{:S(2)}) collective-permute-start(bf16[8,96,128]{2,1,0:T(8,128)(2,1)S(1)} %get-tuple-element.28), channel_id=1, source_target_pairs={{0,32},{32,0},{64,96},{96,64},{1,33},{33,1},{65,97},{97,65},{2,34}... | collective-permute-start | bytes 589832 | tf_op jit(solution)/shard_map/ppermute | solution.py:209
  49.6 1.7 %collective-permute-start.5 = (bf16[8,96,128]{2,1,0:T(8,128)(2,1)S(1)}, bf16[8,96,128]{2,1,0:T(8,128)(2,1)S(1)}, u32[]{:S(2)}, u32[]{:S(2)}) collective-permute-start(bf16[8,96,128]{2,1,0:T(8,128)(2,1)S(1)} %get-tuple-element.29), channel_id=1, source_target_pairs={{0,96},{32,64},{64,32},{96,0},{1,97},{33,65},{65,33},{97,1},{2,98}... | collective-permute-start | bytes 589832 | tf_op jit(solution)/shard_map/ppermute | solution.py:209
  51.3 1.9 %collective-permute-done.4.ra_ref = bf16[8,96,128]{2,1,0:T(8,128)(2,1)S(1)} collective-permute-done((bf16[8,96,128]{2,1,0:T(8,128)(2,1)S(1)}, bf16[8,96,128]{2,1,0:T(8,128)(2,1)S(1)}, u32[]{:S(2)}, u32[]{:S(2)}) %collective-permute-start.4) | collective-permute-done | bytes 196640 | tf_op jit(solution)/shard_map/ppermute | solution.py:209
  53.2 3.2 %collective-permute-done.5.rb_ref = bf16[8,96,128]{2,1,0:T(8,128)(2,1)S(1)} collective-permute-done((bf16[8,96,128]{2,1,0:T(8,128)(2,1)S(1)}, bf16[8,96,128]{2,1,0:T(8,128)(2,1)S(1)}, u32[]{:S(2)}, u32[]{:S(2)}) %collective-permute-start.5) | collective-permute-done | bytes 196640 | tf_op jit(solution)/shard_map/ppermute | solution.py:209
  56.4 0.1 widen.3
  56.5 0.1 collective-permute-start.6
  56.6 1.4 %collective-permute-start.7 = (bf16[4,104,128]{2,1,0:T(8,128)(2,1)S(1)}, bf16[4,104,128]{2,1,0:T(8,128)(2,1)S(1)}, u32[]{:S(2)}, u32[]{:S(2)}) collective-permute-start(bf16[4,104,128]{2,1,0:T(8,128)(2,1)S(1)} %get-tuple-element.32), channel_id=1, source_target_pairs={{0,64},{1,2},{2,1},{3,4},{4,3},{5,6},{6,5},{7,8},{8,7},{9,10},{10,... | collective-permute-start | bytes 319496 | tf_op jit(solution)/shard_map/ppermute | solution.py:224
  58.0 4.9 %collective-permute-done.7.wb_ref = bf16[4,104,128]{2,1,0:T(8,128)(2,1)S(1)} collective-permute-done((bf16[4,104,128]{2,1,0:T(8,128)(2,1)S(1)}, bf16[4,104,128]{2,1,0:T(8,128)(2,1)S(1)}, u32[]{:S(2)}, u32[]{:S(2)}) %collective-permute-start.7) | collective-permute-done | bytes 106528 | tf_op jit(solution)/shard_map/ppermute | solution.py:224
  62.9 8.7 %shard_map.110 = bf16[96,96,128]{2,1,0:T(8,128)(2,1)} custom-call(s32[2,4]{1,0:T(2,128)S(1)} %bitcast.9, s32[2,4]{1,0:T(2,128)S(1)} %bitcast.11, bf16[96,96,128]{2,1,0:T(8,128)(2,1)S(1)} %get-tuple-element.27.grid_ref, bf16[8,96,128]{2,1,0:T(8,128)(2,1)S(1)} %collective-permute-done.4.ra_ref, bf16[8,96,128]{2,1,0:T(8,128)(2,1)S(1)} %collective-permute-done.5.rb_ref, ...), custom_call_target="tpu_custom_call" | custom-call | flops 3623878656 | bytes 9000000 | tf_op jit(solution)/shard_map/pallas_call | solution.py:421
  (21 shorter events, 0.1 us)
Async XLA Ops:
  0.0 5.8 %copy-start.5 = (s32[1024]{0:T(1024)S(1)}, s32[1024]{0:T(1024)}, u32[]{:S(2)}) copy-start(s32[1024]{0:T(1024)} %param.19) | copy-start | bytes 12292
  0.0 5.8 %copy-start.4 = (s32[1024,1]{0,1:T(1,128)S(1)}, s32[1024,1]{0,1:T(1,128)}, u32[]{:S(2)}) copy-start(s32[1024,1]{0,1:T(1,128)} %param.18) | copy-start | bytes 12292
  0.0 5.8 %copy-start.3 = (bf16[1024,128]{1,0:T(8,128)(2,1)S(1)}, bf16[1024,128]{1,0:T(8,128)(2,1)}, u32[]{:S(2)}) copy-start(bf16[1024,128]{1,0:T(8,128)(2,1)} %vals_ref.1) | copy-start | bytes 786436
  1.3 29.2 %copy-start.1 = (bf16[9,128,128]{2,1,0:T(8,128)(2,1)S(1)}, bf16[9,128,128]{2,1,0:T(8,128)(2,1)}, u32[]{:S(2)}) copy-start(bf16[9,128,128]{2,1,0:T(8,128)(2,1)} %taps_ref.2) | copy-start | bytes 884740
  1.3 29.2 %copy-start.6 = (s32[4,2]{0,1:T(2,128)S(1)}, s32[4,2]{0,1:T(2,128)}, u32[]{:S(2)}) copy-start(s32[4,2]{0,1:T(2,128)} %param.20) | copy-start | bytes 100
  1.3 29.2 %copy-start.7 = (s32[4,2]{0,1:T(2,128)S(1)}, s32[4,2]{0,1:T(2,128)}, u32[]{:S(2)}) copy-start(s32[4,2]{0,1:T(2,128)} %param.21) | copy-start | bytes 100
  1.3 29.2 %copy-start.8 = (f32[128]{0:T(128)S(1)}, f32[128]{0:T(128)}, u32[]{:S(2)}) copy-start(f32[128]{0:T(128)} %param.13) | copy-start | bytes 1540
  1.3 7.3 %collective-permute-start = (bf16[4,96,128]{2,1,0:T(8,128)(2,1)S(1)}, bf16[4,96,128]{2,1,0:T(8,128)(2,1)S(1)}, u32[]{:S(2)}, u32[]{:S(2)}) collective-permute-start(bf16[4,96,128]{2,1,0:T(8,128)(2,1)S(1)} %get-tuple-element.20), channel_id=1, source_target_pairs={{0,32},{32,0},{64,96},{96,64},{1,33},{33,1},{65,97},{97,65},{2,34}... | collective-permute-start | bytes 294920 | tf_op jit(solution)/shard_map/ppermute | solution.py:209
  3.3 5.8 %collective-permute-start.1 = (bf16[4,96,128]{2,1,0:T(8,128)(2,1)S(1)}, bf16[4,96,128]{2,1,0:T(8,128)(2,1)S(1)}, u32[]{:S(2)}, u32[]{:S(2)}) collective-permute-start(bf16[4,96,128]{2,1,0:T(8,128)(2,1)S(1)} %get-tuple-element.21), channel_id=1, source_target_pairs={{0,96},{32,64},{64,32},{96,0},{1,97},{33,65},{65,33},{97,1},{2,98}... | collective-permute-start | bytes 294920 | tf_op jit(solution)/shard_map/ppermute | solution.py:209
  9.2 30.8 %all-to-all-start = ((bf16[128,24,128]{2,1,0:T(8,128)(2,1)}), bf16[128,24,128]{2,1,0:T(8,128)(2,1)S(1)}, u32[]{:S(2)}, u32[]{:S(2)}) async-start(bf16[128,24,128]{2,1,0:T(8,128)(2,1)} %pack.1), calls=%async_computation | async-start | bytes 1572864 | tf_op jit(solution)/shard_map/all_to_all | solution.py:568
  18.2 2.9 %collective-permute-start.2 = (bf16[2,100,128]{2,1,0:T(8,128)(2,1)S(1)}, bf16[2,100,128]{2,1,0:T(8,128)(2,1)S(1)}, u32[]{:S(2)}, u32[]{:S(2)}) collective-permute-start(bf16[2,100,128]{2,1,0:T(8,128)(2,1)S(1)} %get-tuple-element.25), channel_id=1, source_target_pairs={{0,1},{1,0},{2,3},{3,2},{4,5},{5,4},{6,7},{7,6},{8,9},{9,8},{10,11... | collective-permute-start | bytes 153608 | tf_op jit(solution)/shard_map/ppermute | solution.py:224
  18.4 12.1 %collective-permute-start.3 = (bf16[2,100,128]{2,1,0:T(8,128)(2,1)S(1)}, bf16[2,100,128]{2,1,0:T(8,128)(2,1)S(1)}, u32[]{:S(2)}, u32[]{:S(2)}) collective-permute-start(bf16[2,100,128]{2,1,0:T(8,128)(2,1)S(1)} %get-tuple-element.26), channel_id=1, source_target_pairs={{0,64},{1,2},{2,1},{3,4},{4,3},{5,6},{6,5},{7,8},{8,7},{9,10},{10,... | collective-permute-start | bytes 153608 | tf_op jit(solution)/shard_map/ppermute | solution.py:224
  30.5 9.6 %copy-start = (bf16[128,128]{1,0:T(8,128)(2,1)S(1)}, bf16[128,128]{1,0:T(8,128)(2,1)}, u32[]{:S(2)}) copy-start(bf16[128,128]{1,0:T(8,128)(2,1)} %weight_ref.1) | copy-start | bytes 98308
  40.0 22.9 %copy-start.2 = (bf16[9,128,128]{2,1,0:T(8,128)(2,1)S(1)}, bf16[9,128,128]{2,1,0:T(8,128)(2,1)}, u32[]{:S(2)}) copy-start(bf16[9,128,128]{2,1,0:T(8,128)(2,1)} %taps_ref.3) | copy-start | bytes 884740
  40.0 22.9 %copy-start.9 = (f32[128]{0:T(128)S(1)}, f32[128]{0:T(128)}, u32[]{:S(2)}) copy-start(f32[128]{0:T(128)} %param.15) | copy-start | bytes 1540
  47.4 5.8 %collective-permute-start.4 = (bf16[8,96,128]{2,1,0:T(8,128)(2,1)S(1)}, bf16[8,96,128]{2,1,0:T(8,128)(2,1)S(1)}, u32[]{:S(2)}, u32[]{:S(2)}) collective-permute-start(bf16[8,96,128]{2,1,0:T(8,128)(2,1)S(1)} %get-tuple-element.28), channel_id=1, source_target_pairs={{0,32},{32,0},{64,96},{96,64},{1,33},{33,1},{65,97},{97,65},{2,34}... | collective-permute-start | bytes 589832 | tf_op jit(solution)/shard_map/ppermute | solution.py:209
  49.6 6.9 %collective-permute-start.5 = (bf16[8,96,128]{2,1,0:T(8,128)(2,1)S(1)}, bf16[8,96,128]{2,1,0:T(8,128)(2,1)S(1)}, u32[]{:S(2)}, u32[]{:S(2)}) collective-permute-start(bf16[8,96,128]{2,1,0:T(8,128)(2,1)S(1)} %get-tuple-element.29), channel_id=1, source_target_pairs={{0,96},{32,64},{64,32},{96,0},{1,97},{33,65},{65,33},{97,1},{2,98}... | collective-permute-start | bytes 589832 | tf_op jit(solution)/shard_map/ppermute | solution.py:209
  56.5 1.5 %collective-permute-start.6 = (bf16[4,104,128]{2,1,0:T(8,128)(2,1)S(1)}, bf16[4,104,128]{2,1,0:T(8,128)(2,1)S(1)}, u32[]{:S(2)}, u32[]{:S(2)}) collective-permute-start(bf16[4,104,128]{2,1,0:T(8,128)(2,1)S(1)} %get-tuple-element.31), channel_id=1, source_target_pairs={{0,1},{1,0},{2,3},{3,2},{4,5},{5,4},{6,7},{7,6},{8,9},{9,8},{10,11... | collective-permute-start | bytes 319496 | tf_op jit(solution)/shard_map/ppermute | solution.py:224
  56.6 6.3 %collective-permute-start.7 = (bf16[4,104,128]{2,1,0:T(8,128)(2,1)S(1)}, bf16[4,104,128]{2,1,0:T(8,128)(2,1)S(1)}, u32[]{:S(2)}, u32[]{:S(2)}) collective-permute-start(bf16[4,104,128]{2,1,0:T(8,128)(2,1)S(1)} %get-tuple-element.32), channel_id=1, source_target_pairs={{0,64},{1,2},{2,1},{3,4},{4,3},{5,6},{6,5},{7,8},{8,7},{9,10},{10,... | collective-permute-start | bytes 319496 | tf_op jit(solution)/shard_map/ppermute | solution.py:224

commit v3 on v2

--- a/solution.py
+++ b/solution.py
@@ -230,37 +230,8 @@
     return half + half * jnp.tanh(inner)
 
 
-def conv_kernel(
-    d,
-    groups,
-    has_residual,
-    neighbor_ref,
-    reversal_ref,
-    grid_ref,
-    ra_ref,
-    rb_ref,
-    wa_ref,
-    wb_ref,
-    taps_ref,
-    bias_ref,
-    *rest,
-):
-    if has_residual:
-        fields_ref, out_ref, strip, weights, wide, acc, result, sems, out_sems, fields = rest
-    else:
-        out_ref, strip, weights, wide, acc, result, sems, out_sems = rest
-    rows, cols, ch = grid_ref.shape
-    face, tile, face_even, tile_even = parities()
-    nface = lax.axis_size("face")
-    last_tile = lax.axis_size("tile") - 1
-    load = pltpu.make_async_copy(
-        grid_ref, strip.at[pl.ds(d, rows), :, pl.ds(ch, ch)], sems.at[0]
-    )
-    load.start()
-    if has_residual:
-        load_fields = pltpu.make_async_copy(fields_ref, fields, sems.at[1])
-        load_fields.start()
-
+def pair_weights_kernel(taps_ref, weights):
+    ch = taps_ref.shape[1]
     for a in range(4):
         for e in range(3):
             at = (a * 3 + e) * ch
@@ -273,17 +244,222 @@
             else:
                 weights[at : at + ch, ch:] = jnp.zeros((ch, ch), BF16)
 
+
+def pair_weights(taps):
+    ch = taps.shape[1]
+    return pl.pallas_call(
+        pair_weights_kernel,
+        out_shape=VMEM((12 * ch, 2 * ch), BF16),
+        in_specs=[full_spec()],
+        out_specs=full_spec(),
+        cost_estimate=pl.CostEstimate(flops=1_000_000, bytes_accessed=1_000_000, transcendentals=0),
+        compiler_params=room(4),
+        name="pair_weights",
+    )(taps)
+
+
+EDGE = 8
+
+
+def shifted_copies(strip_row, west, east, d):
+    cols = strip_row.shape[0]
+    ch = strip_row.shape[1] // 3
+    v = strip_row[:, ch : 2 * ch]
+    strip_row[d:, :ch] = v[: cols - d]
+    strip_row[:d, :ch] = west
+    strip_row[: cols - d, 2 * ch :] = v[d:]
+    strip_row[cols - d :, 2 * ch :] = east
+
+
+def side_tile(ra_ref, rb_ref, p, at, face_even):
+    a = ra_ref[p, at, :].astype(F32)
+    b = rb_ref[p, at, :].astype(F32)
+    west = jnp.where(face_even, b, a).astype(BF16)
+    east = jnp.where(face_even, a, b).astype(BF16)
+    return west, east
+
+
+def pair_rows(strip, bases, d):
+    _, cols, wide = strip.shape
+    parts = []
+    for a in range(4):
+        of_a = [strip[pl.ds(base + a * d, d)].reshape(d * cols, wide) for base in bases]
+        parts.append(jnp.concatenate(of_a, axis=0))
+    return jnp.concatenate(parts, axis=1)
+
+
+def rows_kernel(d, step_rows, has_residual, grid_ref, ra_ref, rb_ref, weights, bias_ref, *rest):
+    if has_residual:
+        fields_ref, out_ref, strip, acc, result, sems, out_sems, fields = rest
+    else:
+        out_ref, strip, acc, result, sems, out_sems = rest
+    rows, cols, ch = grid_ref.shape
+    _, _, face_even, _ = parities()
+    inner = rows - 2 * EDGE
+    first = EDGE - 4
+    load = pltpu.make_async_copy(
+        grid_ref.at[pl.ds(first, inner + 8)], strip.at[:, :, pl.ds(ch, ch)], sems.at[0]
+    )
+    load.start()
+    if has_residual:
+        load_fields = pltpu.make_async_copy(
+            fields_ref.at[pl.ds(EDGE, inner)], fields, sems.at[1]
+        )
+        load_fields.start()
+    load.wait()
+    group = 8 // d
+    per_plane = cols // 8
+
+    def build(t, carry):
+        p = lax.div(t, per_plane)
+        at = pl.multiple_of((t - p * per_plane) * 8, 8)
+        west, east = side_tile(ra_ref, rb_ref, p, pl.ds(at, 8), face_even)
+        for k in range(group):
+            shifted_copies(
+                strip.at[t * group + k - first],
+                west[k * d : (k + 1) * d],
+                east[k * d : (k + 1) * d],
+                d,
+            )
+        return carry
+
+    lax.fori_loop(first // group, (first + inner + 8) // group, build, 0, unroll=2)
+    if has_residual:
+        load_fields.wait()
+
+    bias = bias_ref[...]
+    bias2 = jnp.concatenate([bias, bias], axis=1)
+    m = d * cols
+    groups = step_rows // (2 * d)
+    blocks = inner // step_rows
+
+    def product(i):
+        base = i * step_rows + 4 - d
+        lhs = pair_rows(strip, [base + g * 2 * d for g in range(groups)], d)
+        return jnp.dot(lhs, weights[...], preferred_element_type=F32)
+
+    def send(i):
+        return pltpu.make_async_copy(
+            result.at[pl.ds(i * step_rows, step_rows)],
+            out_ref.at[pl.ds(EDGE + i * step_rows, step_rows)],
+            out_sems.at[i],
+        )
+
+    def finish(i):
+        y = gelu(acc[...] + bias2)
+        for g in range(groups):
+            for half in range(2):
+                at = i * step_rows + g * 2 * d + half * d
+                piece = y[g * m : (g + 1) * m, half * ch : (half + 1) * ch].reshape(d, cols, ch)
+                if has_residual:
+                    piece = piece + fields[pl.ds(at, d)].astype(F32)
+                result[pl.ds(at, d)] = piece.astype(result.dtype)
+
+    acc[...] = product(0)
+
+    def block(i, carry):
+        finish(i - 1)
+        acc[...] = product(i)
+        send(i - 1).start()
+        return carry
+
+    lax.fori_loop(1, blocks, block, 0)
+    finish(blocks - 1)
+    send(blocks - 1).start()
+    for i in range(blocks):
+        send(i).wait()
+
+
+def conv_rows(grid, sides, weights, bias, d, fields, out_dtype):
+    rows, cols, ch = grid.shape
+    step_rows = 16
+    inner = rows - 2 * EDGE
+    operands = [far(grid) if fields is None else keep(grid), *[keep(x) for x in sides]]
+    operands += [keep(weights), bias.reshape(1, ch)]
+    in_specs = [full_spec(pl.ANY)] + [full_spec()] * 4
+    scratch = [
+        VMEM((inner + 8, cols, 3 * ch), BF16),
+        VMEM((step_rows // 2 * cols, 2 * ch), F32),
+        VMEM((inner, cols, ch), out_dtype),
+        pltpu.SemaphoreType.DMA((2,)),
+        pltpu.SemaphoreType.DMA((inner // step_rows,)),
+    ]
+    if fields is not None:
+        operands.append(far(fields))
+        in_specs.append(full_spec(pl.ANY))
+        scratch.append(VMEM((inner, cols, ch), BF16))
+    return pl.pallas_call(
+        functools.partial(rows_kernel, d, step_rows, fields is not None),
+        out_shape=pltpu.HBM((rows, cols, ch), out_dtype),
+        in_specs=in_specs,
+        out_specs=full_spec(pl.ANY),
+        scratch_shapes=scratch,
+        cost_estimate=pl.CostEstimate(
+            flops=2 * 12 * rows * cols * ch * ch, bytes_accessed=9_000_000, transcendentals=0
+        ),
+        compiler_params=room(28),
+        name="conv_rows",
+    )(*operands)
+
+
+def ends_kernel(
+    d,
+    has_residual,
+    neighbor_ref,
+    reversal_ref,
+    grid_ref,
+    ra_ref,
+    rb_ref,
+    wa_ref,
+    wb_ref,
+    weights,
+    bias_ref,
+    *rest,
+):
+    if has_residual:
+        fields_ref, _, out_ref, strip, wide, result, sems, fields = rest
+    else:
+        _, out_ref, strip, wide, result, sems = rest
+    rows, cols, ch = grid_ref.shape
+    face, tile, face_even, tile_even = parities()
+    nface = lax.axis_size("face")
+    last_tile = lax.axis_size("tile") - 1
+    span = EDGE + 2 * d
+    own = EDGE + d
+    loads = []
+    for side, at, to in ((0, 0, d), (1, rows - own, span)):
+        loads.append(
+            pltpu.make_async_copy(
+                grid_ref.at[pl.ds(at, own)],
+                strip.at[pl.ds(to, own), :, pl.ds(ch, ch)],
+                sems.at[side],
+            )
+        )
+        loads[-1].start()
+    if has_residual:
+        for side, at in ((0, 0), (1, rows - EDGE)):
+            loads.append(
+                pltpu.make_async_copy(
+                    fields_ref.at[pl.ds(at, EDGE)],
+                    fields.at[pl.ds(side * EDGE, EDGE)],
+                    sems.at[2 + side],
+                )
+            )
+            loads[-1].start()
     for r in range(d):
-        wide[0, r] = jnp.where(tile_even, wb_ref[r].astype(F32), wa_ref[r].astype(F32)).astype(BF16)
-        wide[1, r] = jnp.where(tile_even, wa_ref[r].astype(F32), wb_ref[r].astype(F32)).astype(BF16)
-    load.wait()
+        a = wa_ref[r].astype(F32)
+        b = wb_ref[r].astype(F32)
+        wide[0, r] = jnp.where(tile_even, b, a).astype(BF16)
+        wide[1, r] = jnp.where(tile_even, a, b).astype(BF16)
+    for load in loads:
+        load.wait()
 
     @pl.when((tile == 0) | (tile == last_tile))
     def _():
         which = jnp.where(tile == 0, 0, 1)
         sector = neighbor_ref[which, face]
         flip = reversal_ref[which, face]
-        own = jnp.where(tile == 0, d, rows)
+        mine = jnp.where(tile == 0, d, span + EDGE)
         width = cols + 2 * d
 
         def source_index(s):
@@ -307,7 +483,7 @@
         for r in range(d):
             source = jnp.concatenate(
                 [
-                    strip[own + r, :, ch : 2 * ch],
+                    strip[mine + r, :, ch : 2 * ch],
                     ra_ref[d + r],
                     rb_ref[d + r],
                     wb_ref[r, d : d + cols, :],
@@ -316,118 +492,82 @@
             )
             wide[which, d - 1 - r] = jnp.dot(pick, source, preferred_element_type=F32).astype(BF16)
 
-    for side, at in ((0, 0), (1, rows + d)):
+    for side, at in ((0, 0), (1, span + own)):
         for r in range(d):
             for e in range(3):
                 strip[at + r, :, e * ch : (e + 1) * ch] = wide[side, r, e * d : e * d + cols, :]
 
-    per = cols // d
     group = 8 // d
-
-    def build(i, p):
-        at = pl.multiple_of(i * 8, 8)
-        a = ra_ref[p, pl.ds(at, 8), :].astype(F32)
-        b = rb_ref[p, pl.ds(at, 8), :].astype(F32)
-        west = jnp.where(face_even, b, a).astype(BF16)
-        east = jnp.where(face_even, a, b).astype(BF16)
-        for k in range(group):
-            row = p * per + i * group + k + d
-            v = strip[row, :, ch : 2 * ch]
-            strip[row, d:, :ch] = v[: cols - d]
-            strip[row, :d, :ch] = west[k * d : (k + 1) * d]
-            strip[row, : cols - d, 2 * ch :] = v[d:]
-            strip[row, cols - d :, 2 * ch :] = east[k * d : (k + 1) * d]
-        return p
-
-    def build_plane(p, carry):
-        lax.fori_loop(0, per // group, build, p, unroll=2)
-        return carry
-
-    lax.fori_loop(0, d, build_plane, 0)
-    if has_residual:
-        load_fields.wait()
+    per_plane = cols // 8
+    for low, high, to in ((0, own, d), (rows - own, rows, span)):
+        for t in range(low // group, -(-high // group)):
+            p, at = divmod(t, per_plane)
+            west, east = side_tile(ra_ref, rb_ref, p, slice(at * 8, at * 8 + 8), face_even)
+            for k in range(group):
+                row = t * group + k
+                if low <= row < high:
+                    shifted_copies(
+                        strip.at[row - low + to],
+                        west[k * d : (k + 1) * d],
+                        east[k * d : (k + 1) * d],
+                        d,
+                    )
 
     bias = bias_ref[...]
     bias2 = jnp.concatenate([bias, bias], axis=1)
     m = d * cols
-    step_rows = groups * 2 * d
-    blocks = rows // step_rows
-
-    def product(i):
-        base = i * step_rows
-        parts = []
-        for a in range(4):
-            of_a = [
-                strip[pl.ds(base + g * 2 * d + a * d, d)].reshape(m, 3 * ch) for g in range(groups)
-            ]
-            parts.append(jnp.concatenate(of_a, axis=0))
-        return jnp.dot(
-            jnp.concatenate(parts, axis=1), weights[...], preferred_element_type=F32
+    starts = [(side, g * 2 * d) for side in range(2) for g in range(EDGE // (2 * d))]
+    lhs = pair_rows(strip, [side * span + at for side, at in starts], d)
+    y = gelu(jnp.dot(lhs, weights[...], preferred_element_type=F32) + bias2)
+    for g, (side, at) in enumerate(starts):
+        for half in range(2):
+            to = side * EDGE + at + half * d
+            piece = y[g * m : (g + 1) * m, half * ch : (half + 1) * ch].reshape(d, cols, ch)
+            if has_residual:
+                piece = piece + fields[to : to + d].astype(F32)
+            result[to : to + d] = piece.astype(result.dtype)
+    stores = [
+        pltpu.make_async_copy(
+            result.at[pl.ds(side * EDGE, EDGE)], out_ref.at[pl.ds(at, EDGE)], sems.at[4 + side]
         )
-
-    def send(i):
-        unit = step_rows if has_residual else step_rows * cols
-        at = pl.ds(i * unit, unit)
-        return pltpu.make_async_copy(result.at[at], out_ref.at[at], out_sems.at[i])
-
-    def finish(i):
-        y = gelu(acc[...] + bias2)
-        for g in range(groups):
-            for half in range(2):
-                at = i * step_rows + g * 2 * d + half * d
-                piece = y[g * m : (g + 1) * m, half * ch : (half + 1) * ch]
-                if has_residual:
-                    piece = piece.reshape(d, cols, ch) + fields[pl.ds(at, d)].astype(F32)
-                    result[pl.ds(at, d)] = piece.astype(BF16)
-                else:
-                    result[pl.ds(pl.multiple_of(at * cols, m), m), :] = piece
-
-    acc[...] = product(0)
-
-    def block(i, carry):
-        finish(i - 1)
-        acc[...] = product(i)
-        send(i - 1).start()
-        return carry
-
-    lax.fori_loop(1, blocks, block, 0)
-    finish(blocks - 1)
-    send(blocks - 1).start()
-    for i in range(blocks):
-        send(i).wait()
-
-
-def conv(grid, sides, wide, neighbor, reversal, taps, bias, d, groups, fields, out_dtype):
-    rows, cols, ch = grid.shape
-    operands = [neighbor.T, reversal.T, far(grid) if fields is None else keep(grid), *[keep(x) for x in (*sides, *wide)], taps, bias.reshape(1, ch)]
+        for side, at in ((0, 0), (1, rows - EDGE))
+    ]
+    for store in stores:
+        store.start()
+    for store in stores:
+        store.wait()
+
+
+def conv_ends(out, grid, sides, wide, neighbor, reversal, weights, bias, d, fields):
+    _, cols, ch = grid.shape
+    operands = [neighbor.T, reversal.T, far(grid) if fields is None else keep(grid)]
+    operands += [keep(x) for x in (*sides, *wide, weights)] + [bias.reshape(1, ch)]
     smem = full_spec(pltpu.SMEM)
     in_specs = [smem, smem, full_spec(pl.ANY)] + [full_spec()] * 6
     scratch = [
-        VMEM((rows + 2 * d, cols, 3 * ch), BF16),
-        VMEM((12 * ch, 2 * ch), BF16),
+        VMEM((2 * (EDGE + 2 * d), cols, 3 * ch), BF16),
         VMEM((2, d, cols + 2 * d, ch), BF16),
-        VMEM((groups * d * cols, 2 * ch), F32),
-        VMEM((rows, cols, ch), out_dtype),
-        pltpu.SemaphoreType.DMA((2,)),
-        pltpu.SemaphoreType.DMA((rows // (groups * 2 * d),)),
+        VMEM((2 * EDGE, cols, ch), out.dtype),
+        pltpu.SemaphoreType.DMA((6,)),
     ]
     if fields is not None:
         operands.append(far(fields))
         in_specs.append(full_spec(pl.ANY))
-        scratch.append(VMEM(fields.shape, BF16))
-    out = (rows, cols, ch) if fields is not None else (rows * cols, ch)
-    scratch[4] = VMEM(out, out_dtype)
-    out = pltpu.HBM(out, out_dtype)
+        scratch.append(VMEM((2 * EDGE, cols, ch), BF16))
+    operands.append(far(out))
+    in_specs.append(full_spec(pl.ANY))
     return pl.pallas_call(
-        functools.partial(conv_kernel, d, groups, fields is not None),
-        out_shape=out,
+        functools.partial(ends_kernel, d, fields is not None),
+        out_shape=pltpu.HBM(out.shape, out.dtype),
         in_specs=in_specs,
         out_specs=full_spec(pl.ANY),
         scratch_shapes=scratch,
+        input_output_aliases={len(operands) - 1: 0},
         cost_estimate=pl.CostEstimate(
-            flops=2 * 12 * rows * cols * ch * ch, bytes_accessed=9_000_000, transcendentals=0
+            flops=4 * 12 * EDGE * cols * ch * ch, bytes_accessed=1_000_000, transcendentals=0
         ),
-        compiler_params=room(28),
+        compiler_params=room(16),
+        name="conv_ends",
     )(*operands)
 
 
@@ -492,7 +632,7 @@
             for k in range(group):
                 row = p * per + i * group + k
                 at = pl.ds(pl.multiple_of(row * side, side), side)
-                v = first[at, :] + even[at, :] + extra[at, :]
+                v = first[row] + even[at, :] + extra[at, :]
                 mixed[row] = v.astype(BF16)
                 west.append(v[:d])
                 east.append(v[side - d :])
@@ -517,8 +657,7 @@
 
 
 def scatter(recv, weight, first, d):
-    cells, ch = first.shape
-    side = cols = round(cells**0.5)
+    side, cols, ch = first.shape
     sources = recv.shape[0]
     out = VMEM((2 * d, cols, ch), BF16)
     return pl.pallas_call(
@@ -528,8 +667,8 @@
         out_specs=(full_spec(),) * 4,
         scratch_shapes=[
             VMEM(first.shape, F32),
-            VMEM(first.shape, F32),
-            VMEM(first.shape, F32),
+            VMEM((side * cols, ch), F32),
+            VMEM((side * cols, ch), F32),
             VMEM((sources * CAP, ch), F32),
             VMEM((sources // 8, 128), I32),
             pltpu.SMEM((sources // 8, 128), I32),
@@ -559,24 +698,26 @@
     side = fields.shape[0]
     dests = lax.axis_size("face") * lax.axis_size("tile")
     d = FIRST_DILATION
+    weights = pair_weights(first_kernel_taps)
     a, b, ends = edges(fields, d)
     sides = swap_faces((a, b))
     send = pack(obs_owner, obs_cells, obs_values, dests, side)
-    wide = widen(ends, sides, d)
-    send, wide = lax.optimization_barrier((send, wide))
-    wide = swap_tiles(wide)
     recv = lax.all_to_all(send, ("face", "tile"), split_axis=0, concat_axis=0, tiled=True)
-    first = conv(
-        fields, sides, wide, polar_neighbor_sector, polar_link_reversal,
-        first_kernel_taps, first_conv_bias, d, 4, None, F32,
+    wide = swap_tiles(widen(ends, sides, d))
+    first = conv_rows(fields, sides, weights, first_conv_bias, d, None, F32)
+    first = conv_ends(
+        first, fields, sides, wide, polar_neighbor_sector, polar_link_reversal,
+        weights, first_conv_bias, d, None,
     )
     d = SECOND_DILATION
+    weights = pair_weights(second_kernel_taps)
     mixed, a, b, ends = scatter(recv, obs_weight, first, d)
     sides = swap_faces((a, b))
     wide = swap_tiles(widen(ends, sides, d))
-    return conv(
-        mixed, sides, wide, polar_neighbor_sector, polar_link_reversal,
-        second_kernel_taps, second_conv_bias, d, 2, fields, BF16,
+    out = conv_rows(mixed, sides, weights, second_conv_bias, d, fields, BF16)
+    return conv_ends(
+        out, mixed, sides, wide, polar_neighbor_sector, polar_link_reversal,
+        weights, second_conv_bias, d, fields,
     )
 
 

time: 71.9 us -> 73.8 us (1.026)
  the two profiles are of different devices: /device:TPU:4 before, /device:TPU:6 now
where the time goes in v3:
time: 73.8 us; the launch traced here: 73.4 us
  Pallas kernels  34 us (46%)
  starting transfers between devices  21.5 us (29%)
  waiting for transfers between devices  15.4 us (21%)
  local copies, waits for them, and re-layouts  2.36 us (3%)
    pallas_call x2, Pallas kernels, conv_rows(): pl.pallas_call(functools.partial(rows_kernel, d, step_rows, fields is not...  15.1 us
    ppermute x2, waiting for transfers between devices, swap_faces(): lax.ppermute(sides[0], 'face', inner)  12.2 us
    all_to_all x1, starting transfers between devices, local(): lax.all_to_all(send, ('face', 'tile'), split_axis=0, concat_axis=0, tiled...  10.5 us
    pallas_call x1, Pallas kernels, scatter(): pl.pallas_call(functools.partial(scatter_kernel, d), out_shape=(VMEM((sid...  7.77 us
    pallas_call x2, Pallas kernels, conv_ends(): pl.pallas_call(functools.partial(ends_kernel, d, fields is not None), out...  6.89 us
    ppermute x2, starting transfers between devices, swap_tiles(): lax.ppermute(wide[1], ('face', 'tile'), outer)  5.11 us
    ppermute x2, starting transfers between devices, swap_faces(): lax.ppermute(sides[1], 'face', outer)  3.85 us
    ppermute x2, waiting for transfers between devices, swap_faces(): lax.ppermute(sides[1], 'face', outer)  3.17 us
  transfers between devices with their start and end apart: 9, of which 4 were waited for; matrix products, arithmetic and copies ran while one was open for 0% of the time, Pallas kernels for 27%

profile of v3, /device:TPU:6, one launch (start us, length us, event | category | flops | bytes accessed | tf_op | source)
XLA Modules:
  0.0 73.4 jit_solution(15695385221195575053)
XLA Ops:
  0.0 0.9 %copy-done.7 = bf16[1024,128]{1,0:T(8,128)(2,1)S(1)} copy-done((bf16[1024,128]{1,0:T(8,128)(2,1)S(1)}, bf16[1024,128]{1,0:T(8,128)(2,1)}, u32[]{:S(2)}) %copy-start.7) | copy-done | bytes 262168
  1.0 0.7 copy-done.8
  1.6 0.7 copy-done.9
  2.3 2.7 %pack.1 = bf16[128,24,128]{2,1,0:T(8,128)(2,1)} custom-call(s32[1,1024]{1,0:T(1,128)S(1)} %bitcast.14, s32[1,1024]{1,0:T(1,128)S(1)} %bitcast.15, bf16[1024,128]{1,0:T(8,128)(2,1)S(1)} %copy-done.7), custom_call_target="tpu_custom_call" | custom-call | flops 536870912 | bytes 2000000 | tf_op jit(solution)/shard_map/pack/pallas_call | solution.py:92
  5.1 10.5 %all-to-all-start = ((bf16[128,24,128]{2,1,0:T(8,128)(2,1)}), bf16[128,24,128]{2,1,0:T(8,128)(2,1)S(1)}, u32[]{:S(2)}, u32[]{:S(2)}) async-start(bf16[128,24,128]{2,1,0:T(8,128)(2,1)} %pack.1), calls=%async_computation | async-start | bytes 1572864 | tf_op jit(solution)/shard_map/all_to_all | solution.py:705
  15.6 1.2 %edges.1 = (bf16[4,96,128]{2,1,0:T(8,128)(2,1)S(1)}, bf16[4,96,128]{2,1,0:T(8,128)(2,1)S(1)}, bf16[2,2,96,128]{3,2,1,0:T(8,128)(2,1)S(1)}) custom-call(bf16[96,96,128]{2,1,0:T(8,128)(2,1)} %rest_0_.3), custom_call_target="tpu_custom_call" | custom-call | flops 1000000 | bytes 800000 | tf_op jit(solution)/shard_map/edges/pallas_call | solution.py:145
  16.8 1.7 %collective-permute-start = (bf16[4,96,128]{2,1,0:T(8,128)(2,1)S(1)}, bf16[4,96,128]{2,1,0:T(8,128)(2,1)S(1)}, u32[]{:S(2)}, u32[]{:S(2)}) collective-permute-start(bf16[4,96,128]{2,1,0:T(8,128)(2,1)S(1)} %get-tuple-element.16), channel_id=1, source_target_pairs={{0,32},{32,0},{64,96},{96,64},{1,33},{33,1},{65,97},{97,65},{2,34}... | collective-permute-start | bytes 294920 | tf_op jit(solution)/shard_map/ppermute | solution.py:209
  18.5 2.3 %collective-permute-start.1 = (bf16[4,96,128]{2,1,0:T(8,128)(2,1)S(1)}, bf16[4,96,128]{2,1,0:T(8,128)(2,1)S(1)}, u32[]{:S(2)}, u32[]{:S(2)}) collective-permute-start(bf16[4,96,128]{2,1,0:T(8,128)(2,1)S(1)} %get-tuple-element.17), channel_id=1, source_target_pairs={{0,96},{32,64},{64,32},{96,0},{1,97},{33,65},{65,33},{97,1},{2,98}... | collective-permute-start | bytes 294920 | tf_op jit(solution)/shard_map/ppermute | solution.py:209
  20.8 0.1 pair_weights.2.weights
  20.9 8.1 %collective-permute-done.ra_ref = bf16[4,96,128]{2,1,0:T(8,128)(2,1)S(1)} collective-permute-done((bf16[4,96,128]{2,1,0:T(8,128)(2,1)S(1)}, bf16[4,96,128]{2,1,0:T(8,128)(2,1)S(1)}, u32[]{:S(2)}, u32[]{:S(2)}) %collective-permute-start) | collective-permute-done | bytes 98336 | tf_op jit(solution)/shard_map/ppermute | solution.py:209
  29.1 1.9 %collective-permute-done.1.rb_ref = bf16[4,96,128]{2,1,0:T(8,128)(2,1)S(1)} collective-permute-done((bf16[4,96,128]{2,1,0:T(8,128)(2,1)S(1)}, bf16[4,96,128]{2,1,0:T(8,128)(2,1)S(1)}, u32[]{:S(2)}, u32[]{:S(2)}) %collective-permute-start.1) | collective-permute-done | bytes 98336 | tf_op jit(solution)/shard_map/ppermute | solution.py:209
  31.0 0.1 collective-permute-start.2
  31.1 2.1 %collective-permute-start.3 = (bf16[2,100,128]{2,1,0:T(8,128)(2,1)S(1)}, bf16[2,100,128]{2,1,0:T(8,128)(2,1)S(1)}, u32[]{:S(2)}, u32[]{:S(2)}) collective-permute-start(bf16[2,100,128]{2,1,0:T(8,128)(2,1)S(1)} %get-tuple-element.20), channel_id=1, source_target_pairs={{0,64},{1,2},{2,1},{3,4},{4,3},{5,6},{6,5},{7,8},{8,7},{9,10},{10,... | collective-permute-start | bytes 153608 | tf_op jit(solution)/shard_map/ppermute | solution.py:224
  33.2 8.0 %conv_rows.2.rest_0_ = f32[96,96,128]{2,1,0:T(8,128)} custom-call(bf16[96,96,128]{2,1,0:T(8,128)(2,1)} %rest_0_.3, bf16[4,96,128]{2,1,0:T(8,128)(2,1)S(1)} %collective-permute-done.ra_ref, bf16[4,96,128]{2,1,0:T(8,128)(2,1)S(1)} %collective-permute-done.1.rb_ref, bf16[1536,256]{1,0:T(8,128)(2,1)S(1)} %pair_weights.2.weights, f32[1,128]{1,0:T(1,128)S(1)} %bitcast.10), custom_call_target="tpu_custom_call" | custom-call | flops 3623878656 | bytes 9000000 | tf_op jit(solution)/shard_map/conv_rows/pallas_call | solution.py:391
  41.3 3.4 %conv_ends.2.first_ref = f32[96,96,128]{2,1,0:T(8,128)} custom-call(s32[2,4]{1,0:T(2,128)S(1)} %bitcast.6, s32[2,4]{1,0:T(2,128)S(1)} %bitcast.8, bf16[96,96,128]{2,1,0:T(8,128)(2,1)} %rest_0_.3, bf16[4,96,128]{2,1,0:T(8,128)(2,1)S(1)} %collective-permute-done.ra_ref, ...), custom_call_target="tpu_custom_call", output_to_operand_aliasing={{}: (9, {})} | custom-call | flops 603979776 | bytes 1000000 | tf_op jit(solution)/shard_map/conv_ends/pallas_call | solution.py:559
  44.8 7.8 %scatter.1 = (bf16[96,96,128]{2,1,0:T(8,128)(2,1)S(1)}, bf16[8,96,128]{2,1,0:T(8,128)(2,1)S(1)}, bf16[8,96,128]{2,1,0:T(8,128)(2,1)S(1)}, bf16[2,4,96,128]{3,2,1,0:T(8,128)(2,1)S(1)}) custom-call(bf16[128,24,128]{2,1,0:T(8,128)(2,1)S(1)} %all-to-all-done.recv, bf16[128,128]{1,0:T(8,128)(2,1)S(1)} %copy-done.2, f32[96,96,128]{2,1,0:T(8,128)} %conv_ends.2.first_ref), custom_call_target="tpu_custom_call" | custom-call | flops 200000000 | bytes 12000000 | tf_op jit(solution)/shard_map/scatter/pallas_call | solution.py:663
  52.5 0.1 collective-permute-start.4
  52.6 1.5 %collective-permute-start.5 = (bf16[8,96,128]{2,1,0:T(8,128)(2,1)S(1)}, bf16[8,96,128]{2,1,0:T(8,128)(2,1)S(1)}, u32[]{:S(2)}, u32[]{:S(2)}) collective-permute-start(bf16[8,96,128]{2,1,0:T(8,128)(2,1)S(1)} %get-tuple-element.23), channel_id=1, source_target_pairs={{0,96},{32,64},{64,32},{96,0},{1,97},{33,65},{65,33},{97,1},{2,98}... | collective-permute-start | bytes 589832 | tf_op jit(solution)/shard_map/ppermute | solution.py:209
  54.2 0.1 pair_weights.3.weights
  54.3 4.0 %collective-permute-done.4.ra_ref = bf16[8,96,128]{2,1,0:T(8,128)(2,1)S(1)} collective-permute-done((bf16[8,96,128]{2,1,0:T(8,128)(2,1)S(1)}, bf16[8,96,128]{2,1,0:T(8,128)(2,1)S(1)}, u32[]{:S(2)}, u32[]{:S(2)}) %collective-permute-start.4) | collective-permute-done | bytes 196640 | tf_op jit(solution)/shard_map/ppermute | solution.py:209
  58.3 1.3 %collective-permute-done.5.rb_ref = bf16[8,96,128]{2,1,0:T(8,128)(2,1)S(1)} collective-permute-done((bf16[8,96,128]{2,1,0:T(8,128)(2,1)S(1)}, bf16[8,96,128]{2,1,0:T(8,128)(2,1)S(1)}, u32[]{:S(2)}, u32[]{:S(2)}) %collective-permute-start.5) | collective-permute-done | bytes 196640 | tf_op jit(solution)/shard_map/ppermute | solution.py:209
  59.8 3.0 %collective-permute-start.7 = (bf16[4,104,128]{2,1,0:T(8,128)(2,1)S(1)}, bf16[4,104,128]{2,1,0:T(8,128)(2,1)S(1)}, u32[]{:S(2)}, u32[]{:S(2)}) collective-permute-start(bf16[4,104,128]{2,1,0:T(8,128)(2,1)S(1)} %get-tuple-element.26), channel_id=1, source_target_pairs={{0,64},{1,2},{2,1},{3,4},{4,3},{5,6},{6,5},{7,8},{8,7},{9,10},{10,... | collective-permute-start | bytes 319496 | tf_op jit(solution)/shard_map/ppermute | solution.py:224
  62.8 7.1 %conv_rows.3.rest_1_ = bf16[96,96,128]{2,1,0:T(8,128)(2,1)} custom-call(bf16[96,96,128]{2,1,0:T(8,128)(2,1)S(1)} %get-tuple-element.21.grid_ref, bf16[8,96,128]{2,1,0:T(8,128)(2,1)S(1)} %collective-permute-done.4.ra_ref, bf16[8,96,128]{2,1,0:T(8,128)(2,1)S(1)} %collective-permute-done.5.rb_ref, bf16[1536,256]{1,0:T(8,128)(2,1)S(1)} %pair_weights.3.weights, ...), custom_call_target="tpu_custom_call" | custom-call | flops 3623878656 | bytes 9000000 | tf_op jit(solution)/shard_map/conv_rows/pallas_call | solution.py:391
  69.9 3.4 %conv_ends.3 = bf16[96,96,128]{2,1,0:T(8,128)(2,1)} custom-call(s32[2,4]{1,0:T(2,128)S(1)} %bitcast.7, s32[2,4]{1,0:T(2,128)S(1)} %bitcast.9, bf16[96,96,128]{2,1,0:T(8,128)(2,1)S(1)} %get-tuple-element.21.grid_ref, bf16[8,96,128]{2,1,0:T(8,128)(2,1)S(1)} %collective-permute-done.4.ra_ref, ...), custom_call_target="tpu_custom_call", output_to_operand_aliasing={{}: (10, {})} | custom-call | flops 603979776 | bytes 1000000 | tf_op jit(solution)/shard_map/conv_ends/pallas_call | solution.py:559
  (25 shorter events, 0.2 us)
Async XLA Ops:
  0.0 0.9 %copy-start.7 = (bf16[1024,128]{1,0:T(8,128)(2,1)S(1)}, bf16[1024,128]{1,0:T(8,128)(2,1)}, u32[]{:S(2)}) copy-start(bf16[1024,128]{1,0:T(8,128)(2,1)} %vals_ref.1) | copy-start | bytes 786436
  1.0 0.7 copy-start.8
  1.6 0.7 copy-start.9
  5.1 15.8 %copy-start = (bf16[9,128,128]{2,1,0:T(8,128)(2,1)S(1)}, bf16[9,128,128]{2,1,0:T(8,128)(2,1)}, u32[]{:S(2)}) copy-start(bf16[9,128,128]{2,1,0:T(8,128)(2,1)} %taps_ref.2) | copy-start | bytes 884740
  5.1 28.2 %copy-start.5 = (f32[128]{0:T(128)S(1)}, f32[128]{0:T(128)}, u32[]{:S(2)}) copy-start(f32[128]{0:T(128)} %param.13) | copy-start | bytes 1540
  5.1 39.7 %all-to-all-start = ((bf16[128,24,128]{2,1,0:T(8,128)(2,1)}), bf16[128,24,128]{2,1,0:T(8,128)(2,1)S(1)}, u32[]{:S(2)}, u32[]{:S(2)}) async-start(bf16[128,24,128]{2,1,0:T(8,128)(2,1)} %pack.1), calls=%async_computation | async-start | bytes 1572864 | tf_op jit(solution)/shard_map/all_to_all | solution.py:705
  16.8 12.3 %collective-permute-start = (bf16[4,96,128]{2,1,0:T(8,128)(2,1)S(1)}, bf16[4,96,128]{2,1,0:T(8,128)(2,1)S(1)}, u32[]{:S(2)}, u32[]{:S(2)}) collective-permute-start(bf16[4,96,128]{2,1,0:T(8,128)(2,1)S(1)} %get-tuple-element.16), channel_id=1, source_target_pairs={{0,32},{32,0},{64,96},{96,64},{1,33},{33,1},{65,97},{97,65},{2,34}... | collective-permute-start | bytes 294920 | tf_op jit(solution)/shard_map/ppermute | solution.py:209
  18.5 12.5 %collective-permute-start.1 = (bf16[4,96,128]{2,1,0:T(8,128)(2,1)S(1)}, bf16[4,96,128]{2,1,0:T(8,128)(2,1)S(1)}, u32[]{:S(2)}, u32[]{:S(2)}) collective-permute-start(bf16[4,96,128]{2,1,0:T(8,128)(2,1)S(1)} %get-tuple-element.17), channel_id=1, source_target_pairs={{0,96},{32,64},{64,32},{96,0},{1,97},{33,65},{65,33},{97,1},{2,98}... | collective-permute-start | bytes 294920 | tf_op jit(solution)/shard_map/ppermute | solution.py:209
  31.0 10.2 %collective-permute-start.2 = (bf16[2,100,128]{2,1,0:T(8,128)(2,1)S(1)}, bf16[2,100,128]{2,1,0:T(8,128)(2,1)S(1)}, u32[]{:S(2)}, u32[]{:S(2)}) collective-permute-start(bf16[2,100,128]{2,1,0:T(8,128)(2,1)S(1)} %get-tuple-element.19), channel_id=1, source_target_pairs={{0,1},{1,0},{2,3},{3,2},{4,5},{5,4},{6,7},{7,6},{8,9},{9,8},{10,11... | collective-permute-start | bytes 153608 | tf_op jit(solution)/shard_map/ppermute | solution.py:224
  31.1 10.1 %collective-permute-start.3 = (bf16[2,100,128]{2,1,0:T(8,128)(2,1)S(1)}, bf16[2,100,128]{2,1,0:T(8,128)(2,1)S(1)}, u32[]{:S(2)}, u32[]{:S(2)}) collective-permute-start(bf16[2,100,128]{2,1,0:T(8,128)(2,1)S(1)} %get-tuple-element.20), channel_id=1, source_target_pairs={{0,64},{1,2},{2,1},{3,4},{4,3},{5,6},{6,5},{7,8},{8,7},{9,10},{10,... | collective-permute-start | bytes 153608 | tf_op jit(solution)/shard_map/ppermute | solution.py:224
  33.2 8.0 %copy-start.3 = (s32[4,2]{0,1:T(2,128)S(1)}, s32[4,2]{0,1:T(2,128)}, u32[]{:S(2)}) copy-start(s32[4,2]{0,1:T(2,128)} %param.20) | copy-start | bytes 100
  33.2 8.0 %copy-start.4 = (s32[4,2]{0,1:T(2,128)S(1)}, s32[4,2]{0,1:T(2,128)}, u32[]{:S(2)}) copy-start(s32[4,2]{0,1:T(2,128)} %param.21) | copy-start | bytes 100
  41.3 3.5 %copy-start.2 = (bf16[128,128]{1,0:T(8,128)(2,1)S(1)}, bf16[128,128]{1,0:T(8,128)(2,1)}, u32[]{:S(2)}) copy-start(bf16[128,128]{1,0:T(8,128)(2,1)} %weight_ref.1) | copy-start | bytes 98308
  44.7 9.4 %copy-start.1 = (bf16[9,128,128]{2,1,0:T(8,128)(2,1)S(1)}, bf16[9,128,128]{2,1,0:T(8,128)(2,1)}, u32[]{:S(2)}) copy-start(bf16[9,128,128]{2,1,0:T(8,128)(2,1)} %taps_ref.3) | copy-start | bytes 884740
  44.7 18.1 %copy-start.6 = (f32[128]{0:T(128)S(1)}, f32[128]{0:T(128)}, u32[]{:S(2)}) copy-start(f32[128]{0:T(128)} %param.15) | copy-start | bytes 1540
  52.5 5.8 %collective-permute-start.4 = (bf16[8,96,128]{2,1,0:T(8,128)(2,1)S(1)}, bf16[8,96,128]{2,1,0:T(8,128)(2,1)S(1)}, u32[]{:S(2)}, u32[]{:S(2)}) collective-permute-start(bf16[8,96,128]{2,1,0:T(8,128)(2,1)S(1)} %get-tuple-element.22), channel_id=1, source_target_pairs={{0,32},{32,0},{64,96},{96,64},{1,33},{33,1},{65,97},{97,65},{2,34}... | collective-permute-start | bytes 589832 | tf_op jit(solution)/shard_map/ppermute | solution.py:209
  52.6 7.0 %collective-permute-start.5 = (bf16[8,96,128]{2,1,0:T(8,128)(2,1)S(1)}, bf16[8,96,128]{2,1,0:T(8,128)(2,1)S(1)}, u32[]{:S(2)}, u32[]{:S(2)}) collective-permute-start(bf16[8,96,128]{2,1,0:T(8,128)(2,1)S(1)} %get-tuple-element.23), channel_id=1, source_target_pairs={{0,96},{32,64},{64,32},{96,0},{1,97},{33,65},{65,33},{97,1},{2,98}... | collective-permute-start | bytes 589832 | tf_op jit(solution)/shard_map/ppermute | solution.py:209
  59.7 10.3 %collective-permute-start.6 = (bf16[4,104,128]{2,1,0:T(8,128)(2,1)S(1)}, bf16[4,104,128]{2,1,0:T(8,128)(2,1)S(1)}, u32[]{:S(2)}, u32[]{:S(2)}) collective-permute-start(bf16[4,104,128]{2,1,0:T(8,128)(2,1)S(1)} %get-tuple-element.25), channel_id=1, source_target_pairs={{0,1},{1,0},{2,3},{3,2},{4,5},{5,4},{6,7},{7,6},{8,9},{9,8},{10,11... | collective-permute-start | bytes 319496 | tf_op jit(solution)/shard_map/ppermute | solution.py:224
  59.8 10.2 %collective-permute-start.7 = (bf16[4,104,128]{2,1,0:T(8,128)(2,1)S(1)}, bf16[4,104,128]{2,1,0:T(8,128)(2,1)S(1)}, u32[]{:S(2)}, u32[]{:S(2)}) collective-permute-start(bf16[4,104,128]{2,1,0:T(8,128)(2,1)S(1)} %get-tuple-element.26), channel_id=1, source_target_pairs={{0,64},{1,2},{2,1},{3,4},{4,3},{5,6},{6,5},{7,8},{8,7},{9,10},{10,... | collective-permute-start | bytes 319496 | tf_op jit(solution)/shard_map/ppermute | solution.py:224

commit v4 on v3

--- a/solution.py
+++ b/solution.py
@@ -400,6 +400,188 @@
         compiler_params=room(28),
         name="conv_rows",
     )(*operands)
+
+
+def core_kernel(d, step_rows, grid_ref, weights, bias_ref, fields_ref, out_ref, strip, acc, result, sems, out_sems, fields):
+    rows, cols, ch = grid_ref.shape
+    inner = rows - 2 * EDGE
+    width = cols - 2 * EDGE
+    low = EDGE - d
+    load = pltpu.make_async_copy(
+        grid_ref.at[pl.ds(low, inner + 2 * d), pl.ds(EDGE, width), :],
+        strip.at[:, :, pl.ds(ch, ch)],
+        sems.at[0],
+    )
+    load.start()
+    load_fields = pltpu.make_async_copy(
+        fields_ref.at[pl.ds(EDGE, inner), pl.ds(EDGE, width), :], fields, sems.at[1]
+    )
+    load_fields.start()
+
+    def build(p, carry):
+        v = grid_ref[p + low]
+        strip[p, :, :ch] = v[EDGE - d : EDGE - d + width]
+        strip[p, :, 2 * ch :] = v[EDGE + d : EDGE + d + width]
+        return carry
+
+    lax.fori_loop(0, inner + 2 * d, build, 0, unroll=4)
+    load.wait()
+    load_fields.wait()
+    bias = bias_ref[...]
+    bias2 = jnp.concatenate([bias, bias], axis=1)
+    m = d * width
+    groups = step_rows // (2 * d)
+    blocks = inner // step_rows
+
+    def product(i):
+        lhs = pair_rows(strip, [i * step_rows + g * 2 * d for g in range(groups)], d)
+        return jnp.dot(lhs, weights[...], preferred_element_type=F32)
+
+    def send(i):
+        return pltpu.make_async_copy(
+            result.at[pl.ds(i * step_rows, step_rows)],
+            out_ref.at[pl.ds(EDGE + i * step_rows, step_rows), pl.ds(EDGE, width), :],
+            out_sems.at[i],
+        )
+
+    def finish(i):
+        y = gelu(acc[...] + bias2)
+        for g in range(groups):
+            for half in range(2):
+                at = i * step_rows + g * 2 * d + half * d
+                piece = y[g * m : (g + 1) * m, half * ch : (half + 1) * ch].reshape(d, width, ch)
+                piece = piece + fields[pl.ds(at, d)].astype(F32)
+                result[pl.ds(at, d)] = piece.astype(result.dtype)
+
+    acc[...] = product(0)
+
+    def block(i, carry):
+        finish(i - 1)
+        acc[...] = product(i)
+        send(i - 1).start()
+        return carry
+
+    lax.fori_loop(1, blocks, block, 0)
+    finish(blocks - 1)
+    send(blocks - 1).start()
+    for i in range(blocks):
+        send(i).wait()
+
+
+def conv_core(grid, weights, bias, d, fields):
+    rows, cols, ch = grid.shape
+    step_rows = 16
+    inner = rows - 2 * EDGE
+    width = cols - 2 * EDGE
+    return pl.pallas_call(
+        functools.partial(core_kernel, d, step_rows),
+        out_shape=pltpu.HBM(grid.shape, BF16),
+        in_specs=[full_spec(), full_spec(), full_spec(), full_spec(pl.ANY)],
+        out_specs=full_spec(pl.ANY),
+        scratch_shapes=[
+            VMEM((inner + 2 * d, width, 3 * ch), BF16),
+            VMEM((step_rows // 2 * width, 2 * ch), F32),
+            VMEM((inner, width, ch), BF16),
+            pltpu.SemaphoreType.DMA((2,)),
+            pltpu.SemaphoreType.DMA((inner // step_rows,)),
+            VMEM((inner, width, ch), BF16),
+        ],
+        cost_estimate=pl.CostEstimate(
+            flops=2 * 12 * inner * width * ch * ch, bytes_accessed=4_000_000, transcendentals=0
+        ),
+        compiler_params=room(20),
+        name="conv_core",
+    )(keep(grid), keep(weights), bias.reshape(1, ch), far(fields))
+
+
+def columns_kernel(d, grid_ref, ra_ref, rb_ref, weights, bias_ref, fields_ref, _, out_ref, strip, result, sems, fields):
+    rows, cols, ch = grid_ref.shape
+    _, _, face_even, _ = parities()
+    inner = rows - 2 * EDGE
+    low = EDGE - d
+    ends = ((0, 0), (1, cols - EDGE))
+    loads = [
+        pltpu.make_async_copy(
+            fields_ref.at[pl.ds(EDGE, inner), pl.ds(at, EDGE), :],
+            fields.at[:, pl.ds(side * EDGE, EDGE), :],
+            sems.at[side],
+        )
+        for side, at in ends
+    ]
+    for load in loads:
+        load.start()
+    group = 8 // d
+    per_plane = cols // 8
+
+    def build(t, carry):
+        p = lax.div(t, per_plane)
+        at = pl.ds(pl.multiple_of((t - p * per_plane) * 8, 8), 8)
+        a = ra_ref[p, at, :].astype(F32)
+        b = rb_ref[p, at, :].astype(F32)
+        west = jnp.where(face_even, b, a)
+        east = jnp.where(face_even, a, b)
+        for k in range(group):
+            row = t * group + k
+            left = grid_ref[row, :16, :].astype(F32)
+            right = grid_ref[row, cols - 16 :, :].astype(F32)
+            first = [west[k * d : (k + 1) * d], left[: 8 - d], right[8 - d : 16 - d]]
+            middle = [left[:8], right[8:]]
+            last = [left[d : 8 + d], right[8 + d :], east[k * d : (k + 1) * d]]
+            for e, parts in enumerate((first, middle, last)):
+                strip[row - low, :, e * ch : (e + 1) * ch] = jnp.concatenate(parts, axis=0).astype(BF16)
+        return carry
+
+    lax.fori_loop(low // group, (low + inner + 2 * d) // group, build, 0, unroll=2)
+    bias = bias_ref[...]
+    bias2 = jnp.concatenate([bias, bias], axis=1)
+    m = d * 2 * EDGE
+    groups = inner // (2 * d)
+    lhs = pair_rows(strip, [g * 2 * d for g in range(groups)], d)
+    y = gelu(jnp.dot(lhs, weights[...], preferred_element_type=F32) + bias2)
+    for load in loads:
+        load.wait()
+    for g in range(groups):
+        for half in range(2):
+            at = g * 2 * d + half * d
+            piece = y[g * m : (g + 1) * m, half * ch : (half + 1) * ch].reshape(d, 2 * EDGE, ch)
+            result[at : at + d] = (piece + fields[at : at + d].astype(F32)).astype(BF16)
+    stores = [
+        pltpu.make_async_copy(
+            result.at[:, pl.ds(side * EDGE, EDGE), :],
+            out_ref.at[pl.ds(EDGE, inner), pl.ds(at, EDGE), :],
+            sems.at[2 + side],
+        )
+        for side, at in ends
+    ]
+    for store in stores:
+        store.start()
+    for store in stores:
+        store.wait()
+
+
+def conv_columns(out, grid, sides, weights, bias, d, fields):
+    rows, _, ch = grid.shape
+    inner = rows - 2 * EDGE
+    return pl.pallas_call(
+        functools.partial(columns_kernel, d),
+        out_shape=pltpu.HBM(out.shape, out.dtype),
+        in_specs=[full_spec()] * 5 + [full_spec(pl.ANY)] * 2,
+        out_specs=full_spec(pl.ANY),
+        scratch_shapes=[
+            VMEM((inner + 2 * d, 2 * EDGE, 3 * ch), BF16),
+            VMEM((inner, 2 * EDGE, ch), BF16),
+            pltpu.SemaphoreType.DMA((4,)),
+            VMEM((inner, 2 * EDGE, ch), BF16),
+        ],
+        input_output_aliases={6: 0},
+        cost_estimate=pl.CostEstimate(
+            flops=4 * 12 * inner * EDGE * ch * ch, bytes_accessed=2_000_000, transcendentals=0
+        ),
+        compiler_params=room(16),
+        name="conv_columns",
+    )(
+        keep(grid), *[keep(x) for x in sides], keep(weights), bias.reshape(1, ch), far(fields), far(out)
+    )
 
 
 def ends_kernel(
@@ -713,8 +895,9 @@
     weights = pair_weights(second_kernel_taps)
     mixed, a, b, ends = scatter(recv, obs_weight, first, d)
     sides = swap_faces((a, b))
+    out = conv_core(mixed, weights, second_conv_bias, d, fields)
     wide = swap_tiles(widen(ends, sides, d))
-    out = conv_rows(mixed, sides, weights, second_conv_bias, d, fields, BF16)
+    out = conv_columns(out, mixed, sides, weights, second_conv_bias, d, fields)
     return conv_ends(
         out, mixed, sides, wide, polar_neighbor_sector, polar_link_reversal,
         weights, second_conv_bias, d, fields,

time: 73.8 us -> 74.9 us (1.015)
  Pallas kernels: 34 us -> 35.2 us
    pallas_call x0 -> x2, Pallas kernels: none -> 8.27 us  [the longest x1 6.28 us: conv_core(): pl.pallas_call(functools.partial(core_kernel, d, step_rows), out_shape=pl...]
    pallas_call x2 -> x1, Pallas kernels: 15.1 us -> 7.97 us  [conv_rows(): pl.pallas_call(functools.partial(rows_kernel, d, step_rows, fields is not...]
  transfers between devices with their start and end apart: 9 -> 9, of which waited for: 4 -> 4; matrix products, arithmetic and copies ran while one was open for 0% -> 0% of each run, Pallas kernels for 27% -> 28%
where the time goes in v4:
time: 74.9 us; the launch traced here: 74.5 us
  Pallas kernels  35.2 us (47%)
  starting transfers between devices  21.5 us (29%)
  waiting for transfers between devices  15.4 us (21%)
  local copies, waits for them, and re-layouts  2.36 us (3%)
    ppermute x2, waiting for transfers between devices, swap_faces(): lax.ppermute(sides[0], 'face', inner)  12.2 us
    all_to_all x1, starting transfers between devices, local(): lax.all_to_all(send, ('face', 'tile'), split_axis=0, concat_axis=0, tiled...  10.5 us
    pallas_call x1, Pallas kernels, conv_rows(): pl.pallas_call(functools.partial(rows_kernel, d, step_rows, fields is not...  7.97 us
    pallas_call x1, Pallas kernels, scatter(): pl.pallas_call(functools.partial(scatter_kernel, d), out_shape=(VMEM((sid...  7.77 us
    pallas_call x2, Pallas kernels, conv_ends(): pl.pallas_call(functools.partial(ends_kernel, d, fields is not None), out...  6.88 us
    pallas_call x1, Pallas kernels, conv_core(): pl.pallas_call(functools.partial(core_kernel, d, step_rows), out_shape=pl...  6.28 us
    ppermute x2, starting transfers between devices, swap_tiles(): lax.ppermute(wide[1], ('face', 'tile'), outer)  5.11 us
    ppermute x2, starting transfers between devices, swap_faces(): lax.ppermute(sides[1], 'face', outer)  3.85 us
  transfers between devices with their start and end apart: 9, of which 4 were waited for; matrix products, arithmetic and copies ran while one was open for 0% of the time, Pallas kernels for 28%

profile of v4, /device:TPU:6, one launch (start us, length us, event | category | flops | bytes accessed | tf_op | source)
XLA Modules:
  0.0 74.5 jit_solution(2678270226638490826)
XLA Ops:
  0.0 0.9 %copy-done.7 = bf16[1024,128]{1,0:T(8,128)(2,1)S(1)} copy-done((bf16[1024,128]{1,0:T(8,128)(2,1)S(1)}, bf16[1024,128]{1,0:T(8,128)(2,1)}, u32[]{:S(2)}) %copy-start.7) | copy-done | bytes 262168
  1.0 0.7 copy-done.8
  1.6 0.7 copy-done.9
  2.3 2.7 %pack.1 = bf16[128,24,128]{2,1,0:T(8,128)(2,1)} custom-call(s32[1,1024]{1,0:T(1,128)S(1)} %bitcast.15, s32[1,1024]{1,0:T(1,128)S(1)} %bitcast.16, bf16[1024,128]{1,0:T(8,128)(2,1)S(1)} %copy-done.7), custom_call_target="tpu_custom_call" | custom-call | flops 536870912 | bytes 2000000 | tf_op jit(solution)/shard_map/pack/pallas_call | solution.py:92
  5.1 10.5 %all-to-all-start = ((bf16[128,24,128]{2,1,0:T(8,128)(2,1)}), bf16[128,24,128]{2,1,0:T(8,128)(2,1)S(1)}, u32[]{:S(2)}, u32[]{:S(2)}) async-start(bf16[128,24,128]{2,1,0:T(8,128)(2,1)} %pack.1), calls=%async_computation | async-start | bytes 1572864 | tf_op jit(solution)/shard_map/all_to_all | solution.py:887
  15.6 1.2 %edges.1 = (bf16[4,96,128]{2,1,0:T(8,128)(2,1)S(1)}, bf16[4,96,128]{2,1,0:T(8,128)(2,1)S(1)}, bf16[2,2,96,128]{3,2,1,0:T(8,128)(2,1)S(1)}) custom-call(bf16[96,96,128]{2,1,0:T(8,128)(2,1)} %rest_0_.1), custom_call_target="tpu_custom_call" | custom-call | flops 1000000 | bytes 800000 | tf_op jit(solution)/shard_map/edges/pallas_call | solution.py:145
  16.8 1.7 %collective-permute-start = (bf16[4,96,128]{2,1,0:T(8,128)(2,1)S(1)}, bf16[4,96,128]{2,1,0:T(8,128)(2,1)S(1)}, u32[]{:S(2)}, u32[]{:S(2)}) collective-permute-start(bf16[4,96,128]{2,1,0:T(8,128)(2,1)S(1)} %get-tuple-element.16), channel_id=1, source_target_pairs={{0,32},{32,0},{64,96},{96,64},{1,33},{33,1},{65,97},{97,65},{2,34}... | collective-permute-start | bytes 294920 | tf_op jit(solution)/shard_map/ppermute | solution.py:209
  18.5 2.3 %collective-permute-start.1 = (bf16[4,96,128]{2,1,0:T(8,128)(2,1)S(1)}, bf16[4,96,128]{2,1,0:T(8,128)(2,1)S(1)}, u32[]{:S(2)}, u32[]{:S(2)}) collective-permute-start(bf16[4,96,128]{2,1,0:T(8,128)(2,1)S(1)} %get-tuple-element.17), channel_id=1, source_target_pairs={{0,96},{32,64},{64,32},{96,0},{1,97},{33,65},{65,33},{97,1},{2,98}... | collective-permute-start | bytes 294920 | tf_op jit(solution)/shard_map/ppermute | solution.py:209
  20.8 0.1 pair_weights.2.weights
  20.9 8.1 %collective-permute-done.ra_ref = bf16[4,96,128]{2,1,0:T(8,128)(2,1)S(1)} collective-permute-done((bf16[4,96,128]{2,1,0:T(8,128)(2,1)S(1)}, bf16[4,96,128]{2,1,0:T(8,128)(2,1)S(1)}, u32[]{:S(2)}, u32[]{:S(2)}) %collective-permute-start) | collective-permute-done | bytes 98336 | tf_op jit(solution)/shard_map/ppermute | solution.py:209
  29.1 1.9 %collective-permute-done.1.rb_ref = bf16[4,96,128]{2,1,0:T(8,128)(2,1)S(1)} collective-permute-done((bf16[4,96,128]{2,1,0:T(8,128)(2,1)S(1)}, bf16[4,96,128]{2,1,0:T(8,128)(2,1)S(1)}, u32[]{:S(2)}, u32[]{:S(2)}) %collective-permute-start.1) | collective-permute-done | bytes 98336 | tf_op jit(solution)/shard_map/ppermute | solution.py:209
  31.0 0.1 collective-permute-start.2
  31.1 2.1 %collective-permute-start.3 = (bf16[2,100,128]{2,1,0:T(8,128)(2,1)S(1)}, bf16[2,100,128]{2,1,0:T(8,128)(2,1)S(1)}, u32[]{:S(2)}, u32[]{:S(2)}) collective-permute-start(bf16[2,100,128]{2,1,0:T(8,128)(2,1)S(1)} %get-tuple-element.20), channel_id=1, source_target_pairs={{0,64},{1,2},{2,1},{3,4},{4,3},{5,6},{6,5},{7,8},{8,7},{9,10},{10,... | collective-permute-start | bytes 153608 | tf_op jit(solution)/shard_map/ppermute | solution.py:224
  33.2 8.0 %conv_rows.1.rest_0_ = f32[96,96,128]{2,1,0:T(8,128)} custom-call(bf16[96,96,128]{2,1,0:T(8,128)(2,1)} %rest_0_.1, bf16[4,96,128]{2,1,0:T(8,128)(2,1)S(1)} %collective-permute-done.ra_ref, bf16[4,96,128]{2,1,0:T(8,128)(2,1)S(1)} %collective-permute-done.1.rb_ref, bf16[1536,256]{1,0:T(8,128)(2,1)S(1)} %pair_weights.2.weights, f32[1,128]{1,0:T(1,128)S(1)} %bitcast.13), custom_call_target="tpu_custom_call" | custom-call | flops 3623878656 | bytes 9000000 | tf_op jit(solution)/shard_map/conv_rows/pallas_call | solution.py:391
  41.3 3.4 %conv_ends.2.first_ref = f32[96,96,128]{2,1,0:T(8,128)} custom-call(s32[2,4]{1,0:T(2,128)S(1)} %bitcast.6, s32[2,4]{1,0:T(2,128)S(1)} %bitcast.8, bf16[96,96,128]{2,1,0:T(8,128)(2,1)} %rest_0_.1, bf16[4,96,128]{2,1,0:T(8,128)(2,1)S(1)} %collective-permute-done.ra_ref, ...), custom_call_target="tpu_custom_call", output_to_operand_aliasing={{}: (9, {})} | custom-call | flops 603979776 | bytes 1000000 | tf_op jit(solution)/shard_map/conv_ends/pallas_call | solution.py:741
  44.8 7.8 %scatter.1 = (bf16[96,96,128]{2,1,0:T(8,128)(2,1)S(1)}, bf16[8,96,128]{2,1,0:T(8,128)(2,1)S(1)}, bf16[8,96,128]{2,1,0:T(8,128)(2,1)S(1)}, bf16[2,4,96,128]{3,2,1,0:T(8,128)(2,1)S(1)}) custom-call(bf16[128,24,128]{2,1,0:T(8,128)(2,1)S(1)} %all-to-all-done.recv, bf16[128,128]{1,0:T(8,128)(2,1)S(1)} %copy-done.2, f32[96,96,128]{2,1,0:T(8,128)} %conv_ends.2.first_ref), custom_call_target="tpu_custom_call" | custom-call | flops 200000000 | bytes 12000000 | tf_op jit(solution)/shard_map/scatter/pallas_call | solution.py:845
  52.6 1.5 %collective-permute-start.5 = (bf16[8,96,128]{2,1,0:T(8,128)(2,1)S(1)}, bf16[8,96,128]{2,1,0:T(8,128)(2,1)S(1)}, u32[]{:S(2)}, u32[]{:S(2)}) collective-permute-start(bf16[8,96,128]{2,1,0:T(8,128)(2,1)S(1)} %get-tuple-element.23), channel_id=1, source_target_pairs={{0,96},{32,64},{64,32},{96,0},{1,97},{33,65},{65,33},{97,1},{2,98}... | collective-permute-start | bytes 589832 | tf_op jit(solution)/shard_map/ppermute | solution.py:209
  54.2 0.1 pair_weights.3.weights
  54.3 4.0 %collective-permute-done.4.ra_ref = bf16[8,96,128]{2,1,0:T(8,128)(2,1)S(1)} collective-permute-done((bf16[8,96,128]{2,1,0:T(8,128)(2,1)S(1)}, bf16[8,96,128]{2,1,0:T(8,128)(2,1)S(1)}, u32[]{:S(2)}, u32[]{:S(2)}) %collective-permute-start.4) | collective-permute-done | bytes 196640 | tf_op jit(solution)/shard_map/ppermute | solution.py:209
  58.3 1.3 %collective-permute-done.5.rb_ref = bf16[8,96,128]{2,1,0:T(8,128)(2,1)S(1)} collective-permute-done((bf16[8,96,128]{2,1,0:T(8,128)(2,1)S(1)}, bf16[8,96,128]{2,1,0:T(8,128)(2,1)S(1)}, u32[]{:S(2)}, u32[]{:S(2)}) %collective-permute-start.5) | collective-permute-done | bytes 196640 | tf_op jit(solution)/shard_map/ppermute | solution.py:209
  59.8 3.0 %collective-permute-start.7 = (bf16[4,104,128]{2,1,0:T(8,128)(2,1)S(1)}, bf16[4,104,128]{2,1,0:T(8,128)(2,1)S(1)}, u32[]{:S(2)}, u32[]{:S(2)}) collective-permute-start(bf16[4,104,128]{2,1,0:T(8,128)(2,1)S(1)} %get-tuple-element.26), channel_id=1, source_target_pairs={{0,64},{1,2},{2,1},{3,4},{4,3},{5,6},{6,5},{7,8},{8,7},{9,10},{10,... | collective-permute-start | bytes 319496 | tf_op jit(solution)/shard_map/ppermute | solution.py:224
  62.8 6.3 %conv_core.1._ = bf16[96,96,128]{2,1,0:T(8,128)(2,1)} custom-call(bf16[96,96,128]{2,1,0:T(8,128)(2,1)S(1)} %get-tuple-element.21.grid_ref, bf16[1536,256]{1,0:T(8,128)(2,1)S(1)} %pair_weights.3.weights, f32[1,128]{1,0:T(1,128)S(1)} %bitcast.10, bf16[96,96,128]{2,1,0:T(8,128)(2,1)} %rest_0_.1), custom_call_target="tpu_custom_call" | custom-call | flops 2516582400 | bytes 4000000 | tf_op jit(solution)/shard_map/conv_core/pallas_call | solution.py:476
  69.1 2.0 %conv_columns.1.rest_1_ = bf16[96,96,128]{2,1,0:T(8,128)(2,1)} custom-call(bf16[96,96,128]{2,1,0:T(8,128)(2,1)S(1)} %get-tuple-element.21.grid_ref, bf16[8,96,128]{2,1,0:T(8,128)(2,1)S(1)} %collective-permute-done.4.ra_ref, bf16[8,96,128]{2,1,0:T(8,128)(2,1)S(1)} %collective-permute-done.5.rb_ref, ...), custom_call_target="tpu_custom_call", output_to_operand_aliasing={{}: (6, {})} | custom-call | flops 503316480 | bytes 2000000 | tf_op jit(solution)/shard_map/conv_columns/pallas_call | solution.py:565
  71.1 3.4 %conv_ends.3 = bf16[96,96,128]{2,1,0:T(8,128)(2,1)} custom-call(s32[2,4]{1,0:T(2,128)S(1)} %bitcast.7, s32[2,4]{1,0:T(2,128)S(1)} %bitcast.9, bf16[96,96,128]{2,1,0:T(8,128)(2,1)S(1)} %get-tuple-element.21.grid_ref, bf16[8,96,128]{2,1,0:T(8,128)(2,1)S(1)} %collective-permute-done.4.ra_ref, ...), custom_call_target="tpu_custom_call", output_to_operand_aliasing={{}: (10, {})} | custom-call | flops 603979776 | bytes 1000000 | tf_op jit(solution)/shard_map/conv_ends/pallas_call | solution.py:741
  (26 shorter events, 0.3 us)
Async XLA Ops:
  0.0 0.9 %copy-start.7 = (bf16[1024,128]{1,0:T(8,128)(2,1)S(1)}, bf16[1024,128]{1,0:T(8,128)(2,1)}, u32[]{:S(2)}) copy-start(bf16[1024,128]{1,0:T(8,128)(2,1)} %vals_ref.1) | copy-start | bytes 786436
  1.0 0.7 copy-start.8
  1.6 0.7 copy-start.9
  5.1 15.8 %copy-start = (bf16[9,128,128]{2,1,0:T(8,128)(2,1)S(1)}, bf16[9,128,128]{2,1,0:T(8,128)(2,1)}, u32[]{:S(2)}) copy-start(bf16[9,128,128]{2,1,0:T(8,128)(2,1)} %taps_ref.2) | copy-start | bytes 884740
  5.1 28.2 %copy-start.6 = (f32[128]{0:T(128)S(1)}, f32[128]{0:T(128)}, u32[]{:S(2)}) copy-start(f32[128]{0:T(128)} %param.13) | copy-start | bytes 1540
  5.1 39.7 %all-to-all-start = ((bf16[128,24,128]{2,1,0:T(8,128)(2,1)}), bf16[128,24,128]{2,1,0:T(8,128)(2,1)S(1)}, u32[]{:S(2)}, u32[]{:S(2)}) async-start(bf16[128,24,128]{2,1,0:T(8,128)(2,1)} %pack.1), calls=%async_computation | async-start | bytes 1572864 | tf_op jit(solution)/shard_map/all_to_all | solution.py:887
  16.8 12.3 %collective-permute-start = (bf16[4,96,128]{2,1,0:T(8,128)(2,1)S(1)}, bf16[4,96,128]{2,1,0:T(8,128)(2,1)S(1)}, u32[]{:S(2)}, u32[]{:S(2)}) collective-permute-start(bf16[4,96,128]{2,1,0:T(8,128)(2,1)S(1)} %get-tuple-element.16), channel_id=1, source_target_pairs={{0,32},{32,0},{64,96},{96,64},{1,33},{33,1},{65,97},{97,65},{2,34}... | collective-permute-start | bytes 294920 | tf_op jit(solution)/shard_map/ppermute | solution.py:209
  18.5 12.5 %collective-permute-start.1 = (bf16[4,96,128]{2,1,0:T(8,128)(2,1)S(1)}, bf16[4,96,128]{2,1,0:T(8,128)(2,1)S(1)}, u32[]{:S(2)}, u32[]{:S(2)}) collective-permute-start(bf16[4,96,128]{2,1,0:T(8,128)(2,1)S(1)} %get-tuple-element.17), channel_id=1, source_target_pairs={{0,96},{32,64},{64,32},{96,0},{1,97},{33,65},{65,33},{97,1},{2,98}... | collective-permute-start | bytes 294920 | tf_op jit(solution)/shard_map/ppermute | solution.py:209
  31.0 10.2 %collective-permute-start.2 = (bf16[2,100,128]{2,1,0:T(8,128)(2,1)S(1)}, bf16[2,100,128]{2,1,0:T(8,128)(2,1)S(1)}, u32[]{:S(2)}, u32[]{:S(2)}) collective-permute-start(bf16[2,100,128]{2,1,0:T(8,128)(2,1)S(1)} %get-tuple-element.19), channel_id=1, source_target_pairs={{0,1},{1,0},{2,3},{3,2},{4,5},{5,4},{6,7},{7,6},{8,9},{9,8},{10,11... | collective-permute-start | bytes 153608 | tf_op jit(solution)/shard_map/ppermute | solution.py:224
  31.1 10.1 %collective-permute-start.3 = (bf16[2,100,128]{2,1,0:T(8,128)(2,1)S(1)}, bf16[2,100,128]{2,1,0:T(8,128)(2,1)S(1)}, u32[]{:S(2)}, u32[]{:S(2)}) collective-permute-start(bf16[2,100,128]{2,1,0:T(8,128)(2,1)S(1)} %get-tuple-element.20), channel_id=1, source_target_pairs={{0,64},{1,2},{2,1},{3,4},{4,3},{5,6},{6,5},{7,8},{8,7},{9,10},{10,... | collective-permute-start | bytes 153608 | tf_op jit(solution)/shard_map/ppermute | solution.py:224
  33.2 8.0 %copy-start.3 = (s32[4,2]{0,1:T(2,128)S(1)}, s32[4,2]{0,1:T(2,128)}, u32[]{:S(2)}) copy-start(s32[4,2]{0,1:T(2,128)} %param.20) | copy-start | bytes 100
  33.2 8.0 %copy-start.4 = (s32[4,2]{0,1:T(2,128)S(1)}, s32[4,2]{0,1:T(2,128)}, u32[]{:S(2)}) copy-start(s32[4,2]{0,1:T(2,128)} %param.21) | copy-start | bytes 100
  41.3 3.5 %copy-start.2 = (bf16[128,128]{1,0:T(8,128)(2,1)S(1)}, bf16[128,128]{1,0:T(8,128)(2,1)}, u32[]{:S(2)}) copy-start(bf16[128,128]{1,0:T(8,128)(2,1)} %weight_ref.1) | copy-start | bytes 98308
  44.7 9.4 %copy-start.1 = (bf16[9,128,128]{2,1,0:T(8,128)(2,1)S(1)}, bf16[9,128,128]{2,1,0:T(8,128)(2,1)}, u32[]{:S(2)}) copy-start(bf16[9,128,128]{2,1,0:T(8,128)(2,1)} %taps_ref.3) | copy-start | bytes 884740
  44.7 18.1 %copy-start.5 = (f32[128]{0:T(128)S(1)}, f32[128]{0:T(128)}, u32[]{:S(2)}) copy-start(f32[128]{0:T(128)} %param.15) | copy-start | bytes 1540
  52.5 5.8 %collective-permute-start.4 = (bf16[8,96,128]{2,1,0:T(8,128)(2,1)S(1)}, bf16[8,96,128]{2,1,0:T(8,128)(2,1)S(1)}, u32[]{:S(2)}, u32[]{:S(2)}) collective-permute-start(bf16[8,96,128]{2,1,0:T(8,128)(2,1)S(1)} %get-tuple-element.22), channel_id=1, source_target_pairs={{0,32},{32,0},{64,96},{96,64},{1,33},{33,1},{65,97},{97,65},{2,34}... | collective-permute-start | bytes 589832 | tf_op jit(solution)/shard_map/ppermute | solution.py:209
  52.6 7.0 %collective-permute-start.5 = (bf16[8,96,128]{2,1,0:T(8,128)(2,1)S(1)}, bf16[8,96,128]{2,1,0:T(8,128)(2,1)S(1)}, u32[]{:S(2)}, u32[]{:S(2)}) collective-permute-start(bf16[8,96,128]{2,1,0:T(8,128)(2,1)S(1)} %get-tuple-element.23), channel_id=1, source_target_pairs={{0,96},{32,64},{64,32},{96,0},{1,97},{33,65},{65,33},{97,1},{2,98}... | collective-permute-start | bytes 589832 | tf_op jit(solution)/shard_map/ppermute | solution.py:209
  59.7 11.4 %collective-permute-start.6 = (bf16[4,104,128]{2,1,0:T(8,128)(2,1)S(1)}, bf16[4,104,128]{2,1,0:T(8,128)(2,1)S(1)}, u32[]{:S(2)}, u32[]{:S(2)}) collective-permute-start(bf16[4,104,128]{2,1,0:T(8,128)(2,1)S(1)} %get-tuple-element.25), channel_id=1, source_target_pairs={{0,1},{1,0},{2,3},{3,2},{4,5},{5,4},{6,7},{7,6},{8,9},{9,8},{10,11... | collective-permute-start | bytes 319496 | tf_op jit(solution)/shard_map/ppermute | solution.py:224
  59.8 11.3 %collective-permute-start.7 = (bf16[4,104,128]{2,1,0:T(8,128)(2,1)S(1)}, bf16[4,104,128]{2,1,0:T(8,128)(2,1)S(1)}, u32[]{:S(2)}, u32[]{:S(2)}) collective-permute-start(bf16[4,104,128]{2,1,0:T(8,128)(2,1)S(1)} %get-tuple-element.26), channel_id=1, source_target_pairs={{0,64},{1,2},{2,1},{3,4},{4,3},{5,6},{6,5},{7,8},{8,7},{9,10},{10,... | collective-permute-start | bytes 319496 | tf_op jit(solution)/shard_map/ppermute | solution.py:224

commit v5 on v4

--- a/solution.py
+++ b/solution.py
@@ -57,7 +57,6 @@
         onehot_parts.append(hit_b)
     rank = jnp.concatenate(rank_parts, axis=1).astype(I32)
     onehot = jnp.concatenate(onehot_parts, axis=1)
-    target = owner * CAP + rank
 
     cell_row = ((cell.astype(F32) + 0.5) * (1.0 / side)).astype(I32)
     cell_col = cell - cell_row * side
@@ -77,10 +76,15 @@
     send_ref[:, CAP:, :] = meta.astype(BF16)
 
     chunk_dests = 16
-    chunk = chunk_dests * CAP
+    at_rank = jnp.where(iota((CAP, rows), 0) == rank, 1.0, 0.0).astype(BF16)
     for c in range(dests // chunk_dests):
-        match = target == iota((chunk, rows), 0) + c * chunk
-        match = jnp.where(match, 1.0, 0.0).astype(BF16)
+        match = jnp.concatenate(
+            [
+                jnp.broadcast_to(onehot[t : t + 1, :], (CAP, rows)) * at_rank
+                for t in range(c * chunk_dests, (c + 1) * chunk_dests)
+            ],
+            axis=0,
+        )
         placed = jnp.dot(match, vals_ref[...], preferred_element_type=F32).astype(BF16)
         send_ref[c * chunk_dests : (c + 1) * chunk_dests, :CAP, :] = placed.reshape(
             chunk_dests, CAP, placed.shape[-1]
@@ -701,6 +705,7 @@
     starts = [(side, g * 2 * d) for side in range(2) for g in range(EDGE // (2 * d))]
     lhs = pair_rows(strip, [side * span + at for side, at in starts], d)
     y = gelu(jnp.dot(lhs, weights[...], preferred_element_type=F32) + bias2)
+    stores = []
     for g, (side, at) in enumerate(starts):
         for half in range(2):
             to = side * EDGE + at + half * d
@@ -708,14 +713,15 @@
             if has_residual:
                 piece = piece + fields[to : to + d].astype(F32)
             result[to : to + d] = piece.astype(result.dtype)
-    stores = [
-        pltpu.make_async_copy(
-            result.at[pl.ds(side * EDGE, EDGE)], out_ref.at[pl.ds(at, EDGE)], sems.at[4 + side]
-        )
-        for side, at in ((0, 0), (1, rows - EDGE))
-    ]
-    for store in stores:
-        store.start()
+        if at + 2 * d == EDGE:
+            stores.append(
+                pltpu.make_async_copy(
+                    result.at[pl.ds(side * EDGE, EDGE)],
+                    out_ref.at[pl.ds(side * (rows - EDGE), EDGE)],
+                    sems.at[4 + side],
+                )
+            )
+            stores[-1].start()
     for store in stores:
         store.wait()
 
@@ -794,14 +800,11 @@
     lax.fori_loop(0, side, clear, 0, unroll=4)
     copy.wait()
 
-    def add_rows(g, carry):
+    for g in range(sources // 8):
         for j in range(0, 128, 2):
             for k, target in ((0, even), (1, extra)):
                 c = cells_s[g, j + k]
                 target[pl.ds(c, 1), :] += enc[pl.ds(g * 128 + j + k, 1), :]
-        return carry
-
-    lax.fori_loop(0, sources // 8, add_rows, 0)
     load.wait()
 
     per = side // d

time: 74.9 us -> 74.8 us (level)
  no operation moved by 1% of the time
where the time goes in v5:
time: 74.8 us; the launch traced here: 74.4 us
  Pallas kernels  34.8 us (47%)
  starting transfers between devices  21.6 us (29%)
  waiting for transfers between devices  15.3 us (20%)
  local copies, waits for them, and re-layouts  2.36 us (3%)
    ppermute x2, waiting for transfers between devices, swap_faces(): lax.ppermute(sides[0], 'face', inner)  12.2 us
    all_to_all x1, starting transfers between devices, local(): lax.all_to_all(send, ('face', 'tile'), split_axis=0, concat_axis=0, tiled...  10.5 us
    pallas_call x1, Pallas kernels, conv_rows(): pl.pallas_call(functools.partial(rows_kernel, d, step_rows, fields is not...  7.98 us
    pallas_call x1, Pallas kernels, scatter(): pl.pallas_call(functools.partial(scatter_kernel, d), out_shape=(VMEM((sid...  7.71 us
    pallas_call x2, Pallas kernels, conv_ends(): pl.pallas_call(functools.partial(ends_kernel, d, fields is not None), out...  6.7 us
    pallas_call x1, Pallas kernels, conv_core(): pl.pallas_call(functools.partial(core_kernel, d, step_rows), out_shape=pl...  6.28 us
    ppermute x2, starting transfers between devices, swap_tiles(): lax.ppermute(wide[1], ('face', 'tile'), outer)  5.3 us
    ppermute x2, starting transfers between devices, swap_faces(): lax.ppermute(sides[1], 'face', outer)  3.87 us
  transfers between devices with their start and end apart: 9, of which 4 were waited for; matrix products, arithmetic and copies ran while one was open for 0% of the time, Pallas kernels for 28%

profile of v5, /device:TPU:6, one launch (start us, length us, event | category | flops | bytes accessed | tf_op | source)
XLA Modules:
  0.0 74.4 jit_solution(8652021117139866115)
XLA Ops:
  0.0 0.9 %copy-done.7 = bf16[1024,128]{1,0:T(8,128)(2,1)S(1)} copy-done((bf16[1024,128]{1,0:T(8,128)(2,1)S(1)}, bf16[1024,128]{1,0:T(8,128)(2,1)}, u32[]{:S(2)}) %copy-start.7) | copy-done | bytes 262168
  1.0 0.7 copy-done.8
  1.6 0.7 copy-done.9
  2.3 2.6 %pack.1 = bf16[128,24,128]{2,1,0:T(8,128)(2,1)} custom-call(s32[1,1024]{1,0:T(1,128)S(1)} %bitcast.15, s32[1,1024]{1,0:T(1,128)S(1)} %bitcast.16, bf16[1024,128]{1,0:T(8,128)(2,1)S(1)} %copy-done.7), custom_call_target="tpu_custom_call" | custom-call | flops 536870912 | bytes 2000000 | tf_op jit(solution)/shard_map/pack/pallas_call | solution.py:96
  4.9 10.5 %all-to-all-start = ((bf16[128,24,128]{2,1,0:T(8,128)(2,1)}), bf16[128,24,128]{2,1,0:T(8,128)(2,1)S(1)}, u32[]{:S(2)}, u32[]{:S(2)}) async-start(bf16[128,24,128]{2,1,0:T(8,128)(2,1)} %pack.1), calls=%async_computation | async-start | bytes 1572864 | tf_op jit(solution)/shard_map/all_to_all | solution.py:890
  15.4 1.2 %edges.1 = (bf16[4,96,128]{2,1,0:T(8,128)(2,1)S(1)}, bf16[4,96,128]{2,1,0:T(8,128)(2,1)S(1)}, bf16[2,2,96,128]{3,2,1,0:T(8,128)(2,1)S(1)}) custom-call(bf16[96,96,128]{2,1,0:T(8,128)(2,1)} %rest_0_.1), custom_call_target="tpu_custom_call" | custom-call | flops 1000000 | bytes 800000 | tf_op jit(solution)/shard_map/edges/pallas_call | solution.py:149
  16.6 1.7 %collective-permute-start = (bf16[4,96,128]{2,1,0:T(8,128)(2,1)S(1)}, bf16[4,96,128]{2,1,0:T(8,128)(2,1)S(1)}, u32[]{:S(2)}, u32[]{:S(2)}) collective-permute-start(bf16[4,96,128]{2,1,0:T(8,128)(2,1)S(1)} %get-tuple-element.16), channel_id=1, source_target_pairs={{0,32},{32,0},{64,96},{96,64},{1,33},{33,1},{65,97},{97,65},{2,34}... | collective-permute-start | bytes 294920 | tf_op jit(solution)/shard_map/ppermute | solution.py:213
  18.3 2.3 %collective-permute-start.1 = (bf16[4,96,128]{2,1,0:T(8,128)(2,1)S(1)}, bf16[4,96,128]{2,1,0:T(8,128)(2,1)S(1)}, u32[]{:S(2)}, u32[]{:S(2)}) collective-permute-start(bf16[4,96,128]{2,1,0:T(8,128)(2,1)S(1)} %get-tuple-element.17), channel_id=1, source_target_pairs={{0,96},{32,64},{64,32},{96,0},{1,97},{33,65},{65,33},{97,1},{2,98}... | collective-permute-start | bytes 294920 | tf_op jit(solution)/shard_map/ppermute | solution.py:213
  20.6 0.1 pair_weights.2.weights
  20.7 8.1 %collective-permute-done.ra_ref = bf16[4,96,128]{2,1,0:T(8,128)(2,1)S(1)} collective-permute-done((bf16[4,96,128]{2,1,0:T(8,128)(2,1)S(1)}, bf16[4,96,128]{2,1,0:T(8,128)(2,1)S(1)}, u32[]{:S(2)}, u32[]{:S(2)}) %collective-permute-start) | collective-permute-done | bytes 98336 | tf_op jit(solution)/shard_map/ppermute | solution.py:213
  28.9 1.9 %collective-permute-done.1.rb_ref = bf16[4,96,128]{2,1,0:T(8,128)(2,1)S(1)} collective-permute-done((bf16[4,96,128]{2,1,0:T(8,128)(2,1)S(1)}, bf16[4,96,128]{2,1,0:T(8,128)(2,1)S(1)}, u32[]{:S(2)}, u32[]{:S(2)}) %collective-permute-start.1) | collective-permute-done | bytes 98336 | tf_op jit(solution)/shard_map/ppermute | solution.py:213
  30.8 0.1 collective-permute-start.2
  30.9 2.1 %collective-permute-start.3 = (bf16[2,100,128]{2,1,0:T(8,128)(2,1)S(1)}, bf16[2,100,128]{2,1,0:T(8,128)(2,1)S(1)}, u32[]{:S(2)}, u32[]{:S(2)}) collective-permute-start(bf16[2,100,128]{2,1,0:T(8,128)(2,1)S(1)} %get-tuple-element.20), channel_id=1, source_target_pairs={{0,64},{1,2},{2,1},{3,4},{4,3},{5,6},{6,5},{7,8},{8,7},{9,10},{10,... | collective-permute-start | bytes 153608 | tf_op jit(solution)/shard_map/ppermute | solution.py:228
  33.0 8.0 %conv_rows.1.rest_0_ = f32[96,96,128]{2,1,0:T(8,128)} custom-call(bf16[96,96,128]{2,1,0:T(8,128)(2,1)} %rest_0_.1, bf16[4,96,128]{2,1,0:T(8,128)(2,1)S(1)} %collective-permute-done.ra_ref, bf16[4,96,128]{2,1,0:T(8,128)(2,1)S(1)} %collective-permute-done.1.rb_ref, bf16[1536,256]{1,0:T(8,128)(2,1)S(1)} %pair_weights.2.weights, f32[1,128]{1,0:T(1,128)S(1)} %bitcast.13), custom_call_target="tpu_custom_call" | custom-call | flops 3623878656 | bytes 9000000 | tf_op jit(solution)/shard_map/conv_rows/pallas_call | solution.py:395
  41.1 3.3 %conv_ends.2.first_ref = f32[96,96,128]{2,1,0:T(8,128)} custom-call(s32[2,4]{1,0:T(2,128)S(1)} %bitcast.6, s32[2,4]{1,0:T(2,128)S(1)} %bitcast.8, bf16[96,96,128]{2,1,0:T(8,128)(2,1)} %rest_0_.1, bf16[4,96,128]{2,1,0:T(8,128)(2,1)S(1)} %collective-permute-done.ra_ref, ...), custom_call_target="tpu_custom_call", output_to_operand_aliasing={{}: (9, {})} | custom-call | flops 603979776 | bytes 1000000 | tf_op jit(solution)/shard_map/conv_ends/pallas_call | solution.py:747
  44.5 7.7 %scatter.1 = (bf16[96,96,128]{2,1,0:T(8,128)(2,1)S(1)}, bf16[8,96,128]{2,1,0:T(8,128)(2,1)S(1)}, bf16[8,96,128]{2,1,0:T(8,128)(2,1)S(1)}, bf16[2,4,96,128]{3,2,1,0:T(8,128)(2,1)S(1)}) custom-call(bf16[128,24,128]{2,1,0:T(8,128)(2,1)S(1)} %all-to-all-done.recv, bf16[128,128]{1,0:T(8,128)(2,1)S(1)} %copy-done.2, f32[96,96,128]{2,1,0:T(8,128)} %conv_ends.2.first_ref), custom_call_target="tpu_custom_call" | custom-call | flops 200000000 | bytes 12000000 | tf_op jit(solution)/shard_map/scatter/pallas_call | solution.py:848
  52.3 1.5 %collective-permute-start.5 = (bf16[8,96,128]{2,1,0:T(8,128)(2,1)S(1)}, bf16[8,96,128]{2,1,0:T(8,128)(2,1)S(1)}, u32[]{:S(2)}, u32[]{:S(2)}) collective-permute-start(bf16[8,96,128]{2,1,0:T(8,128)(2,1)S(1)} %get-tuple-element.23), channel_id=1, source_target_pairs={{0,96},{32,64},{64,32},{96,0},{1,97},{33,65},{65,33},{97,1},{2,98}... | collective-permute-start | bytes 589832 | tf_op jit(solution)/shard_map/ppermute | solution.py:213
  53.8 0.1 pair_weights.3.weights
  53.9 4.0 %collective-permute-done.4.ra_ref = bf16[8,96,128]{2,1,0:T(8,128)(2,1)S(1)} collective-permute-done((bf16[8,96,128]{2,1,0:T(8,128)(2,1)S(1)}, bf16[8,96,128]{2,1,0:T(8,128)(2,1)S(1)}, u32[]{:S(2)}, u32[]{:S(2)}) %collective-permute-start.4) | collective-permute-done | bytes 196640 | tf_op jit(solution)/shard_map/ppermute | solution.py:213
  57.9 1.3 %collective-permute-done.5.rb_ref = bf16[8,96,128]{2,1,0:T(8,128)(2,1)S(1)} collective-permute-done((bf16[8,96,128]{2,1,0:T(8,128)(2,1)S(1)}, bf16[8,96,128]{2,1,0:T(8,128)(2,1)S(1)}, u32[]{:S(2)}, u32[]{:S(2)}) %collective-permute-start.5) | collective-permute-done | bytes 196640 | tf_op jit(solution)/shard_map/ppermute | solution.py:213
  59.4 3.2 %collective-permute-start.7 = (bf16[4,104,128]{2,1,0:T(8,128)(2,1)S(1)}, bf16[4,104,128]{2,1,0:T(8,128)(2,1)S(1)}, u32[]{:S(2)}, u32[]{:S(2)}) collective-permute-start(bf16[4,104,128]{2,1,0:T(8,128)(2,1)S(1)} %get-tuple-element.26), channel_id=1, source_target_pairs={{0,64},{1,2},{2,1},{3,4},{4,3},{5,6},{6,5},{7,8},{8,7},{9,10},{10,... | collective-permute-start | bytes 319496 | tf_op jit(solution)/shard_map/ppermute | solution.py:228
  62.6 6.3 %conv_core.1._ = bf16[96,96,128]{2,1,0:T(8,128)(2,1)} custom-call(bf16[96,96,128]{2,1,0:T(8,128)(2,1)S(1)} %get-tuple-element.21.grid_ref, bf16[1536,256]{1,0:T(8,128)(2,1)S(1)} %pair_weights.3.weights, f32[1,128]{1,0:T(1,128)S(1)} %bitcast.10, bf16[96,96,128]{2,1,0:T(8,128)(2,1)} %rest_0_.1), custom_call_target="tpu_custom_call" | custom-call | flops 2516582400 | bytes 4000000 | tf_op jit(solution)/shard_map/conv_core/pallas_call | solution.py:480
  68.9 2.0 %conv_columns.1.rest_1_ = bf16[96,96,128]{2,1,0:T(8,128)(2,1)} custom-call(bf16[96,96,128]{2,1,0:T(8,128)(2,1)S(1)} %get-tuple-element.21.grid_ref, bf16[8,96,128]{2,1,0:T(8,128)(2,1)S(1)} %collective-permute-done.4.ra_ref, bf16[8,96,128]{2,1,0:T(8,128)(2,1)S(1)} %collective-permute-done.5.rb_ref, ...), custom_call_target="tpu_custom_call", output_to_operand_aliasing={{}: (6, {})} | custom-call | flops 503316480 | bytes 2000000 | tf_op jit(solution)/shard_map/conv_columns/pallas_call | solution.py:569
  70.9 3.4 %conv_ends.3 = bf16[96,96,128]{2,1,0:T(8,128)(2,1)} custom-call(s32[2,4]{1,0:T(2,128)S(1)} %bitcast.7, s32[2,4]{1,0:T(2,128)S(1)} %bitcast.9, bf16[96,96,128]{2,1,0:T(8,128)(2,1)S(1)} %get-tuple-element.21.grid_ref, bf16[8,96,128]{2,1,0:T(8,128)(2,1)S(1)} %collective-permute-done.4.ra_ref, ...), custom_call_target="tpu_custom_call", output_to_operand_aliasing={{}: (10, {})} | custom-call | flops 603979776 | bytes 1000000 | tf_op jit(solution)/shard_map/conv_ends/pallas_call | solution.py:747
  (26 shorter events, 0.3 us)
Async XLA Ops:
  0.0 0.9 %copy-start.7 = (bf16[1024,128]{1,0:T(8,128)(2,1)S(1)}, bf16[1024,128]{1,0:T(8,128)(2,1)}, u32[]{:S(2)}) copy-start(bf16[1024,128]{1,0:T(8,128)(2,1)} %vals_ref.1) | copy-start | bytes 786436
  1.0 0.7 copy-start.8
  1.6 0.7 copy-start.9
  4.9 15.7 %copy-start = (bf16[9,128,128]{2,1,0:T(8,128)(2,1)S(1)}, bf16[9,128,128]{2,1,0:T(8,128)(2,1)}, u32[]{:S(2)}) copy-start(bf16[9,128,128]{2,1,0:T(8,128)(2,1)} %taps_ref.2) | copy-start | bytes 884740
  4.9 28.1 %copy-start.6 = (f32[128]{0:T(128)S(1)}, f32[128]{0:T(128)}, u32[]{:S(2)}) copy-start(f32[128]{0:T(128)} %param.13) | copy-start | bytes 1540
  4.9 39.5 %all-to-all-start = ((bf16[128,24,128]{2,1,0:T(8,128)(2,1)}), bf16[128,24,128]{2,1,0:T(8,128)(2,1)S(1)}, u32[]{:S(2)}, u32[]{:S(2)}) async-start(bf16[128,24,128]{2,1,0:T(8,128)(2,1)} %pack.1), calls=%async_computation | async-start | bytes 1572864 | tf_op jit(solution)/shard_map/all_to_all | solution.py:890
  16.6 12.3 %collective-permute-start = (bf16[4,96,128]{2,1,0:T(8,128)(2,1)S(1)}, bf16[4,96,128]{2,1,0:T(8,128)(2,1)S(1)}, u32[]{:S(2)}, u32[]{:S(2)}) collective-permute-start(bf16[4,96,128]{2,1,0:T(8,128)(2,1)S(1)} %get-tuple-element.16), channel_id=1, source_target_pairs={{0,32},{32,0},{64,96},{96,64},{1,33},{33,1},{65,97},{97,65},{2,34}... | collective-permute-start | bytes 294920 | tf_op jit(solution)/shard_map/ppermute | solution.py:213
  18.3 12.5 %collective-permute-start.1 = (bf16[4,96,128]{2,1,0:T(8,128)(2,1)S(1)}, bf16[4,96,128]{2,1,0:T(8,128)(2,1)S(1)}, u32[]{:S(2)}, u32[]{:S(2)}) collective-permute-start(bf16[4,96,128]{2,1,0:T(8,128)(2,1)S(1)} %get-tuple-element.17), channel_id=1, source_target_pairs={{0,96},{32,64},{64,32},{96,0},{1,97},{33,65},{65,33},{97,1},{2,98}... | collective-permute-start | bytes 294920 | tf_op jit(solution)/shard_map/ppermute | solution.py:213
  30.8 10.2 %collective-permute-start.2 = (bf16[2,100,128]{2,1,0:T(8,128)(2,1)S(1)}, bf16[2,100,128]{2,1,0:T(8,128)(2,1)S(1)}, u32[]{:S(2)}, u32[]{:S(2)}) collective-permute-start(bf16[2,100,128]{2,1,0:T(8,128)(2,1)S(1)} %get-tuple-element.19), channel_id=1, source_target_pairs={{0,1},{1,0},{2,3},{3,2},{4,5},{5,4},{6,7},{7,6},{8,9},{9,8},{10,11... | collective-permute-start | bytes 153608 | tf_op jit(solution)/shard_map/ppermute | solution.py:228
  30.9 10.1 %collective-permute-start.3 = (bf16[2,100,128]{2,1,0:T(8,128)(2,1)S(1)}, bf16[2,100,128]{2,1,0:T(8,128)(2,1)S(1)}, u32[]{:S(2)}, u32[]{:S(2)}) collective-permute-start(bf16[2,100,128]{2,1,0:T(8,128)(2,1)S(1)} %get-tuple-element.20), channel_id=1, source_target_pairs={{0,64},{1,2},{2,1},{3,4},{4,3},{5,6},{6,5},{7,8},{8,7},{9,10},{10,... | collective-permute-start | bytes 153608 | tf_op jit(solution)/shard_map/ppermute | solution.py:228
  33.0 8.0 %copy-start.3 = (s32[4,2]{0,1:T(2,128)S(1)}, s32[4,2]{0,1:T(2,128)}, u32[]{:S(2)}) copy-start(s32[4,2]{0,1:T(2,128)} %param.20) | copy-start | bytes 100
  33.0 8.0 %copy-start.4 = (s32[4,2]{0,1:T(2,128)S(1)}, s32[4,2]{0,1:T(2,128)}, u32[]{:S(2)}) copy-start(s32[4,2]{0,1:T(2,128)} %param.21) | copy-start | bytes 100
  41.1 3.4 %copy-start.2 = (bf16[128,128]{1,0:T(8,128)(2,1)S(1)}, bf16[128,128]{1,0:T(8,128)(2,1)}, u32[]{:S(2)}) copy-start(bf16[128,128]{1,0:T(8,128)(2,1)} %weight_ref.1) | copy-start | bytes 98308
  44.4 9.4 %copy-start.1 = (bf16[9,128,128]{2,1,0:T(8,128)(2,1)S(1)}, bf16[9,128,128]{2,1,0:T(8,128)(2,1)}, u32[]{:S(2)}) copy-start(bf16[9,128,128]{2,1,0:T(8,128)(2,1)} %taps_ref.3) | copy-start | bytes 884740
  44.4 18.2 %copy-start.5 = (f32[128]{0:T(128)S(1)}, f32[128]{0:T(128)}, u32[]{:S(2)}) copy-start(f32[128]{0:T(128)} %param.15) | copy-start | bytes 1540
  52.2 5.8 %collective-permute-start.4 = (bf16[8,96,128]{2,1,0:T(8,128)(2,1)S(1)}, bf16[8,96,128]{2,1,0:T(8,128)(2,1)S(1)}, u32[]{:S(2)}, u32[]{:S(2)}) collective-permute-start(bf16[8,96,128]{2,1,0:T(8,128)(2,1)S(1)} %get-tuple-element.22), channel_id=1, source_target_pairs={{0,32},{32,0},{64,96},{96,64},{1,33},{33,1},{65,97},{97,65},{2,34}... | collective-permute-start | bytes 589832 | tf_op jit(solution)/shard_map/ppermute | solution.py:213
  52.3 7.0 %collective-permute-start.5 = (bf16[8,96,128]{2,1,0:T(8,128)(2,1)S(1)}, bf16[8,96,128]{2,1,0:T(8,128)(2,1)S(1)}, u32[]{:S(2)}, u32[]{:S(2)}) collective-permute-start(bf16[8,96,128]{2,1,0:T(8,128)(2,1)S(1)} %get-tuple-element.23), channel_id=1, source_target_pairs={{0,96},{32,64},{64,32},{96,0},{1,97},{33,65},{65,33},{97,1},{2,98}... | collective-permute-start | bytes 589832 | tf_op jit(solution)/shard_map/ppermute | solution.py:213
  59.3 11.6 %collective-permute-start.6 = (bf16[4,104,128]{2,1,0:T(8,128)(2,1)S(1)}, bf16[4,104,128]{2,1,0:T(8,128)(2,1)S(1)}, u32[]{:S(2)}, u32[]{:S(2)}) collective-permute-start(bf16[4,104,128]{2,1,0:T(8,128)(2,1)S(1)} %get-tuple-element.25), channel_id=1, source_target_pairs={{0,1},{1,0},{2,3},{3,2},{4,5},{5,4},{6,7},{7,6},{8,9},{9,8},{10,11... | collective-permute-start | bytes 319496 | tf_op jit(solution)/shard_map/ppermute | solution.py:228
  59.4 11.5 %collective-permute-start.7 = (bf16[4,104,128]{2,1,0:T(8,128)(2,1)S(1)}, bf16[4,104,128]{2,1,0:T(8,128)(2,1)S(1)}, u32[]{:S(2)}, u32[]{:S(2)}) collective-permute-start(bf16[4,104,128]{2,1,0:T(8,128)(2,1)S(1)} %get-tuple-element.26), channel_id=1, source_target_pairs={{0,64},{1,2},{2,1},{3,4},{4,3},{5,6},{6,5},{7,8},{8,7},{9,10},{10,... | collective-permute-start | bytes 319496 | tf_op jit(solution)/shard_map/ppermute | solution.py:228

commit v6 on v5

--- a/solution.py
+++ b/solution.py
@@ -498,7 +498,7 @@
     )(keep(grid), keep(weights), bias.reshape(1, ch), far(fields))
 
 
-def columns_kernel(d, grid_ref, ra_ref, rb_ref, weights, bias_ref, fields_ref, _, out_ref, strip, result, sems, fields):
+def columns_kernel(d, grid_ref, ra_ref, rb_ref, weights, bias_ref, fields_ref, _, out_ref, own_ref, strip, result, sems, fields):
     rows, cols, ch = grid_ref.shape
     _, _, face_even, _ = parities()
     inner = rows - 2 * EDGE
@@ -559,18 +559,31 @@
     ]
     for store in stores:
         store.start()
+    own = EDGE + d
+    for low_row, high_row, to in ((0, own, 0), (rows - own, rows, own)):
+        for t in range(low_row // group, high_row // group):
+            p, at = divmod(t, per_plane)
+            west, east = side_tile(ra_ref, rb_ref, p, slice(at * 8, at * 8 + 8), face_even)
+            for k in range(group):
+                row = t * group + k
+                target = own_ref.at[row - low_row + to]
+                target[:, ch : 2 * ch] = grid_ref[row]
+                shifted_copies(target, west[k * d : (k + 1) * d], east[k * d : (k + 1) * d], d)
     for store in stores:
         store.wait()
 
 
 def conv_columns(out, grid, sides, weights, bias, d, fields):
-    rows, _, ch = grid.shape
+    rows, cols, ch = grid.shape
     inner = rows - 2 * EDGE
     return pl.pallas_call(
         functools.partial(columns_kernel, d),
-        out_shape=pltpu.HBM(out.shape, out.dtype),
+        out_shape=(
+            pltpu.HBM(out.shape, out.dtype),
+            VMEM((2 * (EDGE + d), cols, 3 * ch), BF16),
+        ),
         in_specs=[full_spec()] * 5 + [full_spec(pl.ANY)] * 2,
-        out_specs=full_spec(pl.ANY),
+        out_specs=(full_spec(pl.ANY), full_spec()),
         scratch_shapes=[
             VMEM((inner + 2 * d, 2 * EDGE, 3 * ch), BF16),
             VMEM((inner, 2 * EDGE, ch), BF16),
@@ -603,7 +616,7 @@
     *rest,
 ):
     if has_residual:
-        fields_ref, _, out_ref, strip, wide, result, sems, fields = rest
+        fields_ref, own_ref, _, out_ref, strip, wide, result, sems, fields = rest
     else:
         _, out_ref, strip, wide, result, sems = rest
     rows, cols, ch = grid_ref.shape
@@ -613,7 +626,7 @@
     span = EDGE + 2 * d
     own = EDGE + d
     loads = []
-    for side, at, to in ((0, 0, d), (1, rows - own, span)):
+    for side, at, to in () if has_residual else ((0, 0, d), (1, rows - own, span)):
         loads.append(
             pltpu.make_async_copy(
                 grid_ref.at[pl.ds(at, own)],
@@ -645,7 +658,10 @@
         which = jnp.where(tile == 0, 0, 1)
         sector = neighbor_ref[which, face]
         flip = reversal_ref[which, face]
-        mine = jnp.where(tile == 0, d, span + EDGE)
+        if has_residual:
+            mine = jnp.where(tile == 0, 0, own + EDGE)
+        else:
+            mine = jnp.where(tile == 0, d, span + EDGE)
         width = cols + 2 * d
 
         def source_index(s):
@@ -669,7 +685,7 @@
         for r in range(d):
             source = jnp.concatenate(
                 [
-                    strip[mine + r, :, ch : 2 * ch],
+                    (own_ref if has_residual else strip)[mine + r, :, ch : 2 * ch],
                     ra_ref[d + r],
                     rb_ref[d + r],
                     wb_ref[r, d : d + cols, :],
@@ -685,7 +701,7 @@
 
     group = 8 // d
     per_plane = cols // 8
-    for low, high, to in ((0, own, d), (rows - own, rows, span)):
+    for low, high, to in () if has_residual else ((0, own, d), (rows - own, rows, span)):
         for t in range(low // group, -(-high // group)):
             p, at = divmod(t, per_plane)
             west, east = side_tile(ra_ref, rb_ref, p, slice(at * 8, at * 8 + 8), face_even)
@@ -703,7 +719,23 @@
     bias2 = jnp.concatenate([bias, bias], axis=1)
     m = d * cols
     starts = [(side, g * 2 * d) for side in range(2) for g in range(EDGE // (2 * d))]
-    lhs = pair_rows(strip, [side * span + at for side, at in starts], d)
+    if has_residual:
+        parts = []
+        for a in range(4):
+            of_a = []
+            for side, at in starts:
+                at = at + a * d
+                inside = d <= at if side == 0 else at < own
+                if inside:
+                    here = side * own + at - (0 if side else d)
+                    slab = own_ref[here : here + d]
+                else:
+                    slab = strip[side * span + at : side * span + at + d]
+                of_a.append(slab.reshape(m, 3 * ch))
+            parts.append(jnp.concatenate(of_a, axis=0))
+        lhs = jnp.concatenate(parts, axis=1)
+    else:
+        lhs = pair_rows(strip, [side * span + at for side, at in starts], d)
     y = gelu(jnp.dot(lhs, weights[...], preferred_element_type=F32) + bias2)
     stores = []
     for g, (side, at) in enumerate(starts):
@@ -726,7 +758,7 @@
         store.wait()
 
 
-def conv_ends(out, grid, sides, wide, neighbor, reversal, weights, bias, d, fields):
+def conv_ends(out, grid, sides, wide, neighbor, reversal, weights, bias, d, fields, own=None):
     _, cols, ch = grid.shape
     operands = [neighbor.T, reversal.T, far(grid) if fields is None else keep(grid)]
     operands += [keep(x) for x in (*sides, *wide, weights)] + [bias.reshape(1, ch)]
@@ -742,6 +774,8 @@
         operands.append(far(fields))
         in_specs.append(full_spec(pl.ANY))
         scratch.append(VMEM((2 * EDGE, cols, ch), BF16))
+        operands.append(keep(own))
+        in_specs.append(full_spec())
     operands.append(far(out))
     in_specs.append(full_spec(pl.ANY))
     return pl.pallas_call(
@@ -900,10 +934,10 @@
     sides = swap_faces((a, b))
     out = conv_core(mixed, weights, second_conv_bias, d, fields)
     wide = swap_tiles(widen(ends, sides, d))
-    out = conv_columns(out, mixed, sides, weights, second_conv_bias, d, fields)
+    out, own = conv_columns(out, mixed, sides, weights, second_conv_bias, d, fields)
     return conv_ends(
         out, mixed, sides, wide, polar_neighbor_sector, polar_link_reversal,
-        weights, second_conv_bias, d, fields,
+        weights, second_conv_bias, d, fields, own,
     )
 
 

time: 74.8 us -> 74.7 us (level)
  no operation moved by 1% of the time
where the time goes in v6:
time: 74.7 us; the launch traced here: 74.4 us
  Pallas kernels  34.7 us (46%)
  starting transfers between devices  21.6 us (29%)
  waiting for transfers between devices  15.3 us (20%)
  local copies, waits for them, and re-layouts  2.36 us (3%)
    ppermute x2, waiting for transfers between devices, swap_faces(): lax.ppermute(sides[0], 'face', inner)  12.2 us
    all_to_all x1, starting transfers between devices, local(): lax.all_to_all(send, ('face', 'tile'), split_axis=0, concat_axis=0, tiled...  10.5 us
    pallas_call x1, Pallas kernels, conv_rows(): pl.pallas_call(functools.partial(rows_kernel, d, step_rows, fields is not...  7.99 us
    pallas_call x1, Pallas kernels, scatter(): pl.pallas_call(functools.partial(scatter_kernel, d), out_shape=(VMEM((sid...  7.72 us
    pallas_call x2, Pallas kernels, conv_ends(): pl.pallas_call(functools.partial(ends_kernel, d, fields is not None), out...  6.55 us
    pallas_call x1, Pallas kernels, conv_core(): pl.pallas_call(functools.partial(core_kernel, d, step_rows), out_shape=pl...  6.3 us
    ppermute x2, starting transfers between devices, swap_tiles(): lax.ppermute(wide[1], ('face', 'tile'), outer)  5.3 us
    ppermute x2, starting transfers between devices, swap_faces(): lax.ppermute(sides[1], 'face', outer)  3.87 us
  transfers between devices with their start and end apart: 9, of which 4 were waited for; matrix products, arithmetic and copies ran while one was open for 0% of the time, Pallas kernels for 28%

profile of v6, /device:TPU:6, one launch (start us, length us, event | category | flops | bytes accessed | tf_op | source)
XLA Modules:
  0.0 74.4 jit_solution(389197293788751866)
XLA Ops:
  0.0 0.9 %copy-done.7 = bf16[1024,128]{1,0:T(8,128)(2,1)S(1)} copy-done((bf16[1024,128]{1,0:T(8,128)(2,1)S(1)}, bf16[1024,128]{1,0:T(8,128)(2,1)}, u32[]{:S(2)}) %copy-start.7) | copy-done | bytes 262168
  1.0 0.7 copy-done.8
  1.6 0.7 copy-done.9
  2.3 2.6 %pack.1 = bf16[128,24,128]{2,1,0:T(8,128)(2,1)} custom-call(s32[1,1024]{1,0:T(1,128)S(1)} %bitcast.15, s32[1,1024]{1,0:T(1,128)S(1)} %bitcast.16, bf16[1024,128]{1,0:T(8,128)(2,1)S(1)} %copy-done.7), custom_call_target="tpu_custom_call" | custom-call | flops 536870912 | bytes 2000000 | tf_op jit(solution)/shard_map/pack/pallas_call | solution.py:96
  4.9 10.5 %all-to-all-start = ((bf16[128,24,128]{2,1,0:T(8,128)(2,1)}), bf16[128,24,128]{2,1,0:T(8,128)(2,1)S(1)}, u32[]{:S(2)}, u32[]{:S(2)}) async-start(bf16[128,24,128]{2,1,0:T(8,128)(2,1)} %pack.1), calls=%async_computation | async-start | bytes 1572864 | tf_op jit(solution)/shard_map/all_to_all | solution.py:924
  15.4 1.2 %edges.1 = (bf16[4,96,128]{2,1,0:T(8,128)(2,1)S(1)}, bf16[4,96,128]{2,1,0:T(8,128)(2,1)S(1)}, bf16[2,2,96,128]{3,2,1,0:T(8,128)(2,1)S(1)}) custom-call(bf16[96,96,128]{2,1,0:T(8,128)(2,1)} %rest_0_.1), custom_call_target="tpu_custom_call" | custom-call | flops 1000000 | bytes 800000 | tf_op jit(solution)/shard_map/edges/pallas_call | solution.py:149
  16.6 1.7 %collective-permute-start = (bf16[4,96,128]{2,1,0:T(8,128)(2,1)S(1)}, bf16[4,96,128]{2,1,0:T(8,128)(2,1)S(1)}, u32[]{:S(2)}, u32[]{:S(2)}) collective-permute-start(bf16[4,96,128]{2,1,0:T(8,128)(2,1)S(1)} %get-tuple-element.18), channel_id=1, source_target_pairs={{0,32},{32,0},{64,96},{96,64},{1,33},{33,1},{65,97},{97,65},{2,34}... | collective-permute-start | bytes 294920 | tf_op jit(solution)/shard_map/ppermute | solution.py:213
  18.3 2.3 %collective-permute-start.1 = (bf16[4,96,128]{2,1,0:T(8,128)(2,1)S(1)}, bf16[4,96,128]{2,1,0:T(8,128)(2,1)S(1)}, u32[]{:S(2)}, u32[]{:S(2)}) collective-permute-start(bf16[4,96,128]{2,1,0:T(8,128)(2,1)S(1)} %get-tuple-element.19), channel_id=1, source_target_pairs={{0,96},{32,64},{64,32},{96,0},{1,97},{33,65},{65,33},{97,1},{2,98}... | collective-permute-start | bytes 294920 | tf_op jit(solution)/shard_map/ppermute | solution.py:213
  20.6 0.1 pair_weights.2.weights
  20.7 8.1 %collective-permute-done.ra_ref = bf16[4,96,128]{2,1,0:T(8,128)(2,1)S(1)} collective-permute-done((bf16[4,96,128]{2,1,0:T(8,128)(2,1)S(1)}, bf16[4,96,128]{2,1,0:T(8,128)(2,1)S(1)}, u32[]{:S(2)}, u32[]{:S(2)}) %collective-permute-start) | collective-permute-done | bytes 98336 | tf_op jit(solution)/shard_map/ppermute | solution.py:213
  28.9 1.9 %collective-permute-done.1.rb_ref = bf16[4,96,128]{2,1,0:T(8,128)(2,1)S(1)} collective-permute-done((bf16[4,96,128]{2,1,0:T(8,128)(2,1)S(1)}, bf16[4,96,128]{2,1,0:T(8,128)(2,1)S(1)}, u32[]{:S(2)}, u32[]{:S(2)}) %collective-permute-start.1) | collective-permute-done | bytes 98336 | tf_op jit(solution)/shard_map/ppermute | solution.py:213
  30.8 0.1 collective-permute-start.2
  30.9 2.1 %collective-permute-start.3 = (bf16[2,100,128]{2,1,0:T(8,128)(2,1)S(1)}, bf16[2,100,128]{2,1,0:T(8,128)(2,1)S(1)}, u32[]{:S(2)}, u32[]{:S(2)}) collective-permute-start(bf16[2,100,128]{2,1,0:T(8,128)(2,1)S(1)} %get-tuple-element.22), channel_id=1, source_target_pairs={{0,64},{1,2},{2,1},{3,4},{4,3},{5,6},{6,5},{7,8},{8,7},{9,10},{10,... | collective-permute-start | bytes 153608 | tf_op jit(solution)/shard_map/ppermute | solution.py:228
  33.0 8.0 %conv_rows.1.rest_0_ = f32[96,96,128]{2,1,0:T(8,128)} custom-call(bf16[96,96,128]{2,1,0:T(8,128)(2,1)} %rest_0_.1, bf16[4,96,128]{2,1,0:T(8,128)(2,1)S(1)} %collective-permute-done.ra_ref, bf16[4,96,128]{2,1,0:T(8,128)(2,1)S(1)} %collective-permute-done.1.rb_ref, bf16[1536,256]{1,0:T(8,128)(2,1)S(1)} %pair_weights.2.weights, f32[1,128]{1,0:T(1,128)S(1)} %bitcast.13), custom_call_target="tpu_custom_call" | custom-call | flops 3623878656 | bytes 9000000 | tf_op jit(solution)/shard_map/conv_rows/pallas_call | solution.py:395
  41.1 3.3 %conv_ends.2.first_ref = f32[96,96,128]{2,1,0:T(8,128)} custom-call(s32[2,4]{1,0:T(2,128)S(1)} %bitcast.6, s32[2,4]{1,0:T(2,128)S(1)} %bitcast.8, bf16[96,96,128]{2,1,0:T(8,128)(2,1)} %rest_0_.1, bf16[4,96,128]{2,1,0:T(8,128)(2,1)S(1)} %collective-permute-done.ra_ref, ...), custom_call_target="tpu_custom_call", output_to_operand_aliasing={{}: (9, {})} | custom-call | flops 603979776 | bytes 1000000 | tf_op jit(solution)/shard_map/conv_ends/pallas_call | solution.py:781
  44.5 7.7 %scatter.1 = (bf16[96,96,128]{2,1,0:T(8,128)(2,1)S(1)}, bf16[8,96,128]{2,1,0:T(8,128)(2,1)S(1)}, bf16[8,96,128]{2,1,0:T(8,128)(2,1)S(1)}, bf16[2,4,96,128]{3,2,1,0:T(8,128)(2,1)S(1)}) custom-call(bf16[128,24,128]{2,1,0:T(8,128)(2,1)S(1)} %all-to-all-done.recv, bf16[128,128]{1,0:T(8,128)(2,1)S(1)} %copy-done.2, f32[96,96,128]{2,1,0:T(8,128)} %conv_ends.2.first_ref), custom_call_target="tpu_custom_call" | custom-call | flops 200000000 | bytes 12000000 | tf_op jit(solution)/shard_map/scatter/pallas_call | solution.py:882
  52.3 1.5 %collective-permute-start.5 = (bf16[8,96,128]{2,1,0:T(8,128)(2,1)S(1)}, bf16[8,96,128]{2,1,0:T(8,128)(2,1)S(1)}, u32[]{:S(2)}, u32[]{:S(2)}) collective-permute-start(bf16[8,96,128]{2,1,0:T(8,128)(2,1)S(1)} %get-tuple-element.25), channel_id=1, source_target_pairs={{0,96},{32,64},{64,32},{96,0},{1,97},{33,65},{65,33},{97,1},{2,98}... | collective-permute-start | bytes 589832 | tf_op jit(solution)/shard_map/ppermute | solution.py:213
  53.8 0.1 pair_weights.3.weights
  53.9 4.0 %collective-permute-done.4.ra_ref = bf16[8,96,128]{2,1,0:T(8,128)(2,1)S(1)} collective-permute-done((bf16[8,96,128]{2,1,0:T(8,128)(2,1)S(1)}, bf16[8,96,128]{2,1,0:T(8,128)(2,1)S(1)}, u32[]{:S(2)}, u32[]{:S(2)}) %collective-permute-start.4) | collective-permute-done | bytes 196640 | tf_op jit(solution)/shard_map/ppermute | solution.py:213
  57.9 1.3 %collective-permute-done.5.rb_ref = bf16[8,96,128]{2,1,0:T(8,128)(2,1)S(1)} collective-permute-done((bf16[8,96,128]{2,1,0:T(8,128)(2,1)S(1)}, bf16[8,96,128]{2,1,0:T(8,128)(2,1)S(1)}, u32[]{:S(2)}, u32[]{:S(2)}) %collective-permute-start.5) | collective-permute-done | bytes 196640 | tf_op jit(solution)/shard_map/ppermute | solution.py:213
  59.4 3.2 %collective-permute-start.7 = (bf16[4,104,128]{2,1,0:T(8,128)(2,1)S(1)}, bf16[4,104,128]{2,1,0:T(8,128)(2,1)S(1)}, u32[]{:S(2)}, u32[]{:S(2)}) collective-permute-start(bf16[4,104,128]{2,1,0:T(8,128)(2,1)S(1)} %get-tuple-element.28), channel_id=1, source_target_pairs={{0,64},{1,2},{2,1},{3,4},{4,3},{5,6},{6,5},{7,8},{8,7},{9,10},{10,... | collective-permute-start | bytes 319496 | tf_op jit(solution)/shard_map/ppermute | solution.py:228
  62.6 6.3 %conv_core.1._ = bf16[96,96,128]{2,1,0:T(8,128)(2,1)} custom-call(bf16[96,96,128]{2,1,0:T(8,128)(2,1)S(1)} %get-tuple-element.23.grid_ref, bf16[1536,256]{1,0:T(8,128)(2,1)S(1)} %pair_weights.3.weights, f32[1,128]{1,0:T(1,128)S(1)} %bitcast.10, bf16[96,96,128]{2,1,0:T(8,128)(2,1)} %rest_0_.1), custom_call_target="tpu_custom_call" | custom-call | flops 2516582400 | bytes 4000000 | tf_op jit(solution)/shard_map/conv_core/pallas_call | solution.py:480
  68.9 2.0 %conv_columns.1 = (bf16[96,96,128]{2,1,0:T(8,128)(2,1)}, bf16[24,96,384]{2,1,0:T(8,128)(2,1)S(1)}) custom-call(bf16[96,96,128]{2,1,0:T(8,128)(2,1)S(1)} %get-tuple-element.23.grid_ref, bf16[8,96,128]{2,1,0:T(8,128)(2,1)S(1)} %collective-permute-done.4.ra_ref, bf16[8,96,128]{2,1,0:T(8,128)(2,1)S(1)} %collective-permute-done.5.rb_ref, ...), custom_call_target="tpu_custom_call", output_to_operand_aliasing={{0}: (6, {})} | custom-call | flops 503316480 | bytes 2000000 | tf_op jit(solution)/shard_map/conv_columns/pallas_call | solution.py:579
  71.0 3.2 %conv_ends.3 = bf16[96,96,128]{2,1,0:T(8,128)(2,1)} custom-call(s32[2,4]{1,0:T(2,128)S(1)} %bitcast.7, s32[2,4]{1,0:T(2,128)S(1)} %bitcast.9, bf16[96,96,128]{2,1,0:T(8,128)(2,1)S(1)} %get-tuple-element.23.grid_ref, bf16[8,96,128]{2,1,0:T(8,128)(2,1)S(1)} %collective-permute-done.4.ra_ref, ...), custom_call_target="tpu_custom_call", output_to_operand_aliasing={{}: (11, {})} | custom-call | flops 603979776 | bytes 1000000 | tf_op jit(solution)/shard_map/conv_ends/pallas_call | solution.py:781
  (26 shorter events, 0.3 us)
Async XLA Ops:
  0.0 0.9 %copy-start.7 = (bf16[1024,128]{1,0:T(8,128)(2,1)S(1)}, bf16[1024,128]{1,0:T(8,128)(2,1)}, u32[]{:S(2)}) copy-start(bf16[1024,128]{1,0:T(8,128)(2,1)} %vals_ref.1) | copy-start | bytes 786436
  1.0 0.7 copy-start.8
  1.6 0.7 copy-start.9
  4.9 15.7 %copy-start = (bf16[9,128,128]{2,1,0:T(8,128)(2,1)S(1)}, bf16[9,128,128]{2,1,0:T(8,128)(2,1)}, u32[]{:S(2)}) copy-start(bf16[9,128,128]{2,1,0:T(8,128)(2,1)} %taps_ref.2) | copy-start | bytes 884740
  4.9 28.1 %copy-start.6 = (f32[128]{0:T(128)S(1)}, f32[128]{0:T(128)}, u32[]{:S(2)}) copy-start(f32[128]{0:T(128)} %param.13) | copy-start | bytes 1540
  4.9 39.5 %all-to-all-start = ((bf16[128,24,128]{2,1,0:T(8,128)(2,1)}), bf16[128,24,128]{2,1,0:T(8,128)(2,1)S(1)}, u32[]{:S(2)}, u32[]{:S(2)}) async-start(bf16[128,24,128]{2,1,0:T(8,128)(2,1)} %pack.1), calls=%async_computation | async-start | bytes 1572864 | tf_op jit(solution)/shard_map/all_to_all | solution.py:924
  16.6 12.3 %collective-permute-start = (bf16[4,96,128]{2,1,0:T(8,128)(2,1)S(1)}, bf16[4,96,128]{2,1,0:T(8,128)(2,1)S(1)}, u32[]{:S(2)}, u32[]{:S(2)}) collective-permute-start(bf16[4,96,128]{2,1,0:T(8,128)(2,1)S(1)} %get-tuple-element.18), channel_id=1, source_target_pairs={{0,32},{32,0},{64,96},{96,64},{1,33},{33,1},{65,97},{97,65},{2,34}... | collective-permute-start | bytes 294920 | tf_op jit(solution)/shard_map/ppermute | solution.py:213
  18.3 12.5 %collective-permute-start.1 = (bf16[4,96,128]{2,1,0:T(8,128)(2,1)S(1)}, bf16[4,96,128]{2,1,0:T(8,128)(2,1)S(1)}, u32[]{:S(2)}, u32[]{:S(2)}) collective-permute-start(bf16[4,96,128]{2,1,0:T(8,128)(2,1)S(1)} %get-tuple-element.19), channel_id=1, source_target_pairs={{0,96},{32,64},{64,32},{96,0},{1,97},{33,65},{65,33},{97,1},{2,98}... | collective-permute-start | bytes 294920 | tf_op jit(solution)/shard_map/ppermute | solution.py:213
  30.8 10.2 %collective-permute-start.2 = (bf16[2,100,128]{2,1,0:T(8,128)(2,1)S(1)}, bf16[2,100,128]{2,1,0:T(8,128)(2,1)S(1)}, u32[]{:S(2)}, u32[]{:S(2)}) collective-permute-start(bf16[2,100,128]{2,1,0:T(8,128)(2,1)S(1)} %get-tuple-element.21), channel_id=1, source_target_pairs={{0,1},{1,0},{2,3},{3,2},{4,5},{5,4},{6,7},{7,6},{8,9},{9,8},{10,11... | collective-permute-start | bytes 153608 | tf_op jit(solution)/shard_map/ppermute | solution.py:228
  30.9 10.1 %collective-permute-start.3 = (bf16[2,100,128]{2,1,0:T(8,128)(2,1)S(1)}, bf16[2,100,128]{2,1,0:T(8,128)(2,1)S(1)}, u32[]{:S(2)}, u32[]{:S(2)}) collective-permute-start(bf16[2,100,128]{2,1,0:T(8,128)(2,1)S(1)} %get-tuple-element.22), channel_id=1, source_target_pairs={{0,64},{1,2},{2,1},{3,4},{4,3},{5,6},{6,5},{7,8},{8,7},{9,10},{10,... | collective-permute-start | bytes 153608 | tf_op jit(solution)/shard_map/ppermute | solution.py:228
  33.0 8.0 %copy-start.3 = (s32[4,2]{0,1:T(2,128)S(1)}, s32[4,2]{0,1:T(2,128)}, u32[]{:S(2)}) copy-start(s32[4,2]{0,1:T(2,128)} %param.20) | copy-start | bytes 100
  33.0 8.0 %copy-start.4 = (s32[4,2]{0,1:T(2,128)S(1)}, s32[4,2]{0,1:T(2,128)}, u32[]{:S(2)}) copy-start(s32[4,2]{0,1:T(2,128)} %param.21) | copy-start | bytes 100
  41.1 3.4 %copy-start.2 = (bf16[128,128]{1,0:T(8,128)(2,1)S(1)}, bf16[128,128]{1,0:T(8,128)(2,1)}, u32[]{:S(2)}) copy-start(bf16[128,128]{1,0:T(8,128)(2,1)} %weight_ref.1) | copy-start | bytes 98308
  44.4 9.4 %copy-start.1 = (bf16[9,128,128]{2,1,0:T(8,128)(2,1)S(1)}, bf16[9,128,128]{2,1,0:T(8,128)(2,1)}, u32[]{:S(2)}) copy-start(bf16[9,128,128]{2,1,0:T(8,128)(2,1)} %taps_ref.3) | copy-start | bytes 884740
  44.4 18.2 %copy-start.5 = (f32[128]{0:T(128)S(1)}, f32[128]{0:T(128)}, u32[]{:S(2)}) copy-start(f32[128]{0:T(128)} %param.15) | copy-start | bytes 1540
  52.2 5.8 %collective-permute-start.4 = (bf16[8,96,128]{2,1,0:T(8,128)(2,1)S(1)}, bf16[8,96,128]{2,1,0:T(8,128)(2,1)S(1)}, u32[]{:S(2)}, u32[]{:S(2)}) collective-permute-start(bf16[8,96,128]{2,1,0:T(8,128)(2,1)S(1)} %get-tuple-element.24), channel_id=1, source_target_pairs={{0,32},{32,0},{64,96},{96,64},{1,33},{33,1},{65,97},{97,65},{2,34}... | collective-permute-start | bytes 589832 | tf_op jit(solution)/shard_map/ppermute | solution.py:213
  52.3 7.0 %collective-permute-start.5 = (bf16[8,96,128]{2,1,0:T(8,128)(2,1)S(1)}, bf16[8,96,128]{2,1,0:T(8,128)(2,1)S(1)}, u32[]{:S(2)}, u32[]{:S(2)}) collective-permute-start(bf16[8,96,128]{2,1,0:T(8,128)(2,1)S(1)} %get-tuple-element.25), channel_id=1, source_target_pairs={{0,96},{32,64},{64,32},{96,0},{1,97},{33,65},{65,33},{97,1},{2,98}... | collective-permute-start | bytes 589832 | tf_op jit(solution)/shard_map/ppermute | solution.py:213
  59.3 11.6 %collective-permute-start.6 = (bf16[4,104,128]{2,1,0:T(8,128)(2,1)S(1)}, bf16[4,104,128]{2,1,0:T(8,128)(2,1)S(1)}, u32[]{:S(2)}, u32[]{:S(2)}) collective-permute-start(bf16[4,104,128]{2,1,0:T(8,128)(2,1)S(1)} %get-tuple-element.27), channel_id=1, source_target_pairs={{0,1},{1,0},{2,3},{3,2},{4,5},{5,4},{6,7},{7,6},{8,9},{9,8},{10,11... | collective-permute-start | bytes 319496 | tf_op jit(solution)/shard_map/ppermute | solution.py:228
  59.4 11.6 %collective-permute-start.7 = (bf16[4,104,128]{2,1,0:T(8,128)(2,1)S(1)}, bf16[4,104,128]{2,1,0:T(8,128)(2,1)S(1)}, u32[]{:S(2)}, u32[]{:S(2)}) collective-permute-start(bf16[4,104,128]{2,1,0:T(8,128)(2,1)S(1)} %get-tuple-element.28), channel_id=1, source_target_pairs={{0,64},{1,2},{2,1},{3,4},{4,3},{5,6},{6,5},{7,8},{8,7},{9,10},{10,... | collective-permute-start | bytes 319496 | tf_op jit(solution)/shard_map/ppermute | solution.py:228
